TPU v7x, 128 devices: a whole 4x4x4 slice. The times are simulated.
128 devices in a mesh: dom: 32 (over y, x, core), rep: 4 (over z).
Axes of the slice: x: 4, y: 4, z: 4, core: 2. Of those that a mesh axis runs over, the one named last changes fastest.
Arguments:
- features: bfloat16 [131072, 512], P('dom', 'rep'), may hold values from -6 to 6
- tile_values: bfloat16 [1024, 8, 128, 128], P('dom'), may hold values from -0.1875 to 0.1875
- tile_columns: int32 [1024, 8], P('dom'), may hold values from 0 to 63
- boundary_rows: int32 [32, 128], P('dom'), may hold values from 0 to 4095
- train_rows: int32 [32, 4096], P('dom'), may hold values from 0 to 4095
- shuffle: int32 [32, 4096], P('dom'), may hold values from 0 to 4095, each once within a row
- labels: int32 [131072], P(('dom', 'rep')), may hold values from 0 to 152
- first_weight: bfloat16 [4, 512, 1024], replicated, may hold values from -0.125 to 0.125
- mid_weight: bfloat16 [1024, 1024], replicated, may hold values from -0.1875 to 0.1875
- out_weight: bfloat16 [1024, 153], replicated, may hold values from -0.1875 to 0.1875
Outputs:
- first_grad: float32 [4, 512, 1024], P('rep', 'dom')
- mid_grad: float32 [1024, 1024], P(('dom', 'rep'))
- out_grad: float32 [1024, 153], P(('dom', 'rep'))
Inputs may be any that keep to these rules, and one draw needn't show every extreme that they name: `tile_columns`: an entry below 32 names a block of the partition's own rows, an entry c of 32 or more names block c - 32 of the gathered boundary rows. `train_rows`: indices may repeat. `shuffle`: each row is a permutation of 0 to 4095.
All inputs are finite; a program needn't handle non-finite values.
Results may differ from a plain program's by a relative error of at most 0.02.
Values may be sent and summed in bfloat16 or wider, within the bound.
No kernel may reach another device: no remote copies, remote signals or barrier semaphores. Data moves between devices by JAX's collectives and lax.ppermute only.
A program may use at most 128 MiB of HBM per device.

v0:
```python
import functools
import math

import jax
import jax.numpy as jnp
from jax import lax
from jax.experimental import pallas as pl
from jax.experimental.pallas import tpu as pltpu
from jax.sharding import Mesh, PartitionSpec as P

HOPS = 3
TILE = 128
NB = 32
K = 8
R = 4096
HID = 1024
C = 153
CP = 256
Y, X, CORE, REP = 4, 4, 2, 4
DOM = Y * X * CORE
ROWS = R // REP
N_TRAIN = DOM * R
BF = jnp.bfloat16
F32 = jnp.float32
LAB = 16
MIB = 2**20

root_two_pi = 0.7978845608028654
cubic_term = 0.044715


def gelu_pair(v):
    sq = v * v
    t = jnp.tanh(root_two_pi * (v + cubic_term * sq * v))
    half = 0.5 * (1.0 + t)
    slope = half + (0.5 * root_two_pi) * v * (1.0 - t * t) * (
        1.0 + (3.0 * cubic_term) * sq
    )
    return v * half, slope


def dot(a, b, ca, cb):
    return lax.dot_general(a, b, (((ca,), (cb,)), ((), ())), preferred_element_type=F32)


def params(mib):
    return pltpu.CompilerParams(vmem_limit_bytes=mib * MIB)


def whole(memory_space=pltpu.VMEM):
    return pl.BlockSpec(memory_space=memory_space)


def struct(shape, dtype=BF):
    return jax.ShapeDtypeStruct(shape, dtype)


def export_rows(hop, brow):
    here = lax.broadcasted_iota(jnp.int32, (TILE, TILE), 0)
    there = lax.broadcasted_iota(jnp.int32, (TILE, TILE), 1)
    column = jnp.sum(jnp.where(here == there, brow[...], 0), axis=1, keepdims=True)
    row = lax.broadcasted_iota(jnp.int32, (TILE, R), 1)
    return dot((row == column).astype(BF), hop[...], 1, 0).astype(BF)


def take_quarters(rep, hop, quarters):
    for d, q in enumerate(quarters):
        start = pl.multiple_of(lax.rem(rep + d, REP) * ROWS, ROWS)
        q[:ROWS] = hop[pl.ds(start, ROWS), :]


def export_kernel(pos, hop, brow, labels, export, *quarters):
    got = export_rows(hop, brow)
    extra = jnp.concatenate([labels[...].astype(F32), jnp.zeros((8, TILE), F32)])
    extra = extra.astype(BF)
    for t in range(Y * X):
        export[t, :TILE] = got
        export[t, TILE:] = extra
    take_quarters(pos[0], hop, quarters)


def export_first(pos, hop, brow, labels):
    return pl.pallas_call(
        export_kernel,
        in_specs=[whole(pltpu.SMEM)] + [whole()] * 3,
        out_specs=[whole()] * 5,
        out_shape=[struct((Y * X, TILE + LAB, TILE))] + [struct((ROWS, TILE))] * 4,
        compiler_params=params(16),
        name="export_first",
        cost_estimate=pl.CostEstimate(
            flops=2 * TILE * TILE * R, bytes_accessed=2 * MIB, transcendentals=0
        ),
    )(pos, hop, brow, labels)


CUTS = 8
STEP = NB // CUTS


def prop_kernel(h, cols, tiles, hop, near, far, brow, *rest):
    last = h == HOPS - 1
    if last:
        q0, q1, q2, q3, joined, held, sem, out = rest
    else:
        out, export, q0, q1, q2, q3, joined, held, sem = rest
    r, core, inner = cols[NB * K], cols[NB * K + 1], cols[NB * K + 2]

    def copy(c):
        here = pl.ds(c * STEP, STEP)
        return pltpu.make_async_copy(tiles.at[here], held.at[here], sem.at[c])

    for c in range(CUTS):
        copy(c).start()
    joined[:R] = hop[...]
    for t in range(Y * X):
        at = R + t * TILE
        joined[at : at + TILE] = near[t, :TILE]
        joined[at + R // 2 : at + R // 2 + TILE] = far[t, :TILE]

    @pl.loop(0, CUTS)
    def _(c):
        copy(c).wait()
        for b in range(STEP):
            b = c * STEP + b
            parts = []
            for k in range(K):
                at = pl.multiple_of(cols[b * K + k] * TILE, TILE)
                parts.append(joined[pl.ds(at, TILE), :])
            left = jnp.concatenate([held[b, k] for k in range(K)], axis=1)
            got = dot(left, jnp.concatenate(parts, axis=0), 1, 0)
            out[pl.ds(pl.multiple_of(b * TILE, TILE), TILE), :] = got.astype(BF)

    if not last:
        got = export_rows(out, brow)
        for t in range(Y * X):
            export[t] = got
    quarters = (q0, q1, q2, q3)
    take_quarters(r, out, quarters)
    if h == 0:
        pick = lax.broadcasted_iota(jnp.int32, (LAB, TILE), 0) == inner
        labs = []
        for t in range(Y * X):
            two = [
                jnp.sum(jnp.where(pick, v[t, TILE:].astype(F32), 0.0), axis=0, keepdims=True)
                for v in (near, far)
            ]
            labs.append(jnp.where(core == 0, two[0], two[1]))
            labs.append(jnp.where(core == 0, two[1], two[0]))
        labs = jnp.concatenate(labs, axis=0).astype(BF)
        for q in quarters:
            q[ROWS:] = labs


def propagate(h, cols, tiles, hop, near, far, brow):
    last = h == HOPS - 1
    outs = [] if last else [(R, TILE), (Y * X, TILE, TILE)]
    outs += [(ROWS + DOM if h == 0 else ROWS, TILE)] * 4
    scratch = [
        pltpu.VMEM((2 * R, TILE), BF),
        pltpu.VMEM((NB, K, TILE, TILE), BF),
        pltpu.SemaphoreType.DMA((CUTS,)),
    ]
    scratch += [pltpu.VMEM((R, TILE), BF)] if last else []
    return pl.pallas_call(
        functools.partial(prop_kernel, h),
        in_specs=[whole(pltpu.SMEM), whole(pltpu.HBM)] + [whole()] * 4,
        out_specs=[whole()] * len(outs),
        scratch_shapes=scratch,
        out_shape=[struct(s) for s in outs],
        compiler_params=params(54),
        name="propagate_" + str(h),
        cost_estimate=pl.CostEstimate(
            flops=2 * NB * K * TILE**3, bytes_accessed=12 * MIB, transcendentals=0
        ),
    )(cols, tiles, hop, near, far, brow)


def count_kernel(pos, lab0, lab1, lab2, lab3, shuffle, train, out):
    labels = jnp.zeros((DOM, TILE), F32)
    for d, v in enumerate((lab0, lab1, lab2, lab3)):
        labels = jnp.where(pos[2] == d, v[...].astype(F32), labels)
    first = lax.broadcasted_iota(jnp.int32, (DOM, TILE), 0)
    second = lax.broadcasted_iota(jnp.int32, (TILE, TILE), 0)
    slots = jnp.zeros((DOM, TILE), F32)
    for lo in range(0, DOM, 8):
        a, b = [], []
        for e in range(lo, lo + 8):
            slot = shuffle[e : e + 1, :]
            label = labels[e : e + 1, :]
            a.append(jnp.where(first == slot // TILE, label, 0.0).astype(BF))
            b.append((second == lax.rem(slot, TILE)).astype(BF))
        slots += dot(jnp.concatenate(a, axis=1), jnp.concatenate(b, axis=1), 1, 1)
    slots = slots.astype(jnp.int32)
    paper = lax.broadcasted_iota(jnp.int32, (ROWS, TILE), 0) + pos[0] * ROWS
    kind = lax.broadcasted_iota(jnp.int32, (CP, TILE), 0)
    total = jnp.zeros((ROWS, CP), F32)
    for lo in range(0, DOM, 8):
        a, b = [], []
        for e in range(lo, lo + 8):
            a.append((paper == train[e : e + 1, :]).astype(BF))
            b.append((kind == slots[e : e + 1, :]).astype(BF))
        total += dot(jnp.concatenate(a, axis=1), jnp.concatenate(b, axis=1), 1, 1)
    out[...] = total


def count_labels(pos, both, shuffle, train):
    def fixed(shape):
        return pl.BlockSpec(shape, lambda i, c: (0, 0))

    tail = pl.BlockSpec((DOM, TILE), lambda i, c: (ROWS // DOM, 0))
    return pl.pallas_call(
        count_kernel,
        grid_spec=pltpu.PrefetchScalarGridSpec(
            num_scalar_prefetch=1,
            grid=(1,),
            in_specs=[tail] * 4 + [fixed((DOM, TILE))] * 2,
            out_specs=fixed((ROWS, CP)),
        ),
        out_shape=struct((ROWS, CP), F32),
        compiler_params=params(24),
        name="count_labels",
        cost_estimate=pl.CostEstimate(
            flops=2 * ROWS * R * CP, bytes_accessed=2 * MIB, transcendentals=0
        ),
    )(pos, *both, shuffle, train)


MLP_ROWS = 256


def slab_of(rep, d):
    return lax.rem(rep + REP - d, REP)


def early_kernel(pos, *refs):
    pieces, (w1, out) = refs[:12], refs[12:]
    total = jnp.zeros((MLP_ROWS, HID), F32)
    for d in range(REP):
        x = jnp.concatenate([pieces[3 * d + h][...] for h in range(HOPS)], axis=1)
        total += dot(x, w1[slab_of(pos[0], d), : HOPS * TILE], 1, 0)
    out[...] = total


def mlp_kernel(pos, *refs):
    pieces, (early, counts, w1, w2, w3, act1, act2, gl, gm, gf) = refs[:4], refs[4:]
    pre1 = early[...]
    for d in range(REP):
        pre1 += dot(pieces[d][...], w1[slab_of(pos[0], d), HOPS * TILE :], 1, 0)
    a1, slope1 = gelu_pair(pre1)
    a1 = a1.astype(BF)
    act1[...] = a1
    a2, slope2 = gelu_pair(dot(a1, w2[...], 1, 0))
    a2 = a2.astype(BF)
    act2[...] = a2
    logits = dot(a2, w3[...], 1, 0)
    kind = lax.broadcasted_iota(jnp.int32, (MLP_ROWS, CP), 1)
    ex = jnp.where(kind < C, jnp.exp(logits), 0.0)
    probs = ex / jnp.sum(ex, axis=1, keepdims=True)
    drawn = counts[...]
    many = jnp.sum(drawn, axis=1, keepdims=True)
    g3 = ((probs * many - drawn) * (1.0 / math.sqrt(N_TRAIN))).astype(BF)
    gl[...] = g3
    g2 = (dot(g3, w3[...], 1, 1) * slope2).astype(BF)
    gm[...] = g2
    gf[...] = (dot(g2, w2[...], 1, 1) * slope1).astype(BF)


def fixed_block(shape):
    return pl.BlockSpec(shape, lambda i, c: (0,) * len(shape))


def row_block(width):
    return pl.BlockSpec((MLP_ROWS, width), lambda i, c: (i, 0))


def first_layer_early(pos, pieces, w1):
    return pl.pallas_call(
        early_kernel,
        grid_spec=pltpu.PrefetchScalarGridSpec(
            num_scalar_prefetch=1,
            grid=(ROWS // MLP_ROWS,),
            in_specs=[row_block(TILE)] * 12 + [fixed_block(w1.shape)],
            out_specs=row_block(HID),
        ),
        out_shape=struct((ROWS, HID), F32),
        compiler_params=params(20),
        name="first_layer_early",
        cost_estimate=pl.CostEstimate(
            flops=2 * ROWS * HID * 3 * 512, bytes_accessed=11 * MIB, transcendentals=0
        ),
    )(pos, *pieces, w1)


def mlp(pos, pieces, early, counts, w1, w2, w3):
    widths = (HID, HID, CP, HID, HID)
    return pl.pallas_call(
        mlp_kernel,
        grid_spec=pltpu.PrefetchScalarGridSpec(
            num_scalar_prefetch=1,
            grid=(ROWS // MLP_ROWS,),
            in_specs=[row_block(TILE)] * 4
            + [row_block(HID), row_block(CP)]
            + [fixed_block(w.shape) for w in (w1, w2, w3)],
            out_specs=[row_block(w) for w in widths],
        ),
        out_shape=[struct((ROWS, w)) for w in widths],
        compiler_params=params(36),
        name="mlp",
        cost_estimate=pl.CostEstimate(
            flops=2 * ROWS * HID * (2 * HID + 512 + 2 * CP),
            bytes_accessed=20 * MIB,
            transcendentals=2 * ROWS * HID,
        ),
    )(pos, *pieces, early, counts, w1, w2, w3)


WIDE = (HID + CP) // 2
SIDE = 16


def outer_kernel(pos, act1, act2, gl, gm, keep, send):
    own = pos[1] == 0
    width = HID // Y
    for k in range(Y):
        at = pl.multiple_of(lax.rem(pos[3] + k, Y) * width, width)
        mid = dot(act1[:, pl.ds(at, width)], gm[...], 0, 0)
        out = dot(act2[:, pl.ds(at, width)], gl[...], 0, 0)
        both = jnp.concatenate([mid, out], axis=1).reshape(X, CORE, REP, 8, HID + CP)
        both = jnp.concatenate([both[..., :WIDE], both[..., WIDE:]], axis=3)
        zero, one = both[:, 0], both[:, 1]
        shape = (SIDE, 16, WIDE)
        keep[k] = jnp.where(own, zero, one).astype(BF).reshape(shape)
        send[k] = jnp.where(own, one, zero).astype(BF).reshape(shape)


def outer_grads(pos, act1, act2, gl, gm):
    return pl.pallas_call(
        outer_kernel,
        in_specs=[whole(pltpu.SMEM)] + [whole()] * 4,
        out_specs=[whole()] * 2,
        out_shape=[struct((Y, SIDE, 16, WIDE))] * 2,
        compiler_params=params(30),
        name="outer_grads",
        cost_estimate=pl.CostEstimate(
            flops=2 * ROWS * HID * (HID + CP), bytes_accessed=8 * MIB, transcendentals=0
        ),
    )(pos, act1, act2, gl, gm)


def first_kernel(steps, pos, *refs):
    n = (HOPS + 1) * len(steps)
    pieces, (gf, keep, send) = refs[:n], refs[n:]
    own = pos[1] == 0
    for at in range(len(steps)):
        for y in range(0, Y, 2):
            two = [pieces[at * (HOPS + 1) + u][:ROWS] for u in (y, y + 1)]
            x = jnp.concatenate(two, axis=1)
            got = dot(x, gf[...], 0, 0).reshape(2 * X, CORE, 16, HID)
            zero, one = got[:, 0], got[:, 1]
            here = slice(y * X, (y + 2) * X)
            keep[at, here] = jnp.where(own, zero, one).astype(BF)
            send[at, here] = jnp.where(own, one, zero).astype(BF)


def first_grads(pos, pieces, gf, steps):
    used = [pieces[h][(REP - k) % REP] for k in steps for h in range(HOPS + 1)]
    return pl.pallas_call(
        functools.partial(first_kernel, steps),
        in_specs=[whole(pltpu.SMEM)] + [whole()] * (len(used) + 1),
        out_specs=[whole()] * 2,
        out_shape=[struct((len(steps), SIDE, 16, HID))] * 2,
        compiler_params=params(24),
        name="first_grads_" + "".join(str(k) for k in steps),
        cost_estimate=pl.CostEstimate(
            flops=len(steps) * ROWS * HID * HID, bytes_accessed=6 * MIB, transcendentals=0
        ),
    )(pos, *used, gf)


def plus(*values):
    return sum(v.astype(F32) for v in values)


def far_kernel(at, keep, got, ahead, behind):
    half = SIDE // 2
    ahead[...] = plus(keep[at, :half], got[at, :half]).astype(BF)
    behind[...] = plus(keep[at, half:], got[at, half:]).astype(BF)


def near_kernel(one, three, keep, got, ahead, behind, q1, q3):
    half = SIDE // 2
    q1[:half] = plus(keep[one, :half], got[one, :half], ahead[...]).astype(BF)
    q1[half:] = plus(keep[one, half:], got[one, half:]).astype(BF)
    q3[:half] = plus(keep[three, :half], got[three, :half]).astype(BF)
    q3[half:] = plus(keep[three, half:], got[three, half:], behind[...]).astype(BF)


def own_kernel(keep, got, r1, r3, out):
    out[...] = plus(keep[0], got[0], r1[...], r3[...]).astype(BF)


def small(kernel, outs, name, *args):
    moved = sum(a.size for a in args) * 2
    return pl.pallas_call(
        kernel,
        in_specs=[whole()] * len(args),
        out_specs=[whole()] * len(outs),
        out_shape=[struct(s) for s in outs],
        compiler_params=params(14),
        name=name,
        cost_estimate=pl.CostEstimate(
            flops=moved, bytes_accessed=2 * moved, transcendentals=0
        ),
    )(*args)


def send_far(at, keep, got, axis, tag):
    half = (SIDE // 2,) + keep.shape[2:]
    kernel = functools.partial(far_kernel, at)
    ahead, behind = small(kernel, [half, half], "far_" + tag, keep, got)
    return shift(ahead, axis, 1), shift(behind, axis, 3)


def send_near(one, three, keep, got, far, axis, tag):
    kernel = functools.partial(near_kernel, one, three)
    q1, q3 = small(kernel, [keep.shape[1:]] * 2, "near_" + tag, keep, got, *far)
    return shift(q1, axis, 1), shift(q3, axis, 3)


def own_share(keep, got, near, tag):
    return small(own_kernel, [keep.shape[1:]], "own_" + tag, keep, got, *near)[0]


def total_kernel(part_f, part_m, first, mid, out):
    first[0] = jnp.sum(part_f[...].astype(F32), axis=0)
    total = jnp.sum(part_m[...].astype(F32), axis=0)
    rest = jnp.concatenate([total[:8], total[8:]], axis=1)
    mid[...] = rest[:, :HID]
    out[...] = rest[:, HID : HID + C]


def total_grads(part_f, part_m):
    return pl.pallas_call(
        total_kernel,
        in_specs=[whole()] * 2,
        out_specs=[whole()] * 3,
        out_shape=[struct((1, 16, HID), F32), struct((8, HID), F32), struct((8, C), F32)],
        compiler_params=params(12),
        name="total_grads",
    )(part_f, part_m)


def shift(value, axis, by):
    size = lax.axis_size(axis)
    return lax.ppermute(value, axis, [(i, (i + by) % size) for i in range(size)])


def swap(value, axes):
    return lax.all_to_all(value, axes, split_axis=0, concat_axis=0, tiled=True)


def exchange(quarters):
    return [quarters[0]] + [shift(quarters[d], "rep", d) for d in (1, 2, 3)]


def per_device(
    features,
    tile_values,
    tile_columns,
    boundary_rows,
    train_rows,
    shuffle,
    labels,
    first_weight,
    mid_weight,
    out_weight,
):
    y, x, core, rep = (lax.axis_index(a) for a in ("y", "x", "core", "rep"))
    pos = jnp.stack([rep, core, lax.rem(rep + REP - y, REP), y]).astype(jnp.int32)

    part = tile_columns - NB
    halo_at = NB + (part + core) % CORE * (NB // CORE) + part // CORE
    cols = jnp.where(tile_columns < NB, tile_columns, halo_at).reshape(-1)
    inner = lax.rem((y * X + x) * CORE + core, DOM // REP)
    cols = jnp.concatenate([cols, jnp.stack([rep, core, inner])]).astype(jnp.int32)
    brow = boundary_rows

    export, *quarters = export_first(pos, features, brow, labels.reshape(8, TILE))
    hop, pieces, counts = features, [], None
    for h in range(HOPS):
        got = exchange(quarters)
        if h == HOPS - 1:
            counts = count_labels(
                pos, pieces[1], shuffle.reshape(DOM, TILE), train_rows.reshape(DOM, TILE)
            )
        near, got[1], got[3], counts = lax.optimization_barrier(
            (swap(export, ("y", "x")), got[1], got[3], counts)
        )
        far = shift(near, "core", 1)
        pieces.append(got)
        made = propagate(h, cols, tile_values, hop, near, far, brow)
        made, got[2] = lax.optimization_barrier((made, got[2]))
        hop, export, quarters = made[0], made[1], made[-4:]
    early = first_layer_early(
        pos, [pieces[h][d] for d in range(REP) for h in range(HOPS)], first_weight
    )
    pieces.append(exchange(quarters))

    w3 = jnp.pad(out_weight, ((0, 0), (0, CP - C)))
    act1, act2, gl, gm, gf = mlp(
        pos, pieces[3], early, counts, first_weight, mid_weight, w3
    )
    keep_m, send_m = outer_grads(pos, act1, act2, gl, gm)
    got_m = shift(send_m, "core", 1)
    keep2, send2 = first_grads(pos, pieces, gf, (2,))
    got_m, send2, gf = lax.optimization_barrier((got_m, send2, gf))
    got2 = shift(send2, "core", 1)
    far_m = send_far(2, keep_m, got_m, "y", "middle")
    keep13, send13 = first_grads(pos, pieces, gf, (1, 3))
    got13 = shift(send13, "core", 1)
    got2, far_m, gf = lax.optimization_barrier((got2, far_m, gf))
    far_f = send_far(0, keep2, got2, "rep", "first")
    keep0, send0 = first_grads(pos, pieces, gf, (0,))
    got0 = shift(send0, "core", 1)
    near_m = send_near(1, 3, keep_m, got_m, far_m, "y", "middle")
    part_m = swap(own_share(keep_m, got_m, near_m, "middle"), ("x", "rep"))
    near_f = send_near(0, 1, keep13, got13, far_f, "rep", "first")
    part_f = swap(own_share(keep0, got0, near_f, "first"), ("y", "x"))
    first, mid, out = total_grads(part_f, part_m)
    return first, mid, out


def solution(mesh):
    fine = Mesh(mesh.devices.reshape(Y, X, CORE, REP), ("y", "x", "core", "rep"))
    dom = ("y", "x", "core")
    every = dom + ("rep",)
    placed = (
        P(dom, "rep"),
        P(dom, None, None, None),
        P(dom, None),
        P(dom, None),
        P(dom, None),
        P(dom, None),
        P(every),
        P(),
        P(),
        P(),
    )
    return jax.shard_map(
        per_device,
        mesh=fine,
        in_specs=placed,
        out_specs=(P("rep", dom, None), P(every, None), P(every, None)),
        check_vma=False,
    )
```

profile of v0, /device:TPU:0, one launch (start us, length us, event | category | flops | bytes accessed | tf_op | source)
XLA Modules:
  0.0 186.9 jit_solution(210388186965259151)
XLA Ops:
  3.3 1.9 %export_first.1 = (bf16[16,144,128]{2,1,0:T(8,128)(2,1)}, bf16[1024,128]{1,0:T(8,128)(2,1)S(1)}, bf16[1024,128]{1,0:T(8,128)(2,1)S(1)}, bf16[1024,128]{1,0:T(8,128)(2,1)S(1)}, bf16[1024,128]{1,0:T(8,128)(2,1)S(1)}) custom-call(s32[4]{0:T(128)S(1)} %pad_add_fusion.1.pos, bf16[4096,128]{1,0:T(8,128)(2,1)S(1)} %copy-done, s32[1,128]{1,0:T(1,128)S(1)} %copy-done.1, ...), custom_call_target="tpu_custom_call" | custom-call | flops 134217728 | bytes 2097152 | tf_op jit(solution)/shard_map/export_first/pallas_call | solution.py:83
  5.2 7.1 %all-to-all-start = ((bf16[16,144,128]{2,1,0:T(8,128)(2,1)}), bf16[16,144,128]{2,1,0:T(8,128)(2,1)S(1)}, u32[]{:S(2)}, u32[]{:S(2)}) async-start(bf16[16,144,128]{2,1,0:T(8,128)(2,1)} %get-tuple-element.82), calls=%async_computation | async-start | bytes 1179648 | tf_op jit(solution)/shard_map/all_to_all | solution.py:459
  12.3 2.0 %collective-permute-start = (bf16[1024,128]{1,0:T(8,128)(2,1)S(1)}, bf16[1024,128]{1,0:T(8,128)(2,1)S(1)}, u32[]{:S(2)}, u32[]{:S(2)}) collective-permute-start(bf16[1024,128]{1,0:T(8,128)(2,1)S(1)} %get-tuple-element.83), channel_id=1, source_target_pairs={{0,1},{1,2},{2,3},{3,0},{4,5},{5,6},{6,7},{7,4},{8,9},{9,10},{10,1... | collective-permute-start | bytes 786440 | tf_op jit(solution)/shard_map/ppermute | solution.py:455
  14.3 2.2 %collective-permute-start.1 = (bf16[1024,128]{1,0:T(8,128)(2,1)S(1)}, bf16[1024,128]{1,0:T(8,128)(2,1)S(1)}, u32[]{:S(2)}, u32[]{:S(2)}) collective-permute-start(bf16[1024,128]{1,0:T(8,128)(2,1)S(1)} %get-tuple-element.84), channel_id=1, source_target_pairs={{0,3},{1,0},{2,1},{3,2},{4,7},{5,4},{6,5},{7,6},{8,11},{9,8},{10,9... | collective-permute-start | bytes 786440 | tf_op jit(solution)/shard_map/ppermute | solution.py:455
  16.5 5.9 %collective-permute-done.refs_3_.refs_4_ = bf16[1024,128]{1,0:T(8,128)(2,1)S(1)} collective-permute-done((bf16[1024,128]{1,0:T(8,128)(2,1)S(1)}, bf16[1024,128]{1,0:T(8,128)(2,1)S(1)}, u32[]{:S(2)}, u32[]{:S(2)}) %collective-permute-start) | collective-permute-done | bytes 262176 | tf_op jit(solution)/shard_map/ppermute | solution.py:455
  22.5 2.1 %all-to-all-done.near = bf16[16,144,128]{2,1,0:T(8,128)(2,1)S(1)} async-done(((bf16[16,144,128]{2,1,0:T(8,128)(2,1)}), bf16[16,144,128]{2,1,0:T(8,128)(2,1)S(1)}, u32[]{:S(2)}, u32[]{:S(2)}) %all-to-all-start) | async-done | bytes 589856 | tf_op jit(solution)/shard_map/all_to_all | solution.py:459
  24.6 3.9 %collective-permute-start.3 = (bf16[1024,128]{1,0:T(8,128)(2,1)S(1)}, bf16[1024,128]{1,0:T(8,128)(2,1)S(1)}, u32[]{:S(2)}, u32[]{:S(2)}) collective-permute-start(bf16[1024,128]{1,0:T(8,128)(2,1)S(1)} %get-tuple-element.92), channel_id=1, source_target_pairs={{0,2},{1,3},{2,0},{3,1},{4,6},{5,7},{6,4},{7,5},{8,10},{9,11},{10,... | collective-permute-start | bytes 786440 | tf_op jit(solution)/shard_map/ppermute | solution.py:455
  30.1 8.1 %propagate_0.1 = (bf16[4096,128]{1,0:T(8,128)(2,1)}, bf16[16,128,128]{2,1,0:T(8,128)(2,1)}, bf16[1056,128]{1,0:T(8,128)(2,1)}, bf16[1056,128]{1,0:T(8,128)(2,1)}...) custom-call(s32[259]{0:T(512)} %pad_add_fusion.cols, bf16[32,8,128,128]{3,2,1,0:T(8,128)(2,1)} %tiles.5, ...), custom_call_target="tpu_custom_call" | custom-call | flops 1073741824 | bytes 12582912 | tf_op jit(solution)/shard_map/propagate_0/pallas_call | solution.py:164
  38.2 3.9 %all-to-all-start.1 = ((bf16[16,128,128]{2,1,0:T(8,128)(2,1)}), bf16[16,128,128]{2,1,0:T(8,128)(2,1)S(1)}, u32[]{:S(2)}, u32[]{:S(2)}) async-start(bf16[16,128,128]{2,1,0:T(8,128)(2,1)} %get-tuple-element.95), calls=%async_computation.1 | async-start | bytes 1048576 | tf_op jit(solution)/shard_map/all_to_all | solution.py:459
  43.2 2.3 %collective-permute-start.5 = (bf16[1056,128]{1,0:T(8,128)(2,1)}, bf16[1056,128]{1,0:T(8,128)(2,1)S(1)}, u32[]{:S(2)}, u32[]{:S(2)}) collective-permute-start(bf16[1056,128]{1,0:T(8,128)(2,1)} %get-tuple-element.97), channel_id=1, source_target_pairs={{0,3},{1,0},{2,1},{3,2},{4,7},{5,4},{6,5},{7,6},{8,11},{9,8},{10,9... | collective-permute-start | bytes 811016 | tf_op jit(solution)/shard_map/ppermute | solution.py:455
  45.4 6.5 %collective-permute-done.4.lab1.refs_4_.refs_5_ = bf16[1056,128]{1,0:T(8,128)(2,1)S(1)} collective-permute-done((bf16[1056,128]{1,0:T(8,128)(2,1)}, bf16[1056,128]{1,0:T(8,128)(2,1)S(1)}, u32[]{:S(2)}, u32[]{:S(2)}) %collective-permute-start.4) | collective-permute-done | bytes 270368 | tf_op jit(solution)/shard_map/ppermute | solution.py:455
  51.9 2.0 %all-to-all-done.1.near = bf16[16,128,128]{2,1,0:T(8,128)(2,1)S(1)} async-done(((bf16[16,128,128]{2,1,0:T(8,128)(2,1)}), bf16[16,128,128]{2,1,0:T(8,128)(2,1)S(1)}, u32[]{:S(2)}, u32[]{:S(2)}) %all-to-all-start.1) | async-done | bytes 524320 | tf_op jit(solution)/shard_map/all_to_all | solution.py:459
  56.7 7.9 %propagate_1.1 = (bf16[4096,128]{1,0:T(8,128)(2,1)}, bf16[16,128,128]{2,1,0:T(8,128)(2,1)}, bf16[1024,128]{1,0:T(8,128)(2,1)}, bf16[1024,128]{1,0:T(8,128)(2,1)}...) custom-call(s32[259]{0:T(512)} %pad_add_fusion.cols, bf16[32,8,128,128]{3,2,1,0:T(8,128)(2,1)} %tiles.5, ...), custom_call_target="tpu_custom_call" | custom-call | flops 1073741824 | bytes 12582912 | tf_op jit(solution)/shard_map/propagate_1/pallas_call | solution.py:164
  64.6 5.0 %all-to-all-start.2 = ((bf16[16,128,128]{2,1,0:T(8,128)(2,1)}), bf16[16,128,128]{2,1,0:T(8,128)(2,1)}, u32[]{:S(2)}, u32[]{:S(2)}) async-start(bf16[16,128,128]{2,1,0:T(8,128)(2,1)} %get-tuple-element.108), calls=%async_computation.2 | async-start | bytes 1048576 | tf_op jit(solution)/shard_map/all_to_all | solution.py:459
  69.6 2.0 %collective-permute-start.8 = (bf16[1024,128]{1,0:T(8,128)(2,1)}, bf16[1024,128]{1,0:T(8,128)(2,1)S(1)}, u32[]{:S(2)}, u32[]{:S(2)}) collective-permute-start(bf16[1024,128]{1,0:T(8,128)(2,1)} %get-tuple-element.109), channel_id=1, source_target_pairs={{0,1},{1,2},{2,3},{3,0},{4,5},{5,6},{6,7},{7,4},{8,9},{9,10},{10,1... | collective-permute-start | bytes 786440 | tf_op jit(solution)/shard_map/ppermute | solution.py:455
  72.9 3.8 %count_labels.1.refs_5_ = f32[1024,256]{1,0:T(8,128)S(1)} custom-call(s32[4]{0:T(128)S(1)} %pad_add_fusion.1.pos, bf16[1056,128]{1,0:T(8,128)(2,1)S(1)} %copy-done.5, bf16[1056,128]{1,0:T(8,128)(2,1)S(1)} %collective-permute-done.4.lab1.refs_4_.refs_5_, bf16[1056,128]{1,0:T(8,128)(2,1)S(1)} %collective-permute-done.7.lab2.refs_7_.refs_1_, ...), custom_call_target="tpu_custom_call" | custom-call | flops 2147483648 | bytes 2097152 | tf_op jit(solution)/shard_map/count_labels/pallas_call | solution.py:211
  79.6 1.9 %all-to-all-done.2.near = bf16[16,128,128]{2,1,0:T(8,128)(2,1)} async-done(((bf16[16,128,128]{2,1,0:T(8,128)(2,1)}), bf16[16,128,128]{2,1,0:T(8,128)(2,1)}, u32[]{:S(2)}, u32[]{:S(2)}) %all-to-all-start.2) | async-done | bytes 524320 | tf_op jit(solution)/shard_map/all_to_all | solution.py:459
  84.6 7.8 %propagate_2.1 = (bf16[1024,128]{1,0:T(8,128)(2,1)}, bf16[1024,128]{1,0:T(8,128)(2,1)}, bf16[1024,128]{1,0:T(8,128)(2,1)}, bf16[1024,128]{1,0:T(8,128)(2,1)}) custom-call(s32[259]{0:T(512)} %pad_add_fusion.cols, bf16[32,8,128,128]{3,2,1,0:T(8,128)(2,1)} %tiles.5, bf16[4096,128]{1,0:T(8,128)(2,1)} %get-tuple-element.107.hop, ...), custom_call_target="tpu_custom_call" | custom-call | flops 1073741824 | bytes 12582912 | tf_op jit(solution)/shard_map/propagate_2/pallas_call | solution.py:164
  92.3 2.1 %collective-permute-start.12 = (bf16[1024,128]{1,0:T(8,128)(2,1)}, bf16[1024,128]{1,0:T(8,128)(2,1)S(1)}, u32[]{:S(2)}, u32[]{:S(2)}) collective-permute-start(bf16[1024,128]{1,0:T(8,128)(2,1)} %get-tuple-element.121), channel_id=1, source_target_pairs={{0,1},{1,2},{2,3},{3,0},{4,5},{5,6},{6,7},{7,4},{8,9},{9,10},{10,1... | collective-permute-start | bytes 786440 | tf_op jit(solution)/shard_map/ppermute | solution.py:455
  94.4 2.3 %collective-permute-start.13 = (bf16[1024,128]{1,0:T(8,128)(2,1)}, bf16[1024,128]{1,0:T(8,128)(2,1)S(1)}, u32[]{:S(2)}, u32[]{:S(2)}) collective-permute-start(bf16[1024,128]{1,0:T(8,128)(2,1)} %get-tuple-element.122), channel_id=1, source_target_pairs={{0,2},{1,3},{2,0},{3,1},{4,6},{5,7},{6,4},{7,5},{8,10},{9,11},{10,... | collective-permute-start | bytes 786440 | tf_op jit(solution)/shard_map/ppermute | solution.py:455
  97.4 5.6 %first_layer_early.1.refs_4_ = f32[1024,1024]{1,0:T(8,128)S(1)} custom-call(s32[4]{0:T(128)S(1)} %pad_add_fusion.1.pos, bf16[1024,128]{1,0:T(8,128)(2,1)S(1)} %get-tuple-element.81.refs_0_, bf16[1056,128]{1,0:T(8,128)(2,1)S(1)} %copy-done.5, bf16[1024,128]{1,0:T(8,128)(2,1)S(1)} %copy-done.6, bf16[1024,128]{1,0:T(8,128)(2,1)S(1)} %collective-permute-done.refs_3_.refs_4_, ...), custom_call_target="tpu_custom_call" | custom-call | flops 3221225472 | bytes 11534336 | tf_op jit(solution)/shard_map/first_layer_early/pallas_call | solution.py:277
  103.0 6.0 %collective-permute-done.13.refs_2_.refs_3_ = bf16[1024,128]{1,0:T(8,128)(2,1)S(1)} collective-permute-done((bf16[1024,128]{1,0:T(8,128)(2,1)}, bf16[1024,128]{1,0:T(8,128)(2,1)S(1)}, u32[]{:S(2)}, u32[]{:S(2)}) %collective-permute-start.13) | collective-permute-done | bytes 262176 | tf_op jit(solution)/shard_map/ppermute | solution.py:455
  109.0 14.0 %mlp.1 = (bf16[1024,1024]{1,0:T(8,128)(2,1)S(1)}, bf16[1024,1024]{1,0:T(8,128)(2,1)S(1)}, bf16[1024,256]{1,0:T(8,128)(2,1)S(1)}, bf16[1024,1024]{1,0:T(8,128)(2,1)S(1)}, bf16[1024,1024]{1,0:T(8,128)(2,1)S(1)}) custom-call(s32[4]{0:T(128)S(1)} %pad_add_fusion.1.pos, bf16[1024,128]{1,0:T(8,128)(2,1)S(1)} %copy-done.7, ...), custom_call_target="tpu_custom_call" | custom-call | flops 6442450944 | bytes 20971520 | tf_op jit(solution)/shard_map/mlp/pallas_call | solution.py:296
  123.0 3.7 %outer_grads.1 = (bf16[4,16,16,640]{3,2,1,0:T(8,128)(2,1)S(1)}, bf16[4,16,16,640]{3,2,1,0:T(8,128)(2,1)S(1)}) custom-call(s32[4]{0:T(128)S(1)} %pad_add_fusion.1.pos, bf16[1024,1024]{1,0:T(8,128)(2,1)S(1)} %get-tuple-element.131.act1, bf16[1024,1024]{1,0:T(8,128)(2,1)S(1)} %get-tuple-element.132.act2, bf16[1024,256]{1,0:T(8,128)(2,1)S(1)} %get-tuple-element.133.gl, ...), custom_call_target="tpu_custom_call" | custom-call | flops 2684354560 | bytes 8388608 | tf_op jit(solution)/shard_map/outer_grads/pallas_call | solution.py:337
  129.8 3.0 %first_grads_13.1 = (bf16[2,16,16,1024]{3,2,1,0:T(8,128)(2,1)S(1)}, bf16[2,16,16,1024]{3,2,1,0:T(8,128)(2,1)S(1)}) custom-call(s32[4]{0:T(128)S(1)} %pad_add_fusion.1.pos, bf16[1024,128]{1,0:T(8,128)(2,1)S(1)} %collective-permute-done.1.refs_9_.refs_0_, bf16[1056,128]{1,0:T(8,128)(2,1)S(1)} %collective-permute-done.5.lab3.refs_10_.refs_1_, ...), custom_call_target="tpu_custom_call" | custom-call | flops 2147483648 | bytes 6291456 | tf_op jit(solution)/shard_map/first_grads_13/pallas_call | solution.py:367
  133.5 3.2 %collective-permute-start.18 = (bf16[8,16,640]{2,1,0:T(8,128)(2,1)S(1)}, bf16[8,16,640]{2,1,0:T(8,128)(2,1)S(1)}, u32[]{:S(2)}, u32[]{:S(2)}) collective-permute-start(bf16[8,16,640]{2,1,0:T(8,128)(2,1)S(1)} %get-tuple-element.142), channel_id=1, source_target_pairs={{0,96},{32,0},{64,32},{96,64},{1,97},{33,1},{65,33},{97,65},{2,98}... | collective-permute-start | bytes 491528 | tf_op jit(solution)/shard_map/ppermute | solution.py:455
  136.7 4.2 %collective-permute-done.17.ahead = bf16[8,16,640]{2,1,0:T(8,128)(2,1)S(1)} collective-permute-done((bf16[8,16,640]{2,1,0:T(8,128)(2,1)S(1)}, bf16[8,16,640]{2,1,0:T(8,128)(2,1)S(1)}, u32[]{:S(2)}, u32[]{:S(2)}) %collective-permute-start.17) | collective-permute-done | bytes 163872 | tf_op jit(solution)/shard_map/ppermute | solution.py:455
  144.7 3.2 %collective-permute-start.26 = (bf16[16,16,640]{2,1,0:T(8,128)(2,1)S(1)}, bf16[16,16,640]{2,1,0:T(8,128)(2,1)S(1)}, u32[]{:S(2)}, u32[]{:S(2)}) collective-permute-start(bf16[16,16,640]{2,1,0:T(8,128)(2,1)S(1)} %get-tuple-element.158), channel_id=1, source_target_pairs={{0,96},{32,0},{64,32},{96,64},{1,97},{33,1},{65,33},{97,65},{2,98}... | collective-permute-start | bytes 983048 | tf_op jit(solution)/shard_map/ppermute | solution.py:455
  151.5 2.7 %collective-permute-start.24 = (bf16[16,16,1024]{2,1,0:T(8,128)(2,1)S(1)}, bf16[16,16,1024]{2,1,0:T(8,128)(2,1)S(1)}, u32[]{:S(2)}, u32[]{:S(2)}) collective-permute-start(bf16[16,16,1024]{2,1,0:T(8,128)(2,1)S(1)} %get-tuple-element.154), channel_id=1, source_target_pairs={{0,3},{1,0},{2,1},{3,2},{4,7},{5,4},{6,5},{7,6},{8,11},{9,8},{10,9... | collective-permute-start | bytes 1572872 | tf_op jit(solution)/shard_map/ppermute | solution.py:455
  155.1 3.8 %all-to-all-start.4 = ((bf16[16,16,640]{2,1,0:T(8,128)(2,1)}), bf16[16,16,640]{2,1,0:T(8,128)(2,1)S(1)}, u32[]{:S(2)}, u32[]{:S(2)}) async-start(bf16[16,16,640]{2,1,0:T(8,128)(2,1)} %own_middle.1), calls=%async_computation.4 | async-start | bytes 655360 | tf_op jit(solution)/shard_map/all_to_all | solution.py:459
  159.0 11.0 %collective-permute-done.23.r1 = bf16[16,16,1024]{2,1,0:T(8,128)(2,1)S(1)} collective-permute-done((bf16[16,16,1024]{2,1,0:T(8,128)(2,1)}, bf16[16,16,1024]{2,1,0:T(8,128)(2,1)S(1)}, u32[]{:S(2)}, u32[]{:S(2)}) %collective-permute-start.23) | collective-permute-done | bytes 524320 | tf_op jit(solution)/shard_map/ppermute | solution.py:455
  170.2 15.9 %all_to_all.25.part_f = bf16[16,16,1024]{2,1,0:T(8,128)(2,1)S(1)} all-to-all(bf16[16,16,1024]{2,1,0:T(8,128)(2,1)S(1)} %own_first.1), channel_id=1, replica_groups=mesh['y'=4,'x'=4,'core'=2,'rep'=4] {'y','x'}, dimensions={0} | all-to-all | bytes 1048576 | tf_op jit(solution)/shard_map/all_to_all | solution.py:459
  (90 shorter events, 29.0 us)
Async XLA Ops:
  5.2 19.4 %all-to-all-start = ((bf16[16,144,128]{2,1,0:T(8,128)(2,1)}), bf16[16,144,128]{2,1,0:T(8,128)(2,1)S(1)}, u32[]{:S(2)}, u32[]{:S(2)}) async-start(bf16[16,144,128]{2,1,0:T(8,128)(2,1)} %get-tuple-element.82), calls=%async_computation | async-start | bytes 1179648 | tf_op jit(solution)/shard_map/all_to_all | solution.py:459
  12.3 10.1 %collective-permute-start = (bf16[1024,128]{1,0:T(8,128)(2,1)S(1)}, bf16[1024,128]{1,0:T(8,128)(2,1)S(1)}, u32[]{:S(2)}, u32[]{:S(2)}) collective-permute-start(bf16[1024,128]{1,0:T(8,128)(2,1)S(1)} %get-tuple-element.83), channel_id=1, source_target_pairs={{0,1},{1,2},{2,3},{3,0},{4,5},{5,6},{6,7},{7,4},{8,9},{9,10},{10,1... | collective-permute-start | bytes 786440 | tf_op jit(solution)/shard_map/ppermute | solution.py:455
  14.3 8.1 %collective-permute-start.1 = (bf16[1024,128]{1,0:T(8,128)(2,1)S(1)}, bf16[1024,128]{1,0:T(8,128)(2,1)S(1)}, u32[]{:S(2)}, u32[]{:S(2)}) collective-permute-start(bf16[1024,128]{1,0:T(8,128)(2,1)S(1)} %get-tuple-element.84), channel_id=1, source_target_pairs={{0,3},{1,0},{2,1},{3,2},{4,7},{5,4},{6,5},{7,6},{8,11},{9,8},{10,9... | collective-permute-start | bytes 786440 | tf_op jit(solution)/shard_map/ppermute | solution.py:455
  24.6 4.7 %collective-permute-start.2 = (bf16[16,144,128]{2,1,0:T(8,128)(2,1)S(1)}, bf16[16,144,128]{2,1,0:T(8,128)(2,1)S(1)}, u32[]{:S(2)}, u32[]{:S(2)}) collective-permute-start(bf16[16,144,128]{2,1,0:T(8,128)(2,1)S(1)} %all-to-all-done.near), channel_id=1, source_target_pairs={{0,4},{4,0},{1,5},{5,1},{2,6},{6,2},{3,7},{7,3},{8,12},{12,8},{9,1... | collective-permute-start | bytes 1769480 | tf_op jit(solution)/shard_map/ppermute | solution.py:455
  24.6 13.6 %collective-permute-start.3 = (bf16[1024,128]{1,0:T(8,128)(2,1)S(1)}, bf16[1024,128]{1,0:T(8,128)(2,1)S(1)}, u32[]{:S(2)}, u32[]{:S(2)}) collective-permute-start(bf16[1024,128]{1,0:T(8,128)(2,1)S(1)} %get-tuple-element.92), channel_id=1, source_target_pairs={{0,2},{1,3},{2,0},{3,1},{4,6},{5,7},{6,4},{7,5},{8,10},{9,11},{10,... | collective-permute-start | bytes 786440 | tf_op jit(solution)/shard_map/ppermute | solution.py:455
  38.2 15.8 %all-to-all-start.1 = ((bf16[16,128,128]{2,1,0:T(8,128)(2,1)}), bf16[16,128,128]{2,1,0:T(8,128)(2,1)S(1)}, u32[]{:S(2)}, u32[]{:S(2)}) async-start(bf16[16,128,128]{2,1,0:T(8,128)(2,1)} %get-tuple-element.95), calls=%async_computation.1 | async-start | bytes 1048576 | tf_op jit(solution)/shard_map/all_to_all | solution.py:459
  42.1 30.8 %copy-start.5 = (bf16[1056,128]{1,0:T(8,128)(2,1)S(1)}, bf16[1056,128]{1,0:T(8,128)(2,1)}, u32[]{:S(2)}) copy-start(bf16[1056,128]{1,0:T(8,128)(2,1)} %get-tuple-element.93.lab0.refs_1_) | copy-start | bytes 811012
  42.1 9.8 %collective-permute-start.4 = (bf16[1056,128]{1,0:T(8,128)(2,1)}, bf16[1056,128]{1,0:T(8,128)(2,1)S(1)}, u32[]{:S(2)}, u32[]{:S(2)}) collective-permute-start(bf16[1056,128]{1,0:T(8,128)(2,1)} %get-tuple-element.96), channel_id=1, source_target_pairs={{0,1},{1,2},{2,3},{3,0},{4,5},{5,6},{6,7},{7,4},{8,9},{9,10},{10,1... | collective-permute-start | bytes 811016 | tf_op jit(solution)/shard_map/ppermute | solution.py:455
  43.2 8.8 %collective-permute-start.5 = (bf16[1056,128]{1,0:T(8,128)(2,1)}, bf16[1056,128]{1,0:T(8,128)(2,1)S(1)}, u32[]{:S(2)}, u32[]{:S(2)}) collective-permute-start(bf16[1056,128]{1,0:T(8,128)(2,1)} %get-tuple-element.97), channel_id=1, source_target_pairs={{0,3},{1,0},{2,1},{3,2},{4,7},{5,4},{6,5},{7,6},{8,11},{9,8},{10,9... | collective-permute-start | bytes 811016 | tf_op jit(solution)/shard_map/ppermute | solution.py:455
  54.0 1.9 %collective-permute-start.6 = (bf16[16,128,128]{2,1,0:T(8,128)(2,1)S(1)}, bf16[16,128,128]{2,1,0:T(8,128)(2,1)S(1)}, u32[]{:S(2)}, u32[]{:S(2)}) collective-permute-start(bf16[16,128,128]{2,1,0:T(8,128)(2,1)S(1)} %all-to-all-done.1.near), channel_id=1, source_target_pairs={{0,4},{4,0},{1,5},{5,1},{2,6},{6,2},{3,7},{7,3},{8,12},{12,8},{9,1... | collective-permute-start | bytes 1572872 | tf_op jit(solution)/shard_map/ppermute | solution.py:455
  54.0 10.6 %collective-permute-start.7 = (bf16[1056,128]{1,0:T(8,128)(2,1)}, bf16[1056,128]{1,0:T(8,128)(2,1)S(1)}, u32[]{:S(2)}, u32[]{:S(2)}) collective-permute-start(bf16[1056,128]{1,0:T(8,128)(2,1)} %get-tuple-element.105), channel_id=1, source_target_pairs={{0,2},{1,3},{2,0},{3,1},{4,6},{5,7},{6,4},{7,5},{8,10},{9,11},{10,... | collective-permute-start | bytes 811016 | tf_op jit(solution)/shard_map/ppermute | solution.py:455
  64.6 16.9 %all-to-all-start.2 = ((bf16[16,128,128]{2,1,0:T(8,128)(2,1)}), bf16[16,128,128]{2,1,0:T(8,128)(2,1)}, u32[]{:S(2)}, u32[]{:S(2)}) async-start(bf16[16,128,128]{2,1,0:T(8,128)(2,1)} %get-tuple-element.108), calls=%async_computation.2 | async-start | bytes 1048576 | tf_op jit(solution)/shard_map/all_to_all | solution.py:459
  69.6 9.6 %collective-permute-start.8 = (bf16[1024,128]{1,0:T(8,128)(2,1)}, bf16[1024,128]{1,0:T(8,128)(2,1)S(1)}, u32[]{:S(2)}, u32[]{:S(2)}) collective-permute-start(bf16[1024,128]{1,0:T(8,128)(2,1)} %get-tuple-element.109), channel_id=1, source_target_pairs={{0,1},{1,2},{2,3},{3,0},{4,5},{5,6},{6,7},{7,4},{8,9},{9,10},{10,1... | collective-permute-start | bytes 786440 | tf_op jit(solution)/shard_map/ppermute | solution.py:455
  71.6 8.0 %collective-permute-start.9 = (bf16[1024,128]{1,0:T(8,128)(2,1)}, bf16[1024,128]{1,0:T(8,128)(2,1)S(1)}, u32[]{:S(2)}, u32[]{:S(2)}) collective-permute-start(bf16[1024,128]{1,0:T(8,128)(2,1)} %get-tuple-element.110), channel_id=1, source_target_pairs={{0,3},{1,0},{2,1},{3,2},{4,7},{5,4},{6,5},{7,6},{8,11},{9,8},{10,9... | collective-permute-start | bytes 786440 | tf_op jit(solution)/shard_map/ppermute | solution.py:455
  81.5 3.0 %collective-permute-start.10 = (bf16[16,128,128]{2,1,0:T(8,128)(2,1)}, bf16[16,128,128]{2,1,0:T(8,128)(2,1)}, u32[]{:S(2)}, u32[]{:S(2)}) collective-permute-start(bf16[16,128,128]{2,1,0:T(8,128)(2,1)} %all-to-all-done.2.near), channel_id=1, source_target_pairs={{0,4},{4,0},{1,5},{5,1},{2,6},{6,2},{3,7},{7,3},{8,12},{12,8},{9,1... | collective-permute-start | bytes 1572872 | tf_op jit(solution)/shard_map/ppermute | solution.py:455
  81.5 10.8 %collective-permute-start.11 = (bf16[1024,128]{1,0:T(8,128)(2,1)}, bf16[1024,128]{1,0:T(8,128)(2,1)S(1)}, u32[]{:S(2)}, u32[]{:S(2)}) collective-permute-start(bf16[1024,128]{1,0:T(8,128)(2,1)} %get-tuple-element.119), channel_id=1, source_target_pairs={{0,2},{1,3},{2,0},{3,1},{4,6},{5,7},{6,4},{7,5},{8,10},{9,11},{10,... | collective-permute-start | bytes 786440 | tf_op jit(solution)/shard_map/ppermute | solution.py:455
  92.3 10.6 %collective-permute-start.12 = (bf16[1024,128]{1,0:T(8,128)(2,1)}, bf16[1024,128]{1,0:T(8,128)(2,1)S(1)}, u32[]{:S(2)}, u32[]{:S(2)}) collective-permute-start(bf16[1024,128]{1,0:T(8,128)(2,1)} %get-tuple-element.121), channel_id=1, source_target_pairs={{0,1},{1,2},{2,3},{3,0},{4,5},{5,6},{6,7},{7,4},{8,9},{9,10},{10,1... | collective-permute-start | bytes 786440 | tf_op jit(solution)/shard_map/ppermute | solution.py:455
  94.4 14.6 %collective-permute-start.13 = (bf16[1024,128]{1,0:T(8,128)(2,1)}, bf16[1024,128]{1,0:T(8,128)(2,1)S(1)}, u32[]{:S(2)}, u32[]{:S(2)}) collective-permute-start(bf16[1024,128]{1,0:T(8,128)(2,1)} %get-tuple-element.122), channel_id=1, source_target_pairs={{0,2},{1,3},{2,0},{3,1},{4,6},{5,7},{6,4},{7,5},{8,10},{9,11},{10,... | collective-permute-start | bytes 786440 | tf_op jit(solution)/shard_map/ppermute | solution.py:455
  96.7 12.2 %collective-permute-start.14 = (bf16[1024,128]{1,0:T(8,128)(2,1)}, bf16[1024,128]{1,0:T(8,128)(2,1)S(1)}, u32[]{:S(2)}, u32[]{:S(2)}) collective-permute-start(bf16[1024,128]{1,0:T(8,128)(2,1)} %get-tuple-element.123), channel_id=1, source_target_pairs={{0,3},{1,0},{2,1},{3,2},{4,7},{5,4},{6,5},{7,6},{8,11},{9,8},{10,9... | collective-permute-start | bytes 786440 | tf_op jit(solution)/shard_map/ppermute | solution.py:455
  126.7 3.1 %collective-permute-start.15 = (bf16[4,16,16,640]{3,2,1,0:T(8,128)(2,1)S(1)}, bf16[4,16,16,640]{3,2,1,0:T(8,128)(2,1)S(1)}, u32[]{:S(2)}, u32[]{:S(2)}) collective-permute-start(bf16[4,16,16,640]{3,2,1,0:T(8,128)(2,1)S(1)} %get-tuple-element.135), channel_id=1, source_target_pairs={{0,4},{4,0},{1,5},{5,1},{2,6},{6,2},{3,7},{7,3},{8,12},{12,8},{9,1... | collective-permute-start | bytes 3932168 | tf_op jit(solution)/shard_map/ppermute | solution.py:455
  132.8 17.1 %collective-permute-start.20 = (bf16[2,16,16,1024]{3,2,1,0:T(8,128)(2,1)S(1)}, bf16[2,16,16,1024]{3,2,1,0:T(8,128)(2,1)S(1)}, u32[]{:S(2)}, u32[]{:S(2)}) collective-permute-start(bf16[2,16,16,1024]{3,2,1,0:T(8,128)(2,1)S(1)} %get-tuple-element.148), channel_id=1, source_target_pairs={{0,4},{4,0},{1,5},{5,1},{2,6},{6,2},{3,7},{7,3},{8,12},{12,8},{9,1... | collective-permute-start | bytes 3145736 | tf_op jit(solution)/shard_map/ppermute | solution.py:455
  133.0 8.0 %collective-permute-start.16 = (bf16[1,16,16,1024]{3,2,1,0:T(8,128)(2,1)S(1)}, bf16[1,16,16,1024]{3,2,1,0:T(8,128)(2,1)S(1)}, u32[]{:S(2)}, u32[]{:S(2)}) collective-permute-start(bf16[1,16,16,1024]{3,2,1,0:T(8,128)(2,1)S(1)} %get-tuple-element.138), channel_id=1, source_target_pairs={{0,4},{4,0},{1,5},{5,1},{2,6},{6,2},{3,7},{7,3},{8,12},{12,8},{9,1... | collective-permute-start | bytes 1572872 | tf_op jit(solution)/shard_map/ppermute | solution.py:455
  133.4 7.5 %collective-permute-start.17 = (bf16[8,16,640]{2,1,0:T(8,128)(2,1)S(1)}, bf16[8,16,640]{2,1,0:T(8,128)(2,1)S(1)}, u32[]{:S(2)}, u32[]{:S(2)}) collective-permute-start(bf16[8,16,640]{2,1,0:T(8,128)(2,1)S(1)} %get-tuple-element.141), channel_id=1, source_target_pairs={{0,32},{32,64},{64,96},{96,0},{1,33},{33,65},{65,97},{97,1},{2,34}... | collective-permute-start | bytes 491528 | tf_op jit(solution)/shard_map/ppermute | solution.py:455
  133.5 7.4 %collective-permute-start.18 = (bf16[8,16,640]{2,1,0:T(8,128)(2,1)S(1)}, bf16[8,16,640]{2,1,0:T(8,128)(2,1)S(1)}, u32[]{:S(2)}, u32[]{:S(2)}) collective-permute-start(bf16[8,16,640]{2,1,0:T(8,128)(2,1)S(1)} %get-tuple-element.142), channel_id=1, source_target_pairs={{0,96},{32,0},{64,32},{96,64},{1,97},{33,1},{65,33},{97,65},{2,98}... | collective-permute-start | bytes 491528 | tf_op jit(solution)/shard_map/ppermute | solution.py:455
  141.1 8.8 %collective-permute-start.21 = (bf16[8,16,1024]{2,1,0:T(8,128)(2,1)S(1)}, bf16[8,16,1024]{2,1,0:T(8,128)(2,1)S(1)}, u32[]{:S(2)}, u32[]{:S(2)}) collective-permute-start(bf16[8,16,1024]{2,1,0:T(8,128)(2,1)S(1)} %get-tuple-element.151), channel_id=1, source_target_pairs={{0,1},{1,2},{2,3},{3,0},{4,5},{5,6},{6,7},{7,4},{8,9},{9,10},{10,1... | collective-permute-start | bytes 786440 | tf_op jit(solution)/shard_map/ppermute | solution.py:455
  142.6 7.3 %collective-permute-start.22 = (bf16[8,16,1024]{2,1,0:T(8,128)(2,1)S(1)}, bf16[8,16,1024]{2,1,0:T(8,128)(2,1)S(1)}, u32[]{:S(2)}, u32[]{:S(2)}) collective-permute-start(bf16[8,16,1024]{2,1,0:T(8,128)(2,1)S(1)} %get-tuple-element.152), channel_id=1, source_target_pairs={{0,3},{1,0},{2,1},{3,2},{4,7},{5,4},{6,5},{7,6},{8,11},{9,8},{10,9... | collective-permute-start | bytes 786440 | tf_op jit(solution)/shard_map/ppermute | solution.py:455
  144.6 9.6 %collective-permute-start.25 = (bf16[16,16,640]{2,1,0:T(8,128)(2,1)S(1)}, bf16[16,16,640]{2,1,0:T(8,128)(2,1)S(1)}, u32[]{:S(2)}, u32[]{:S(2)}) collective-permute-start(bf16[16,16,640]{2,1,0:T(8,128)(2,1)S(1)} %get-tuple-element.157), channel_id=1, source_target_pairs={{0,32},{32,64},{64,96},{96,0},{1,33},{33,65},{65,97},{97,1},{2,34}... | collective-permute-start | bytes 983048 | tf_op jit(solution)/shard_map/ppermute | solution.py:455
  144.7 9.6 %collective-permute-start.26 = (bf16[16,16,640]{2,1,0:T(8,128)(2,1)S(1)}, bf16[16,16,640]{2,1,0:T(8,128)(2,1)S(1)}, u32[]{:S(2)}, u32[]{:S(2)}) collective-permute-start(bf16[16,16,640]{2,1,0:T(8,128)(2,1)S(1)} %get-tuple-element.158), channel_id=1, source_target_pairs={{0,96},{32,0},{64,32},{96,64},{1,97},{33,1},{65,33},{97,65},{2,98}... | collective-permute-start | bytes 983048 | tf_op jit(solution)/shard_map/ppermute | solution.py:455
  149.9 9.1 %collective-permute-start.19 = (bf16[1,16,16,1024]{3,2,1,0:T(8,128)(2,1)S(1)}, bf16[1,16,16,1024]{3,2,1,0:T(8,128)(2,1)S(1)}, u32[]{:S(2)}, u32[]{:S(2)}) collective-permute-start(bf16[1,16,16,1024]{3,2,1,0:T(8,128)(2,1)S(1)} %get-tuple-element.146), channel_id=1, source_target_pairs={{0,4},{4,0},{1,5},{5,1},{2,6},{6,2},{3,7},{7,3},{8,12},{12,8},{9,1... | collective-permute-start | bytes 1572872 | tf_op jit(solution)/shard_map/ppermute | solution.py:455
  150.9 19.0 %collective-permute-start.23 = (bf16[16,16,1024]{2,1,0:T(8,128)(2,1)}, bf16[16,16,1024]{2,1,0:T(8,128)(2,1)S(1)}, u32[]{:S(2)}, u32[]{:S(2)}) collective-permute-start(bf16[16,16,1024]{2,1,0:T(8,128)(2,1)} %get-tuple-element.153), channel_id=1, source_target_pairs={{0,1},{1,2},{2,3},{3,0},{4,5},{5,6},{6,7},{7,4},{8,9},{9,10},{10,1... | collective-permute-start | bytes 1572872 | tf_op jit(solution)/shard_map/ppermute | solution.py:455
  151.5 18.5 %collective-permute-start.24 = (bf16[16,16,1024]{2,1,0:T(8,128)(2,1)S(1)}, bf16[16,16,1024]{2,1,0:T(8,128)(2,1)S(1)}, u32[]{:S(2)}, u32[]{:S(2)}) collective-permute-start(bf16[16,16,1024]{2,1,0:T(8,128)(2,1)S(1)} %get-tuple-element.154), channel_id=1, source_target_pairs={{0,3},{1,0},{2,1},{3,2},{4,7},{5,4},{6,5},{7,6},{8,11},{9,8},{10,9... | collective-permute-start | bytes 1572872 | tf_op jit(solution)/shard_map/ppermute | solution.py:455
  155.1 15.1 %all-to-all-start.4 = ((bf16[16,16,640]{2,1,0:T(8,128)(2,1)}), bf16[16,16,640]{2,1,0:T(8,128)(2,1)S(1)}, u32[]{:S(2)}, u32[]{:S(2)}) async-start(bf16[16,16,640]{2,1,0:T(8,128)(2,1)} %own_middle.1), calls=%async_computation.4 | async-start | bytes 655360 | tf_op jit(solution)/shard_map/all_to_all | solution.py:459
  (16 other events, 161.8 us)
where the time goes:
time: 188 us; the launch traced here: 187 us
  Pallas kernels  62.7 us (33%)
  starting transfers between devices  56.2 us (30%)
  waiting for transfers between devices  43.8 us (23%)
  blocking collectives  15.9 us (8%)
  local copies, waits for them, and re-layouts  6.64 us (4%)
    ppermute x27, waiting for transfers between devices, shift(): lax.ppermute(value, axis, [(i, (i + by) % size) for i in range(size)])  37.7 us
    ppermute x27, starting transfers between devices, shift(): lax.ppermute(value, axis, [(i, (i + by) % size) for i in range(size)])  36.3 us
    pallas_call x3, Pallas kernels, propagate(): pl.pallas_call(functools.partial(prop_kernel, h), in_specs=[whole(pltpu.S...  23.7 us
    all_to_all x4, starting transfers between devices, swap(): return lax.all_to_all(value, axes, split_axis=0, concat_axis=0, tiled=True)  19.9 us
    all_to_all x1, blocking collectives, swap(): return lax.all_to_all(value, axes, split_axis=0, concat_axis=0, tiled=True)  15.9 us
    pallas_call x1, Pallas kernels, mlp(): pl.pallas_call(mlp_kernel, grid_spec=pltpu.PrefetchScalarGridSpec(num_sca...  14 us
    pallas_call x3, Pallas kernels, first_grads(): pl.pallas_call(functools.partial(first_kernel, steps), in_specs=[whole(pl...  6.67 us
    unnamed x35, local copies, waits for them, and re-layouts  6.38 us
  transfers between devices with their start and end apart: 31, of which 14 were waited for; matrix products, arithmetic and copies ran while one was open for 1% of the time, Pallas kernels for 21%

commit v1 on v0

--- a/solution.py
+++ b/solution.py
@@ -513,12 +513,12 @@
     keep_m, send_m = outer_grads(pos, act1, act2, gl, gm)
     got_m = shift(send_m, "core", 1)
     keep2, send2 = first_grads(pos, pieces, gf, (2,))
-    got_m, send2, gf = lax.optimization_barrier((got_m, send2, gf))
     got2 = shift(send2, "core", 1)
-    far_m = send_far(2, keep_m, got_m, "y", "middle")
+    keep2, gf = lax.optimization_barrier((keep2, gf))
     keep13, send13 = first_grads(pos, pieces, gf, (1, 3))
     got13 = shift(send13, "core", 1)
-    got2, far_m, gf = lax.optimization_barrier((got2, far_m, gf))
+    got_m, got2, keep13, gf = lax.optimization_barrier((got_m, got2, keep13, gf))
+    far_m = send_far(2, keep_m, got_m, "y", "middle")
     far_f = send_far(0, keep2, got2, "rep", "first")
     keep0, send0 = first_grads(pos, pieces, gf, (0,))
     got0 = shift(send0, "core", 1)

time: 188 us -> 185 us (0.984)
  waiting for transfers between devices: 43.8 us -> 41.5 us
    ppermute x27, waiting for transfers between devices: 37.7 us -> 35 us  [shift(): lax.ppermute(value, axis, [(i, (i + by) % size) for i in range(size)])]
  transfers between devices with their start and end apart: 31 -> 31, of which waited for: 14 -> 14; matrix products, arithmetic and copies ran while one was open for 1% -> 1% of each run, Pallas kernels for 21% -> 23%
where the time goes in v1:
time: 185 us; the launch traced here: 184 us
  Pallas kernels  62.7 us (34%)
  starting transfers between devices  57.3 us (31%)
  waiting for transfers between devices  41.5 us (22%)
  blocking collectives  14.1 us (8%)
  local copies, waits for them, and re-layouts  6.64 us (4%)
    ppermute x27, starting transfers between devices, shift(): lax.ppermute(value, axis, [(i, (i + by) % size) for i in range(size)])  36.4 us
    ppermute x27, waiting for transfers between devices, shift(): lax.ppermute(value, axis, [(i, (i + by) % size) for i in range(size)])  35 us
    pallas_call x3, Pallas kernels, propagate(): pl.pallas_call(functools.partial(prop_kernel, h), in_specs=[whole(pltpu.S...  23.7 us
    all_to_all x4, starting transfers between devices, swap(): return lax.all_to_all(value, axes, split_axis=0, concat_axis=0, tiled=True)  20.8 us
    all_to_all x1, blocking collectives, swap(): return lax.all_to_all(value, axes, split_axis=0, concat_axis=0, tiled=True)  14.1 us
    pallas_call x1, Pallas kernels, mlp(): pl.pallas_call(mlp_kernel, grid_spec=pltpu.PrefetchScalarGridSpec(num_sca...  14 us
    pallas_call x3, Pallas kernels, first_grads(): pl.pallas_call(functools.partial(first_kernel, steps), in_specs=[whole(pl...  6.68 us
    all_to_all x4, waiting for transfers between devices, swap(): return lax.all_to_all(value, axes, split_axis=0, concat_axis=0, tiled=True)  6.54 us
  transfers between devices with their start and end apart: 31, of which 14 were waited for; matrix products, arithmetic and copies ran while one was open for 1% of the time, Pallas kernels for 23%

profile of v1, /device:TPU:0, one launch (start us, length us, event | category | flops | bytes accessed | tf_op | source)
XLA Modules:
  0.0 184.0 jit_solution(373488776698841898)
XLA Ops:
  3.3 1.9 %export_first.1 = (bf16[16,144,128]{2,1,0:T(8,128)(2,1)}, bf16[1024,128]{1,0:T(8,128)(2,1)S(1)}, bf16[1024,128]{1,0:T(8,128)(2,1)S(1)}, bf16[1024,128]{1,0:T(8,128)(2,1)S(1)}, bf16[1024,128]{1,0:T(8,128)(2,1)S(1)}) custom-call(s32[4]{0:T(128)S(1)} %pad_add_fusion.1.pos, bf16[4096,128]{1,0:T(8,128)(2,1)S(1)} %copy-done, s32[1,128]{1,0:T(1,128)S(1)} %copy-done.1, ...), custom_call_target="tpu_custom_call" | custom-call | flops 134217728 | bytes 2097152 | tf_op jit(solution)/shard_map/export_first/pallas_call | solution.py:83
  5.2 7.1 %all-to-all-start = ((bf16[16,144,128]{2,1,0:T(8,128)(2,1)}), bf16[16,144,128]{2,1,0:T(8,128)(2,1)S(1)}, u32[]{:S(2)}, u32[]{:S(2)}) async-start(bf16[16,144,128]{2,1,0:T(8,128)(2,1)} %get-tuple-element.81), calls=%async_computation | async-start | bytes 1179648 | tf_op jit(solution)/shard_map/all_to_all | solution.py:459
  12.3 2.0 %collective-permute-start = (bf16[1024,128]{1,0:T(8,128)(2,1)S(1)}, bf16[1024,128]{1,0:T(8,128)(2,1)S(1)}, u32[]{:S(2)}, u32[]{:S(2)}) collective-permute-start(bf16[1024,128]{1,0:T(8,128)(2,1)S(1)} %get-tuple-element.82), channel_id=1, source_target_pairs={{0,1},{1,2},{2,3},{3,0},{4,5},{5,6},{6,7},{7,4},{8,9},{9,10},{10,1... | collective-permute-start | bytes 786440 | tf_op jit(solution)/shard_map/ppermute | solution.py:455
  14.3 2.2 %collective-permute-start.1 = (bf16[1024,128]{1,0:T(8,128)(2,1)S(1)}, bf16[1024,128]{1,0:T(8,128)(2,1)S(1)}, u32[]{:S(2)}, u32[]{:S(2)}) collective-permute-start(bf16[1024,128]{1,0:T(8,128)(2,1)S(1)} %get-tuple-element.83), channel_id=1, source_target_pairs={{0,3},{1,0},{2,1},{3,2},{4,7},{5,4},{6,5},{7,6},{8,11},{9,8},{10,9... | collective-permute-start | bytes 786440 | tf_op jit(solution)/shard_map/ppermute | solution.py:455
  16.5 5.9 %collective-permute-done.refs_3_.refs_4_ = bf16[1024,128]{1,0:T(8,128)(2,1)S(1)} collective-permute-done((bf16[1024,128]{1,0:T(8,128)(2,1)S(1)}, bf16[1024,128]{1,0:T(8,128)(2,1)S(1)}, u32[]{:S(2)}, u32[]{:S(2)}) %collective-permute-start) | collective-permute-done | bytes 262176 | tf_op jit(solution)/shard_map/ppermute | solution.py:455
  22.5 2.1 %all-to-all-done.near = bf16[16,144,128]{2,1,0:T(8,128)(2,1)S(1)} async-done(((bf16[16,144,128]{2,1,0:T(8,128)(2,1)}), bf16[16,144,128]{2,1,0:T(8,128)(2,1)S(1)}, u32[]{:S(2)}, u32[]{:S(2)}) %all-to-all-start) | async-done | bytes 589856 | tf_op jit(solution)/shard_map/all_to_all | solution.py:459
  24.6 3.9 %collective-permute-start.3 = (bf16[1024,128]{1,0:T(8,128)(2,1)S(1)}, bf16[1024,128]{1,0:T(8,128)(2,1)S(1)}, u32[]{:S(2)}, u32[]{:S(2)}) collective-permute-start(bf16[1024,128]{1,0:T(8,128)(2,1)S(1)} %get-tuple-element.91), channel_id=1, source_target_pairs={{0,2},{1,3},{2,0},{3,1},{4,6},{5,7},{6,4},{7,5},{8,10},{9,11},{10,... | collective-permute-start | bytes 786440 | tf_op jit(solution)/shard_map/ppermute | solution.py:455
  30.1 8.1 %propagate_0.1 = (bf16[4096,128]{1,0:T(8,128)(2,1)}, bf16[16,128,128]{2,1,0:T(8,128)(2,1)}, bf16[1056,128]{1,0:T(8,128)(2,1)}, bf16[1056,128]{1,0:T(8,128)(2,1)}...) custom-call(s32[259]{0:T(512)} %pad_add_fusion.cols, bf16[32,8,128,128]{3,2,1,0:T(8,128)(2,1)} %tiles.5, ...), custom_call_target="tpu_custom_call" | custom-call | flops 1073741824 | bytes 12582912 | tf_op jit(solution)/shard_map/propagate_0/pallas_call | solution.py:164
  38.2 3.9 %all-to-all-start.1 = ((bf16[16,128,128]{2,1,0:T(8,128)(2,1)}), bf16[16,128,128]{2,1,0:T(8,128)(2,1)S(1)}, u32[]{:S(2)}, u32[]{:S(2)}) async-start(bf16[16,128,128]{2,1,0:T(8,128)(2,1)} %get-tuple-element.94), calls=%async_computation.1 | async-start | bytes 1048576 | tf_op jit(solution)/shard_map/all_to_all | solution.py:459
  43.2 2.3 %collective-permute-start.5 = (bf16[1056,128]{1,0:T(8,128)(2,1)}, bf16[1056,128]{1,0:T(8,128)(2,1)S(1)}, u32[]{:S(2)}, u32[]{:S(2)}) collective-permute-start(bf16[1056,128]{1,0:T(8,128)(2,1)} %get-tuple-element.96), channel_id=1, source_target_pairs={{0,3},{1,0},{2,1},{3,2},{4,7},{5,4},{6,5},{7,6},{8,11},{9,8},{10,9... | collective-permute-start | bytes 811016 | tf_op jit(solution)/shard_map/ppermute | solution.py:455
  45.4 6.5 %collective-permute-done.4.lab1.refs_4_.refs_5_ = bf16[1056,128]{1,0:T(8,128)(2,1)S(1)} collective-permute-done((bf16[1056,128]{1,0:T(8,128)(2,1)}, bf16[1056,128]{1,0:T(8,128)(2,1)S(1)}, u32[]{:S(2)}, u32[]{:S(2)}) %collective-permute-start.4) | collective-permute-done | bytes 270368 | tf_op jit(solution)/shard_map/ppermute | solution.py:455
  51.9 2.0 %all-to-all-done.1.near = bf16[16,128,128]{2,1,0:T(8,128)(2,1)S(1)} async-done(((bf16[16,128,128]{2,1,0:T(8,128)(2,1)}), bf16[16,128,128]{2,1,0:T(8,128)(2,1)S(1)}, u32[]{:S(2)}, u32[]{:S(2)}) %all-to-all-start.1) | async-done | bytes 524320 | tf_op jit(solution)/shard_map/all_to_all | solution.py:459
  56.7 7.9 %propagate_1.1 = (bf16[4096,128]{1,0:T(8,128)(2,1)}, bf16[16,128,128]{2,1,0:T(8,128)(2,1)}, bf16[1024,128]{1,0:T(8,128)(2,1)}, bf16[1024,128]{1,0:T(8,128)(2,1)}...) custom-call(s32[259]{0:T(512)} %pad_add_fusion.cols, bf16[32,8,128,128]{3,2,1,0:T(8,128)(2,1)} %tiles.5, ...), custom_call_target="tpu_custom_call" | custom-call | flops 1073741824 | bytes 12582912 | tf_op jit(solution)/shard_map/propagate_1/pallas_call | solution.py:164
  64.6 5.0 %all-to-all-start.2 = ((bf16[16,128,128]{2,1,0:T(8,128)(2,1)}), bf16[16,128,128]{2,1,0:T(8,128)(2,1)}, u32[]{:S(2)}, u32[]{:S(2)}) async-start(bf16[16,128,128]{2,1,0:T(8,128)(2,1)} %get-tuple-element.107), calls=%async_computation.2 | async-start | bytes 1048576 | tf_op jit(solution)/shard_map/all_to_all | solution.py:459
  69.6 2.0 %collective-permute-start.8 = (bf16[1024,128]{1,0:T(8,128)(2,1)}, bf16[1024,128]{1,0:T(8,128)(2,1)S(1)}, u32[]{:S(2)}, u32[]{:S(2)}) collective-permute-start(bf16[1024,128]{1,0:T(8,128)(2,1)} %get-tuple-element.108), channel_id=1, source_target_pairs={{0,1},{1,2},{2,3},{3,0},{4,5},{5,6},{6,7},{7,4},{8,9},{9,10},{10,1... | collective-permute-start | bytes 786440 | tf_op jit(solution)/shard_map/ppermute | solution.py:455
  72.9 3.8 %count_labels.1.refs_5_ = f32[1024,256]{1,0:T(8,128)S(1)} custom-call(s32[4]{0:T(128)S(1)} %pad_add_fusion.1.pos, bf16[1056,128]{1,0:T(8,128)(2,1)S(1)} %copy-done.5, bf16[1056,128]{1,0:T(8,128)(2,1)S(1)} %collective-permute-done.4.lab1.refs_4_.refs_5_, bf16[1056,128]{1,0:T(8,128)(2,1)S(1)} %collective-permute-done.7.lab2.refs_7_.refs_1_, ...), custom_call_target="tpu_custom_call" | custom-call | flops 2147483648 | bytes 2097152 | tf_op jit(solution)/shard_map/count_labels/pallas_call | solution.py:211
  79.6 1.9 %all-to-all-done.2.near = bf16[16,128,128]{2,1,0:T(8,128)(2,1)} async-done(((bf16[16,128,128]{2,1,0:T(8,128)(2,1)}), bf16[16,128,128]{2,1,0:T(8,128)(2,1)}, u32[]{:S(2)}, u32[]{:S(2)}) %all-to-all-start.2) | async-done | bytes 524320 | tf_op jit(solution)/shard_map/all_to_all | solution.py:459
  84.6 7.8 %propagate_2.1 = (bf16[1024,128]{1,0:T(8,128)(2,1)}, bf16[1024,128]{1,0:T(8,128)(2,1)}, bf16[1024,128]{1,0:T(8,128)(2,1)}, bf16[1024,128]{1,0:T(8,128)(2,1)}) custom-call(s32[259]{0:T(512)} %pad_add_fusion.cols, bf16[32,8,128,128]{3,2,1,0:T(8,128)(2,1)} %tiles.5, bf16[4096,128]{1,0:T(8,128)(2,1)} %get-tuple-element.106.hop, ...), custom_call_target="tpu_custom_call" | custom-call | flops 1073741824 | bytes 12582912 | tf_op jit(solution)/shard_map/propagate_2/pallas_call | solution.py:164
  92.3 2.1 %collective-permute-start.12 = (bf16[1024,128]{1,0:T(8,128)(2,1)}, bf16[1024,128]{1,0:T(8,128)(2,1)S(1)}, u32[]{:S(2)}, u32[]{:S(2)}) collective-permute-start(bf16[1024,128]{1,0:T(8,128)(2,1)} %get-tuple-element.120), channel_id=1, source_target_pairs={{0,1},{1,2},{2,3},{3,0},{4,5},{5,6},{6,7},{7,4},{8,9},{9,10},{10,1... | collective-permute-start | bytes 786440 | tf_op jit(solution)/shard_map/ppermute | solution.py:455
  94.4 2.3 %collective-permute-start.13 = (bf16[1024,128]{1,0:T(8,128)(2,1)}, bf16[1024,128]{1,0:T(8,128)(2,1)S(1)}, u32[]{:S(2)}, u32[]{:S(2)}) collective-permute-start(bf16[1024,128]{1,0:T(8,128)(2,1)} %get-tuple-element.121), channel_id=1, source_target_pairs={{0,2},{1,3},{2,0},{3,1},{4,6},{5,7},{6,4},{7,5},{8,10},{9,11},{10,... | collective-permute-start | bytes 786440 | tf_op jit(solution)/shard_map/ppermute | solution.py:455
  97.4 5.6 %first_layer_early.1.refs_4_ = f32[1024,1024]{1,0:T(8,128)S(1)} custom-call(s32[4]{0:T(128)S(1)} %pad_add_fusion.1.pos, bf16[1024,128]{1,0:T(8,128)(2,1)S(1)} %get-tuple-element.80.refs_0_, bf16[1056,128]{1,0:T(8,128)(2,1)S(1)} %copy-done.5, bf16[1024,128]{1,0:T(8,128)(2,1)S(1)} %copy-done.6, bf16[1024,128]{1,0:T(8,128)(2,1)S(1)} %collective-permute-done.refs_3_.refs_4_, ...), custom_call_target="tpu_custom_call" | custom-call | flops 3221225472 | bytes 11534336 | tf_op jit(solution)/shard_map/first_layer_early/pallas_call | solution.py:277
  103.0 6.0 %collective-permute-done.13.refs_2_.refs_3_ = bf16[1024,128]{1,0:T(8,128)(2,1)S(1)} collective-permute-done((bf16[1024,128]{1,0:T(8,128)(2,1)}, bf16[1024,128]{1,0:T(8,128)(2,1)S(1)}, u32[]{:S(2)}, u32[]{:S(2)}) %collective-permute-start.13) | collective-permute-done | bytes 262176 | tf_op jit(solution)/shard_map/ppermute | solution.py:455
  109.0 14.0 %mlp.1 = (bf16[1024,1024]{1,0:T(8,128)(2,1)S(1)}, bf16[1024,1024]{1,0:T(8,128)(2,1)S(1)}, bf16[1024,256]{1,0:T(8,128)(2,1)S(1)}, bf16[1024,1024]{1,0:T(8,128)(2,1)S(1)}, bf16[1024,1024]{1,0:T(8,128)(2,1)S(1)}) custom-call(s32[4]{0:T(128)S(1)} %pad_add_fusion.1.pos, bf16[1024,128]{1,0:T(8,128)(2,1)S(1)} %copy-done.7, ...), custom_call_target="tpu_custom_call" | custom-call | flops 6442450944 | bytes 20971520 | tf_op jit(solution)/shard_map/mlp/pallas_call | solution.py:296
  123.0 3.7 %outer_grads.1 = (bf16[4,16,16,640]{3,2,1,0:T(8,128)(2,1)S(1)}, bf16[4,16,16,640]{3,2,1,0:T(8,128)(2,1)S(1)}) custom-call(s32[4]{0:T(128)S(1)} %pad_add_fusion.1.pos, bf16[1024,1024]{1,0:T(8,128)(2,1)S(1)} %get-tuple-element.130.act1, bf16[1024,1024]{1,0:T(8,128)(2,1)S(1)} %get-tuple-element.131.act2, bf16[1024,256]{1,0:T(8,128)(2,1)S(1)} %get-tuple-element.132.gl, ...), custom_call_target="tpu_custom_call" | custom-call | flops 2684354560 | bytes 8388608 | tf_op jit(solution)/shard_map/outer_grads/pallas_call | solution.py:337
  126.8 1.9 %first_grads_2.1 = (bf16[1,16,16,1024]{3,2,1,0:T(8,128)(2,1)S(1)}, bf16[1,16,16,1024]{3,2,1,0:T(8,128)(2,1)S(1)}) custom-call(s32[4]{0:T(128)S(1)} %pad_add_fusion.1.pos, bf16[1024,128]{1,0:T(8,128)(2,1)S(1)} %collective-permute-done.3.refs_6_.refs_0_, bf16[1056,128]{1,0:T(8,128)(2,1)S(1)} %collective-permute-done.7.lab2.refs_7_.refs_1_, ...), custom_call_target="tpu_custom_call" | custom-call | flops 1073741824 | bytes 6291456 | tf_op jit(solution)/shard_map/first_grads_2/pallas_call | solution.py:367
  128.7 3.0 %first_grads_13.1 = (bf16[2,16,16,1024]{3,2,1,0:T(8,128)(2,1)S(1)}, bf16[2,16,16,1024]{3,2,1,0:T(8,128)(2,1)S(1)}) custom-call(s32[4]{0:T(128)S(1)} %pad_add_fusion.1.pos, bf16[1024,128]{1,0:T(8,128)(2,1)S(1)} %collective-permute-done.1.refs_9_.refs_0_, bf16[1056,128]{1,0:T(8,128)(2,1)S(1)} %collective-permute-done.5.lab3.refs_10_.refs_1_, ...), custom_call_target="tpu_custom_call" | custom-call | flops 2147483648 | bytes 6291456 | tf_op jit(solution)/shard_map/first_grads_13/pallas_call | solution.py:367
  132.3 2.9 %collective-permute-done.16.got = bf16[1,16,16,1024]{3,2,1,0:T(8,128)(2,1)S(1)} collective-permute-done((bf16[1,16,16,1024]{3,2,1,0:T(8,128)(2,1)S(1)}, bf16[1,16,16,1024]{3,2,1,0:T(8,128)(2,1)S(1)}, u32[]{:S(2)}, u32[]{:S(2)}) %collective-permute-start.16) | collective-permute-done | bytes 524320 | tf_op jit(solution)/shard_map/ppermute | solution.py:455
  135.4 3.2 %collective-permute-start.24 = (bf16[8,16,640]{2,1,0:T(8,128)(2,1)S(1)}, bf16[8,16,640]{2,1,0:T(8,128)(2,1)S(1)}, u32[]{:S(2)}, u32[]{:S(2)}) collective-permute-start(bf16[8,16,640]{2,1,0:T(8,128)(2,1)S(1)} %get-tuple-element.154), channel_id=1, source_target_pairs={{0,96},{32,0},{64,32},{96,64},{1,97},{33,1},{65,33},{97,65},{2,98}... | collective-permute-start | bytes 491528 | tf_op jit(solution)/shard_map/ppermute | solution.py:455
  143.3 3.2 %collective-permute-start.26 = (bf16[16,16,640]{2,1,0:T(8,128)(2,1)S(1)}, bf16[16,16,640]{2,1,0:T(8,128)(2,1)S(1)}, u32[]{:S(2)}, u32[]{:S(2)}) collective-permute-start(bf16[16,16,640]{2,1,0:T(8,128)(2,1)S(1)} %get-tuple-element.156), channel_id=1, source_target_pairs={{0,96},{32,0},{64,32},{96,64},{1,97},{33,1},{65,33},{97,65},{2,98}... | collective-permute-start | bytes 983048 | tf_op jit(solution)/shard_map/ppermute | solution.py:455
  154.6 4.8 %all-to-all-start.4 = ((bf16[16,16,640]{2,1,0:T(8,128)(2,1)}), bf16[16,16,640]{2,1,0:T(8,128)(2,1)S(1)}, u32[]{:S(2)}, u32[]{:S(2)}) async-start(bf16[16,16,640]{2,1,0:T(8,128)(2,1)} %own_middle.1), calls=%async_computation.4 | async-start | bytes 655360 | tf_op jit(solution)/shard_map/all_to_all | solution.py:459
  159.4 8.9 %collective-permute-done.21.r1 = bf16[16,16,1024]{2,1,0:T(8,128)(2,1)S(1)} collective-permute-done((bf16[16,16,1024]{2,1,0:T(8,128)(2,1)}, bf16[16,16,1024]{2,1,0:T(8,128)(2,1)S(1)}, u32[]{:S(2)}, u32[]{:S(2)}) %collective-permute-start.21) | collective-permute-done | bytes 524320 | tf_op jit(solution)/shard_map/ppermute | solution.py:455
  169.2 14.1 %all_to_all.25.part_f = bf16[16,16,1024]{2,1,0:T(8,128)(2,1)S(1)} all-to-all(bf16[16,16,1024]{2,1,0:T(8,128)(2,1)S(1)} %own_first.1), channel_id=1, replica_groups=mesh['y'=4,'x'=4,'core'=2,'rep'=4] {'y','x'}, dimensions={0} | all-to-all | bytes 1048576 | tf_op jit(solution)/shard_map/all_to_all | solution.py:459
  (90 shorter events, 31.0 us)
Async XLA Ops:
  5.2 19.4 %all-to-all-start = ((bf16[16,144,128]{2,1,0:T(8,128)(2,1)}), bf16[16,144,128]{2,1,0:T(8,128)(2,1)S(1)}, u32[]{:S(2)}, u32[]{:S(2)}) async-start(bf16[16,144,128]{2,1,0:T(8,128)(2,1)} %get-tuple-element.81), calls=%async_computation | async-start | bytes 1179648 | tf_op jit(solution)/shard_map/all_to_all | solution.py:459
  12.3 10.1 %collective-permute-start = (bf16[1024,128]{1,0:T(8,128)(2,1)S(1)}, bf16[1024,128]{1,0:T(8,128)(2,1)S(1)}, u32[]{:S(2)}, u32[]{:S(2)}) collective-permute-start(bf16[1024,128]{1,0:T(8,128)(2,1)S(1)} %get-tuple-element.82), channel_id=1, source_target_pairs={{0,1},{1,2},{2,3},{3,0},{4,5},{5,6},{6,7},{7,4},{8,9},{9,10},{10,1... | collective-permute-start | bytes 786440 | tf_op jit(solution)/shard_map/ppermute | solution.py:455
  14.3 8.1 %collective-permute-start.1 = (bf16[1024,128]{1,0:T(8,128)(2,1)S(1)}, bf16[1024,128]{1,0:T(8,128)(2,1)S(1)}, u32[]{:S(2)}, u32[]{:S(2)}) collective-permute-start(bf16[1024,128]{1,0:T(8,128)(2,1)S(1)} %get-tuple-element.83), channel_id=1, source_target_pairs={{0,3},{1,0},{2,1},{3,2},{4,7},{5,4},{6,5},{7,6},{8,11},{9,8},{10,9... | collective-permute-start | bytes 786440 | tf_op jit(solution)/shard_map/ppermute | solution.py:455
  24.6 4.7 %collective-permute-start.2 = (bf16[16,144,128]{2,1,0:T(8,128)(2,1)S(1)}, bf16[16,144,128]{2,1,0:T(8,128)(2,1)S(1)}, u32[]{:S(2)}, u32[]{:S(2)}) collective-permute-start(bf16[16,144,128]{2,1,0:T(8,128)(2,1)S(1)} %all-to-all-done.near), channel_id=1, source_target_pairs={{0,4},{4,0},{1,5},{5,1},{2,6},{6,2},{3,7},{7,3},{8,12},{12,8},{9,1... | collective-permute-start | bytes 1769480 | tf_op jit(solution)/shard_map/ppermute | solution.py:455
  24.6 13.6 %collective-permute-start.3 = (bf16[1024,128]{1,0:T(8,128)(2,1)S(1)}, bf16[1024,128]{1,0:T(8,128)(2,1)S(1)}, u32[]{:S(2)}, u32[]{:S(2)}) collective-permute-start(bf16[1024,128]{1,0:T(8,128)(2,1)S(1)} %get-tuple-element.91), channel_id=1, source_target_pairs={{0,2},{1,3},{2,0},{3,1},{4,6},{5,7},{6,4},{7,5},{8,10},{9,11},{10,... | collective-permute-start | bytes 786440 | tf_op jit(solution)/shard_map/ppermute | solution.py:455
  38.2 15.8 %all-to-all-start.1 = ((bf16[16,128,128]{2,1,0:T(8,128)(2,1)}), bf16[16,128,128]{2,1,0:T(8,128)(2,1)S(1)}, u32[]{:S(2)}, u32[]{:S(2)}) async-start(bf16[16,128,128]{2,1,0:T(8,128)(2,1)} %get-tuple-element.94), calls=%async_computation.1 | async-start | bytes 1048576 | tf_op jit(solution)/shard_map/all_to_all | solution.py:459
  42.1 30.8 %copy-start.5 = (bf16[1056,128]{1,0:T(8,128)(2,1)S(1)}, bf16[1056,128]{1,0:T(8,128)(2,1)}, u32[]{:S(2)}) copy-start(bf16[1056,128]{1,0:T(8,128)(2,1)} %get-tuple-element.92.lab0.refs_1_) | copy-start | bytes 811012
  42.1 9.8 %collective-permute-start.4 = (bf16[1056,128]{1,0:T(8,128)(2,1)}, bf16[1056,128]{1,0:T(8,128)(2,1)S(1)}, u32[]{:S(2)}, u32[]{:S(2)}) collective-permute-start(bf16[1056,128]{1,0:T(8,128)(2,1)} %get-tuple-element.95), channel_id=1, source_target_pairs={{0,1},{1,2},{2,3},{3,0},{4,5},{5,6},{6,7},{7,4},{8,9},{9,10},{10,1... | collective-permute-start | bytes 811016 | tf_op jit(solution)/shard_map/ppermute | solution.py:455
  43.2 8.8 %collective-permute-start.5 = (bf16[1056,128]{1,0:T(8,128)(2,1)}, bf16[1056,128]{1,0:T(8,128)(2,1)S(1)}, u32[]{:S(2)}, u32[]{:S(2)}) collective-permute-start(bf16[1056,128]{1,0:T(8,128)(2,1)} %get-tuple-element.96), channel_id=1, source_target_pairs={{0,3},{1,0},{2,1},{3,2},{4,7},{5,4},{6,5},{7,6},{8,11},{9,8},{10,9... | collective-permute-start | bytes 811016 | tf_op jit(solution)/shard_map/ppermute | solution.py:455
  54.0 1.9 %collective-permute-start.6 = (bf16[16,128,128]{2,1,0:T(8,128)(2,1)S(1)}, bf16[16,128,128]{2,1,0:T(8,128)(2,1)S(1)}, u32[]{:S(2)}, u32[]{:S(2)}) collective-permute-start(bf16[16,128,128]{2,1,0:T(8,128)(2,1)S(1)} %all-to-all-done.1.near), channel_id=1, source_target_pairs={{0,4},{4,0},{1,5},{5,1},{2,6},{6,2},{3,7},{7,3},{8,12},{12,8},{9,1... | collective-permute-start | bytes 1572872 | tf_op jit(solution)/shard_map/ppermute | solution.py:455
  54.0 10.6 %collective-permute-start.7 = (bf16[1056,128]{1,0:T(8,128)(2,1)}, bf16[1056,128]{1,0:T(8,128)(2,1)S(1)}, u32[]{:S(2)}, u32[]{:S(2)}) collective-permute-start(bf16[1056,128]{1,0:T(8,128)(2,1)} %get-tuple-element.104), channel_id=1, source_target_pairs={{0,2},{1,3},{2,0},{3,1},{4,6},{5,7},{6,4},{7,5},{8,10},{9,11},{10,... | collective-permute-start | bytes 811016 | tf_op jit(solution)/shard_map/ppermute | solution.py:455
  64.6 16.9 %all-to-all-start.2 = ((bf16[16,128,128]{2,1,0:T(8,128)(2,1)}), bf16[16,128,128]{2,1,0:T(8,128)(2,1)}, u32[]{:S(2)}, u32[]{:S(2)}) async-start(bf16[16,128,128]{2,1,0:T(8,128)(2,1)} %get-tuple-element.107), calls=%async_computation.2 | async-start | bytes 1048576 | tf_op jit(solution)/shard_map/all_to_all | solution.py:459
  69.6 9.6 %collective-permute-start.8 = (bf16[1024,128]{1,0:T(8,128)(2,1)}, bf16[1024,128]{1,0:T(8,128)(2,1)S(1)}, u32[]{:S(2)}, u32[]{:S(2)}) collective-permute-start(bf16[1024,128]{1,0:T(8,128)(2,1)} %get-tuple-element.108), channel_id=1, source_target_pairs={{0,1},{1,2},{2,3},{3,0},{4,5},{5,6},{6,7},{7,4},{8,9},{9,10},{10,1... | collective-permute-start | bytes 786440 | tf_op jit(solution)/shard_map/ppermute | solution.py:455
  71.6 8.0 %collective-permute-start.9 = (bf16[1024,128]{1,0:T(8,128)(2,1)}, bf16[1024,128]{1,0:T(8,128)(2,1)S(1)}, u32[]{:S(2)}, u32[]{:S(2)}) collective-permute-start(bf16[1024,128]{1,0:T(8,128)(2,1)} %get-tuple-element.109), channel_id=1, source_target_pairs={{0,3},{1,0},{2,1},{3,2},{4,7},{5,4},{6,5},{7,6},{8,11},{9,8},{10,9... | collective-permute-start | bytes 786440 | tf_op jit(solution)/shard_map/ppermute | solution.py:455
  81.5 3.0 %collective-permute-start.10 = (bf16[16,128,128]{2,1,0:T(8,128)(2,1)}, bf16[16,128,128]{2,1,0:T(8,128)(2,1)}, u32[]{:S(2)}, u32[]{:S(2)}) collective-permute-start(bf16[16,128,128]{2,1,0:T(8,128)(2,1)} %all-to-all-done.2.near), channel_id=1, source_target_pairs={{0,4},{4,0},{1,5},{5,1},{2,6},{6,2},{3,7},{7,3},{8,12},{12,8},{9,1... | collective-permute-start | bytes 1572872 | tf_op jit(solution)/shard_map/ppermute | solution.py:455
  81.5 10.8 %collective-permute-start.11 = (bf16[1024,128]{1,0:T(8,128)(2,1)}, bf16[1024,128]{1,0:T(8,128)(2,1)S(1)}, u32[]{:S(2)}, u32[]{:S(2)}) collective-permute-start(bf16[1024,128]{1,0:T(8,128)(2,1)} %get-tuple-element.118), channel_id=1, source_target_pairs={{0,2},{1,3},{2,0},{3,1},{4,6},{5,7},{6,4},{7,5},{8,10},{9,11},{10,... | collective-permute-start | bytes 786440 | tf_op jit(solution)/shard_map/ppermute | solution.py:455
  92.3 10.6 %collective-permute-start.12 = (bf16[1024,128]{1,0:T(8,128)(2,1)}, bf16[1024,128]{1,0:T(8,128)(2,1)S(1)}, u32[]{:S(2)}, u32[]{:S(2)}) collective-permute-start(bf16[1024,128]{1,0:T(8,128)(2,1)} %get-tuple-element.120), channel_id=1, source_target_pairs={{0,1},{1,2},{2,3},{3,0},{4,5},{5,6},{6,7},{7,4},{8,9},{9,10},{10,1... | collective-permute-start | bytes 786440 | tf_op jit(solution)/shard_map/ppermute | solution.py:455
  94.4 14.6 %collective-permute-start.13 = (bf16[1024,128]{1,0:T(8,128)(2,1)}, bf16[1024,128]{1,0:T(8,128)(2,1)S(1)}, u32[]{:S(2)}, u32[]{:S(2)}) collective-permute-start(bf16[1024,128]{1,0:T(8,128)(2,1)} %get-tuple-element.121), channel_id=1, source_target_pairs={{0,2},{1,3},{2,0},{3,1},{4,6},{5,7},{6,4},{7,5},{8,10},{9,11},{10,... | collective-permute-start | bytes 786440 | tf_op jit(solution)/shard_map/ppermute | solution.py:455
  96.7 12.2 %collective-permute-start.14 = (bf16[1024,128]{1,0:T(8,128)(2,1)}, bf16[1024,128]{1,0:T(8,128)(2,1)S(1)}, u32[]{:S(2)}, u32[]{:S(2)}) collective-permute-start(bf16[1024,128]{1,0:T(8,128)(2,1)} %get-tuple-element.122), channel_id=1, source_target_pairs={{0,3},{1,0},{2,1},{3,2},{4,7},{5,4},{6,5},{7,6},{8,11},{9,8},{10,9... | collective-permute-start | bytes 786440 | tf_op jit(solution)/shard_map/ppermute | solution.py:455
  126.7 8.5 %collective-permute-start.15 = (bf16[4,16,16,640]{3,2,1,0:T(8,128)(2,1)S(1)}, bf16[4,16,16,640]{3,2,1,0:T(8,128)(2,1)S(1)}, u32[]{:S(2)}, u32[]{:S(2)}) collective-permute-start(bf16[4,16,16,640]{3,2,1,0:T(8,128)(2,1)S(1)} %get-tuple-element.134), channel_id=1, source_target_pairs={{0,4},{4,0},{1,5},{5,1},{2,6},{6,2},{3,7},{7,3},{8,12},{12,8},{9,1... | collective-permute-start | bytes 3932168 | tf_op jit(solution)/shard_map/ppermute | solution.py:455
  131.6 16.8 %collective-permute-start.18 = (bf16[2,16,16,1024]{3,2,1,0:T(8,128)(2,1)S(1)}, bf16[2,16,16,1024]{3,2,1,0:T(8,128)(2,1)S(1)}, u32[]{:S(2)}, u32[]{:S(2)}) collective-permute-start(bf16[2,16,16,1024]{3,2,1,0:T(8,128)(2,1)S(1)} %get-tuple-element.144), channel_id=1, source_target_pairs={{0,4},{4,0},{1,5},{5,1},{2,6},{6,2},{3,7},{7,3},{8,12},{12,8},{9,1... | collective-permute-start | bytes 3145736 | tf_op jit(solution)/shard_map/ppermute | solution.py:455
  132.2 3.0 %collective-permute-start.16 = (bf16[1,16,16,1024]{3,2,1,0:T(8,128)(2,1)S(1)}, bf16[1,16,16,1024]{3,2,1,0:T(8,128)(2,1)S(1)}, u32[]{:S(2)}, u32[]{:S(2)}) collective-permute-start(bf16[1,16,16,1024]{3,2,1,0:T(8,128)(2,1)S(1)} %get-tuple-element.136), channel_id=1, source_target_pairs={{0,4},{4,0},{1,5},{5,1},{2,6},{6,2},{3,7},{7,3},{8,12},{12,8},{9,1... | collective-permute-start | bytes 1572872 | tf_op jit(solution)/shard_map/ppermute | solution.py:455
  135.3 7.8 %collective-permute-start.23 = (bf16[8,16,640]{2,1,0:T(8,128)(2,1)S(1)}, bf16[8,16,640]{2,1,0:T(8,128)(2,1)S(1)}, u32[]{:S(2)}, u32[]{:S(2)}) collective-permute-start(bf16[8,16,640]{2,1,0:T(8,128)(2,1)S(1)} %get-tuple-element.153), channel_id=1, source_target_pairs={{0,32},{32,64},{64,96},{96,0},{1,33},{33,65},{65,97},{97,1},{2,34}... | collective-permute-start | bytes 491528 | tf_op jit(solution)/shard_map/ppermute | solution.py:455
  135.4 7.7 %collective-permute-start.24 = (bf16[8,16,640]{2,1,0:T(8,128)(2,1)S(1)}, bf16[8,16,640]{2,1,0:T(8,128)(2,1)S(1)}, u32[]{:S(2)}, u32[]{:S(2)}) collective-permute-start(bf16[8,16,640]{2,1,0:T(8,128)(2,1)S(1)} %get-tuple-element.154), channel_id=1, source_target_pairs={{0,96},{32,0},{64,32},{96,64},{1,97},{33,1},{65,33},{97,65},{2,98}... | collective-permute-start | bytes 491528 | tf_op jit(solution)/shard_map/ppermute | solution.py:455
  138.7 9.8 %collective-permute-start.19 = (bf16[8,16,1024]{2,1,0:T(8,128)(2,1)S(1)}, bf16[8,16,1024]{2,1,0:T(8,128)(2,1)S(1)}, u32[]{:S(2)}, u32[]{:S(2)}) collective-permute-start(bf16[8,16,1024]{2,1,0:T(8,128)(2,1)S(1)} %get-tuple-element.147), channel_id=1, source_target_pairs={{0,1},{1,2},{2,3},{3,0},{4,5},{5,6},{6,7},{7,4},{8,9},{9,10},{10,1... | collective-permute-start | bytes 786440 | tf_op jit(solution)/shard_map/ppermute | solution.py:455
  140.2 8.3 %collective-permute-start.20 = (bf16[8,16,1024]{2,1,0:T(8,128)(2,1)S(1)}, bf16[8,16,1024]{2,1,0:T(8,128)(2,1)S(1)}, u32[]{:S(2)}, u32[]{:S(2)}) collective-permute-start(bf16[8,16,1024]{2,1,0:T(8,128)(2,1)S(1)} %get-tuple-element.148), channel_id=1, source_target_pairs={{0,3},{1,0},{2,1},{3,2},{4,7},{5,4},{6,5},{7,6},{8,11},{9,8},{10,9... | collective-permute-start | bytes 786440 | tf_op jit(solution)/shard_map/ppermute | solution.py:455
  143.3 10.5 %collective-permute-start.25 = (bf16[16,16,640]{2,1,0:T(8,128)(2,1)S(1)}, bf16[16,16,640]{2,1,0:T(8,128)(2,1)S(1)}, u32[]{:S(2)}, u32[]{:S(2)}) collective-permute-start(bf16[16,16,640]{2,1,0:T(8,128)(2,1)S(1)} %get-tuple-element.155), channel_id=1, source_target_pairs={{0,32},{32,64},{64,96},{96,0},{1,33},{33,65},{65,97},{97,1},{2,34}... | collective-permute-start | bytes 983048 | tf_op jit(solution)/shard_map/ppermute | solution.py:455
  143.3 10.4 %collective-permute-start.26 = (bf16[16,16,640]{2,1,0:T(8,128)(2,1)S(1)}, bf16[16,16,640]{2,1,0:T(8,128)(2,1)S(1)}, u32[]{:S(2)}, u32[]{:S(2)}) collective-permute-start(bf16[16,16,640]{2,1,0:T(8,128)(2,1)S(1)} %get-tuple-element.156), channel_id=1, source_target_pairs={{0,96},{32,0},{64,32},{96,64},{1,97},{33,1},{65,33},{97,65},{2,98}... | collective-permute-start | bytes 983048 | tf_op jit(solution)/shard_map/ppermute | solution.py:455
  148.4 11.0 %collective-permute-start.17 = (bf16[1,16,16,1024]{3,2,1,0:T(8,128)(2,1)S(1)}, bf16[1,16,16,1024]{3,2,1,0:T(8,128)(2,1)S(1)}, u32[]{:S(2)}, u32[]{:S(2)}) collective-permute-start(bf16[1,16,16,1024]{3,2,1,0:T(8,128)(2,1)S(1)} %get-tuple-element.142), channel_id=1, source_target_pairs={{0,4},{4,0},{1,5},{5,1},{2,6},{6,2},{3,7},{7,3},{8,12},{12,8},{9,1... | collective-permute-start | bytes 1572872 | tf_op jit(solution)/shard_map/ppermute | solution.py:455
  149.6 18.8 %collective-permute-start.21 = (bf16[16,16,1024]{2,1,0:T(8,128)(2,1)}, bf16[16,16,1024]{2,1,0:T(8,128)(2,1)S(1)}, u32[]{:S(2)}, u32[]{:S(2)}) collective-permute-start(bf16[16,16,1024]{2,1,0:T(8,128)(2,1)} %get-tuple-element.149), channel_id=1, source_target_pairs={{0,1},{1,2},{2,3},{3,0},{4,5},{5,6},{6,7},{7,4},{8,9},{9,10},{10,1... | collective-permute-start | bytes 1572872 | tf_op jit(solution)/shard_map/ppermute | solution.py:455
  151.0 17.4 %collective-permute-start.22 = (bf16[16,16,1024]{2,1,0:T(8,128)(2,1)S(1)}, bf16[16,16,1024]{2,1,0:T(8,128)(2,1)S(1)}, u32[]{:S(2)}, u32[]{:S(2)}) collective-permute-start(bf16[16,16,1024]{2,1,0:T(8,128)(2,1)S(1)} %get-tuple-element.150), channel_id=1, source_target_pairs={{0,3},{1,0},{2,1},{3,2},{4,7},{5,4},{6,5},{7,6},{8,11},{9,8},{10,9... | collective-permute-start | bytes 1572872 | tf_op jit(solution)/shard_map/ppermute | solution.py:455
  154.6 14.5 %all-to-all-start.4 = ((bf16[16,16,640]{2,1,0:T(8,128)(2,1)}), bf16[16,16,640]{2,1,0:T(8,128)(2,1)S(1)}, u32[]{:S(2)}, u32[]{:S(2)}) async-start(bf16[16,16,640]{2,1,0:T(8,128)(2,1)} %own_middle.1), calls=%async_computation.4 | async-start | bytes 655360 | tf_op jit(solution)/shard_map/all_to_all | solution.py:459
  (16 other events, 161.8 us)

commit v2 on v1

--- a/solution.py
+++ b/solution.py
@@ -321,16 +321,19 @@
 def outer_kernel(pos, act1, act2, gl, gm, keep, send):
     own = pos[1] == 0
     width = HID // Y
-    for k in range(Y):
-        at = pl.multiple_of(lax.rem(pos[3] + k, Y) * width, width)
-        mid = dot(act1[:, pl.ds(at, width)], gm[...], 0, 0)
-        out = dot(act2[:, pl.ds(at, width)], gl[...], 0, 0)
+    for y in range(Y):
+        cut = slice(y * width, (y + 1) * width)
+        mid = dot(act1[:, cut], gm[...], 0, 0)
+        out = dot(act2[:, cut], gl[...], 0, 0)
         both = jnp.concatenate([mid, out], axis=1).reshape(X, CORE, REP, 8, HID + CP)
         both = jnp.concatenate([both[..., :WIDE], both[..., WIDE:]], axis=3)
         zero, one = both[:, 0], both[:, 1]
-        shape = (SIDE, 16, WIDE)
-        keep[k] = jnp.where(own, zero, one).astype(BF).reshape(shape)
-        send[k] = jnp.where(own, one, zero).astype(BF).reshape(shape)
+        kept = jnp.where(own, zero, one).astype(BF)
+        sent = jnp.where(own, one, zero).astype(BF)
+        for z in range(REP):
+            k = lax.rem(z + REP - pos[0], REP)
+            keep[k, y * X : (y + 1) * X] = kept[:, z]
+            send[k, y * X : (y + 1) * X] = sent[:, z]
 
 
 def outer_grads(pos, act1, act2, gl, gm):
@@ -338,7 +341,7 @@
         outer_kernel,
         in_specs=[whole(pltpu.SMEM)] + [whole()] * 4,
         out_specs=[whole()] * 2,
-        out_shape=[struct((Y, SIDE, 16, WIDE))] * 2,
+        out_shape=[struct((REP, SIDE, 16, WIDE))] * 2,
         compiler_params=params(30),
         name="outer_grads",
         cost_estimate=pl.CostEstimate(
@@ -395,8 +398,9 @@
     q3[half:] = plus(keep[three, half:], got[three, half:], behind[...]).astype(BF)
 
 
-def own_kernel(keep, got, r1, r3, out):
-    out[...] = plus(keep[0], got[0], r1[...], r3[...]).astype(BF)
+def own_kernel(kf, gf, rf1, rf3, km, gm, rm1, rm3, out):
+    out[:, :, :HID] = plus(kf[0], gf[0], rf1[...], rf3[...]).astype(BF)
+    out[:, :, HID:] = plus(km[0], gm[0], rm1[...], rm3[...]).astype(BF)
 
 
 def small(kernel, outs, name, *args):
@@ -414,11 +418,14 @@
     )(*args)
 
 
-def send_far(at, keep, got, axis, tag):
+def far_parts(at, keep, got, tag):
     half = (SIDE // 2,) + keep.shape[2:]
     kernel = functools.partial(far_kernel, at)
-    ahead, behind = small(kernel, [half, half], "far_" + tag, keep, got)
-    return shift(ahead, axis, 1), shift(behind, axis, 3)
+    return small(kernel, [half, half], "far_" + tag, keep, got)
+
+
+def send_far(parts, axis):
+    return shift(parts[0], axis, 1), shift(parts[1], axis, 3)
 
 
 def send_near(one, three, keep, got, far, axis, tag):
@@ -427,27 +434,23 @@
     return shift(q1, axis, 1), shift(q3, axis, 3)
 
 
-def own_share(keep, got, near, tag):
-    return small(own_kernel, [keep.shape[1:]], "own_" + tag, keep, got, *near)[0]
-
-
-def total_kernel(part_f, part_m, first, mid, out):
-    first[0] = jnp.sum(part_f[...].astype(F32), axis=0)
-    total = jnp.sum(part_m[...].astype(F32), axis=0)
-    rest = jnp.concatenate([total[:8], total[8:]], axis=1)
+def total_kernel(parts, first, mid, out):
+    total = jnp.sum(parts[...].astype(F32), axis=0)
+    first[0] = total[:, :HID]
+    rest = jnp.concatenate([total[:8, HID:], total[8:, HID:]], axis=1)
     mid[...] = rest[:, :HID]
     out[...] = rest[:, HID : HID + C]
 
 
-def total_grads(part_f, part_m):
+def total_grads(parts):
     return pl.pallas_call(
         total_kernel,
-        in_specs=[whole()] * 2,
+        in_specs=[whole()],
         out_specs=[whole()] * 3,
         out_shape=[struct((1, 16, HID), F32), struct((8, HID), F32), struct((8, C), F32)],
         compiler_params=params(12),
         name="total_grads",
-    )(part_f, part_m)
+    )(parts)
 
 
 def shift(value, axis, by):
@@ -510,23 +513,29 @@
     act1, act2, gl, gm, gf = mlp(
         pos, pieces[3], early, counts, first_weight, mid_weight, w3
     )
-    keep_m, send_m = outer_grads(pos, act1, act2, gl, gm)
-    got_m = shift(send_m, "core", 1)
     keep2, send2 = first_grads(pos, pieces, gf, (2,))
     got2 = shift(send2, "core", 1)
-    keep2, gf = lax.optimization_barrier((keep2, gf))
+    keep2, gm = lax.optimization_barrier((keep2, gm))
+    keep_m, send_m = outer_grads(pos, act1, act2, gl, gm)
+    got2, keep_m, send_m, gf = lax.optimization_barrier((got2, keep_m, send_m, gf))
+    got_m = shift(send_m, "core", 1)
+    parts_f = far_parts(0, keep2, got2, "first")
+    parts_f, gf = lax.optimization_barrier((parts_f, gf))
+    far_f = send_far(parts_f, "rep")
     keep13, send13 = first_grads(pos, pieces, gf, (1, 3))
+    got_m, far_f, keep13, send13, gf = lax.optimization_barrier(
+        (got_m, far_f, keep13, send13, gf)
+    )
     got13 = shift(send13, "core", 1)
-    got_m, got2, keep13, gf = lax.optimization_barrier((got_m, got2, keep13, gf))
-    far_m = send_far(2, keep_m, got_m, "y", "middle")
-    far_f = send_far(0, keep2, got2, "rep", "first")
+    far_m = send_far(far_parts(2, keep_m, got_m, "middle"), "rep")
     keep0, send0 = first_grads(pos, pieces, gf, (0,))
     got0 = shift(send0, "core", 1)
-    near_m = send_near(1, 3, keep_m, got_m, far_m, "y", "middle")
-    part_m = swap(own_share(keep_m, got_m, near_m, "middle"), ("x", "rep"))
+    got13, far_m = lax.optimization_barrier((got13, far_m))
     near_f = send_near(0, 1, keep13, got13, far_f, "rep", "first")
-    part_f = swap(own_share(keep0, got0, near_f, "first"), ("y", "x"))
-    first, mid, out = total_grads(part_f, part_m)
+    near_m = send_near(1, 3, keep_m, got_m, far_m, "rep", "middle")
+    args = (keep0, got0, *near_f, keep_m, got_m, *near_m)
+    parts = small(own_kernel, [(SIDE, 16, HID + WIDE)], "own_share", *args)[0]
+    first, mid, out = total_grads(swap(parts, ("y", "x")))
     return first, mid, out
 
 

time: 185 us -> 191 us (1.032)
  waiting for transfers between devices: 41.5 us -> 47.8 us
  blocking collectives: 14.1 us -> 19.6 us
  starting transfers between devices: 57.3 us -> 52.6 us
    ppermute x27, waiting for transfers between devices: 35 us -> 41.7 us  [shift(): lax.ppermute(value, axis, [(i, (i + by) % size) for i in range(size)])]
    all_to_all x1, blocking collectives: 14.1 us -> 19.6 us  [swap(): return lax.all_to_all(value, axes, split_axis=0, concat_axis=0, tiled=True)]
    all_to_all x4 -> x3, starting transfers between devices: 20.8 us -> 16 us  [swap(): return lax.all_to_all(value, axes, split_axis=0, concat_axis=0, tiled=True)]
    all_to_all x4 -> x3, waiting for transfers between devices: 6.54 us -> 6.04 us  [swap(): return lax.all_to_all(value, axes, split_axis=0, concat_axis=0, tiled=True)]
    unnamed x35 -> x37, local copies, waits for them, and re-layouts: 6.38 us -> 6.2 us
  transfers between devices with their start and end apart: 31 -> 30, of which waited for: 14 -> 15; matrix products, arithmetic and copies ran while one was open for 1% -> 2% of each run, Pallas kernels for 23% -> 22%
where the time goes in v2:
time: 191 us; the launch traced here: 190 us
  Pallas kernels  61.2 us (32%)
  starting transfers between devices  52.6 us (28%)
  waiting for transfers between devices  47.8 us (25%)
  blocking collectives  19.6 us (10%)
  local copies, waits for them, and re-layouts  7.49 us (4%)
    ppermute x27, waiting for transfers between devices, shift(): lax.ppermute(value, axis, [(i, (i + by) % size) for i in range(size)])  41.7 us
    ppermute x27, starting transfers between devices, shift(): lax.ppermute(value, axis, [(i, (i + by) % size) for i in range(size)])  36.5 us
    pallas_call x3, Pallas kernels, propagate(): pl.pallas_call(functools.partial(prop_kernel, h), in_specs=[whole(pltpu.S...  23.7 us
    all_to_all x1, blocking collectives, swap(): return lax.all_to_all(value, axes, split_axis=0, concat_axis=0, tiled=True)  19.6 us
    all_to_all x3, starting transfers between devices, swap(): return lax.all_to_all(value, axes, split_axis=0, concat_axis=0, tiled=True)  16 us
    pallas_call x1, Pallas kernels, mlp(): pl.pallas_call(mlp_kernel, grid_spec=pltpu.PrefetchScalarGridSpec(num_sca...  14 us
    pallas_call x3, Pallas kernels, first_grads(): pl.pallas_call(functools.partial(first_kernel, steps), in_specs=[whole(pl...  6.61 us
    unnamed x37, local copies, waits for them, and re-layouts  6.2 us
  transfers between devices with their start and end apart: 30, of which 15 were waited for; matrix products, arithmetic and copies ran while one was open for 2% of the time, Pallas kernels for 22%

profile of v2, /device:TPU:0, one launch (start us, length us, event | category | flops | bytes accessed | tf_op | source)
XLA Modules:
  0.0 190.4 jit_solution(5302199773918318660)
XLA Ops:
  3.3 1.9 export_first.1
  5.2 7.1 %all-to-all-start = ((bf16[16,144,128]{2,1,0:T(8,128)(2,1)}), bf16[16,144,128]{2,1,0:T(8,128)(2,1)S(1)}, u32[]{:S(2)}, u32[]{:S(2)}) async-start(bf16[16,144,128]{2,1,0:T(8,128)(2,1)} %get-tuple-element.93), calls=%async_computation | async-start | bytes 1179648 | tf_op jit(solution)/shard_map/all_to_all | solution.py:462
  12.3 2.0 %collective-permute-start = (bf16[1024,128]{1,0:T(8,128)(2,1)S(1)}, bf16[1024,128]{1,0:T(8,128)(2,1)S(1)}, u32[]{:S(2)}, u32[]{:S(2)}) collective-permute-start(bf16[1024,128]{1,0:T(8,128)(2,1)S(1)} %get-tuple-element.94), channel_id=1, source_target_pairs={{0,1},{1,2},{2,3},{3,0},{4,5},{5,6},{6,7},{7,4},{8,9},{9,10},{10,1... | collective-permute-start | bytes 786440 | tf_op jit(solution)/shard_map/ppermute | solution.py:458
  14.3 2.2 %collective-permute-start.1 = (bf16[1024,128]{1,0:T(8,128)(2,1)S(1)}, bf16[1024,128]{1,0:T(8,128)(2,1)S(1)}, u32[]{:S(2)}, u32[]{:S(2)}) collective-permute-start(bf16[1024,128]{1,0:T(8,128)(2,1)S(1)} %get-tuple-element.95), channel_id=1, source_target_pairs={{0,3},{1,0},{2,1},{3,2},{4,7},{5,4},{6,5},{7,6},{8,11},{9,8},{10,9... | collective-permute-start | bytes 786440 | tf_op jit(solution)/shard_map/ppermute | solution.py:458
  16.5 5.9 %collective-permute-done.refs_3_.refs_4_ = bf16[1024,128]{1,0:T(8,128)(2,1)S(1)} collective-permute-done((bf16[1024,128]{1,0:T(8,128)(2,1)S(1)}, bf16[1024,128]{1,0:T(8,128)(2,1)S(1)}, u32[]{:S(2)}, u32[]{:S(2)}) %collective-permute-start) | collective-permute-done | bytes 262176 | tf_op jit(solution)/shard_map/ppermute | solution.py:458
  22.5 2.1 %all-to-all-done.near = bf16[16,144,128]{2,1,0:T(8,128)(2,1)S(1)} async-done(((bf16[16,144,128]{2,1,0:T(8,128)(2,1)}), bf16[16,144,128]{2,1,0:T(8,128)(2,1)S(1)}, u32[]{:S(2)}, u32[]{:S(2)}) %all-to-all-start) | async-done | bytes 589856 | tf_op jit(solution)/shard_map/all_to_all | solution.py:462
  24.6 3.9 %collective-permute-start.3 = (bf16[1024,128]{1,0:T(8,128)(2,1)S(1)}, bf16[1024,128]{1,0:T(8,128)(2,1)S(1)}, u32[]{:S(2)}, u32[]{:S(2)}) collective-permute-start(bf16[1024,128]{1,0:T(8,128)(2,1)S(1)} %get-tuple-element.103), channel_id=1, source_target_pairs={{0,2},{1,3},{2,0},{3,1},{4,6},{5,7},{6,4},{7,5},{8,10},{9,11},{10,... | collective-permute-start | bytes 786440 | tf_op jit(solution)/shard_map/ppermute | solution.py:458
  30.1 8.1 %propagate_0.1 = (bf16[4096,128]{1,0:T(8,128)(2,1)}, bf16[16,128,128]{2,1,0:T(8,128)(2,1)}, bf16[1056,128]{1,0:T(8,128)(2,1)}, bf16[1056,128]{1,0:T(8,128)(2,1)}...) custom-call(s32[259]{0:T(512)} %pad_add_fusion.cols, bf16[32,8,128,128]{3,2,1,0:T(8,128)(2,1)} %tiles.5, ...), custom_call_target="tpu_custom_call" | custom-call | flops 1073741824 | bytes 12582912 | tf_op jit(solution)/shard_map/propagate_0/pallas_call | solution.py:164
  38.2 3.9 %all-to-all-start.1 = ((bf16[16,128,128]{2,1,0:T(8,128)(2,1)}), bf16[16,128,128]{2,1,0:T(8,128)(2,1)S(1)}, u32[]{:S(2)}, u32[]{:S(2)}) async-start(bf16[16,128,128]{2,1,0:T(8,128)(2,1)} %get-tuple-element.106), calls=%async_computation.1 | async-start | bytes 1048576 | tf_op jit(solution)/shard_map/all_to_all | solution.py:462
  43.2 2.3 %collective-permute-start.5 = (bf16[1056,128]{1,0:T(8,128)(2,1)}, bf16[1056,128]{1,0:T(8,128)(2,1)S(1)}, u32[]{:S(2)}, u32[]{:S(2)}) collective-permute-start(bf16[1056,128]{1,0:T(8,128)(2,1)} %get-tuple-element.108), channel_id=1, source_target_pairs={{0,3},{1,0},{2,1},{3,2},{4,7},{5,4},{6,5},{7,6},{8,11},{9,8},{10,9... | collective-permute-start | bytes 811016 | tf_op jit(solution)/shard_map/ppermute | solution.py:458
  45.5 6.5 %collective-permute-done.4.lab1.refs_4_.refs_5_ = bf16[1056,128]{1,0:T(8,128)(2,1)S(1)} collective-permute-done((bf16[1056,128]{1,0:T(8,128)(2,1)}, bf16[1056,128]{1,0:T(8,128)(2,1)S(1)}, u32[]{:S(2)}, u32[]{:S(2)}) %collective-permute-start.4) | collective-permute-done | bytes 270368 | tf_op jit(solution)/shard_map/ppermute | solution.py:458
  51.9 2.0 %all-to-all-done.1.near = bf16[16,128,128]{2,1,0:T(8,128)(2,1)S(1)} async-done(((bf16[16,128,128]{2,1,0:T(8,128)(2,1)}), bf16[16,128,128]{2,1,0:T(8,128)(2,1)S(1)}, u32[]{:S(2)}, u32[]{:S(2)}) %all-to-all-start.1) | async-done | bytes 524320 | tf_op jit(solution)/shard_map/all_to_all | solution.py:462
  56.7 7.9 %propagate_1.1 = (bf16[4096,128]{1,0:T(8,128)(2,1)}, bf16[16,128,128]{2,1,0:T(8,128)(2,1)}, bf16[1024,128]{1,0:T(8,128)(2,1)}, bf16[1024,128]{1,0:T(8,128)(2,1)}...) custom-call(s32[259]{0:T(512)} %pad_add_fusion.cols, bf16[32,8,128,128]{3,2,1,0:T(8,128)(2,1)} %tiles.5, ...), custom_call_target="tpu_custom_call" | custom-call | flops 1073741824 | bytes 12582912 | tf_op jit(solution)/shard_map/propagate_1/pallas_call | solution.py:164
  64.6 5.0 %all-to-all-start.2 = ((bf16[16,128,128]{2,1,0:T(8,128)(2,1)}), bf16[16,128,128]{2,1,0:T(8,128)(2,1)}, u32[]{:S(2)}, u32[]{:S(2)}) async-start(bf16[16,128,128]{2,1,0:T(8,128)(2,1)} %get-tuple-element.119), calls=%async_computation.2 | async-start | bytes 1048576 | tf_op jit(solution)/shard_map/all_to_all | solution.py:462
  69.6 2.0 %collective-permute-start.8 = (bf16[1024,128]{1,0:T(8,128)(2,1)}, bf16[1024,128]{1,0:T(8,128)(2,1)S(1)}, u32[]{:S(2)}, u32[]{:S(2)}) collective-permute-start(bf16[1024,128]{1,0:T(8,128)(2,1)} %get-tuple-element.120), channel_id=1, source_target_pairs={{0,1},{1,2},{2,3},{3,0},{4,5},{5,6},{6,7},{7,4},{8,9},{9,10},{10,1... | collective-permute-start | bytes 786440 | tf_op jit(solution)/shard_map/ppermute | solution.py:458
  73.0 3.8 %count_labels.1.refs_5_ = f32[1024,256]{1,0:T(8,128)S(1)} custom-call(s32[4]{0:T(128)S(1)} %pad_add_fusion.1.pos, bf16[1056,128]{1,0:T(8,128)(2,1)S(1)} %copy-done.5, bf16[1056,128]{1,0:T(8,128)(2,1)S(1)} %collective-permute-done.4.lab1.refs_4_.refs_5_, bf16[1056,128]{1,0:T(8,128)(2,1)S(1)} %collective-permute-done.7.lab2.refs_7_.refs_1_, ...), custom_call_target="tpu_custom_call" | custom-call | flops 2147483648 | bytes 2097152 | tf_op jit(solution)/shard_map/count_labels/pallas_call | solution.py:211
  79.6 1.9 all-to-all-done.2.near
  85.4 7.8 %propagate_2.1 = (bf16[1024,128]{1,0:T(8,128)(2,1)}, bf16[1024,128]{1,0:T(8,128)(2,1)}, bf16[1024,128]{1,0:T(8,128)(2,1)}, bf16[1024,128]{1,0:T(8,128)(2,1)}) custom-call(s32[259]{0:T(512)} %pad_add_fusion.cols, bf16[32,8,128,128]{3,2,1,0:T(8,128)(2,1)} %tiles.5, bf16[4096,128]{1,0:T(8,128)(2,1)} %get-tuple-element.118.hop, ...), custom_call_target="tpu_custom_call" | custom-call | flops 1073741824 | bytes 12582912 | tf_op jit(solution)/shard_map/propagate_2/pallas_call | solution.py:164
  93.2 1.9 collective-permute-start.12
  95.1 1.9 %collective-permute-start.13 = (bf16[1024,128]{1,0:T(8,128)(2,1)}, bf16[1024,128]{1,0:T(8,128)(2,1)S(1)}, u32[]{:S(2)}, u32[]{:S(2)}) collective-permute-start(bf16[1024,128]{1,0:T(8,128)(2,1)} %get-tuple-element.135), channel_id=1, source_target_pairs={{0,1},{1,2},{2,3},{3,0},{4,5},{5,6},{6,7},{7,4},{8,9},{9,10},{10,1... | collective-permute-start | bytes 786440 | tf_op jit(solution)/shard_map/ppermute | solution.py:458
  98.4 5.6 %first_layer_early.1.refs_4_ = f32[1024,1024]{1,0:T(8,128)S(1)} custom-call(s32[4]{0:T(128)S(1)} %pad_add_fusion.1.pos, bf16[1024,128]{1,0:T(8,128)(2,1)S(1)} %get-tuple-element.92.refs_0_, bf16[1056,128]{1,0:T(8,128)(2,1)S(1)} %copy-done.5, bf16[1024,128]{1,0:T(8,128)(2,1)S(1)} %copy-done.6, bf16[1024,128]{1,0:T(8,128)(2,1)S(1)} %collective-permute-done.refs_3_.refs_4_, ...), custom_call_target="tpu_custom_call" | custom-call | flops 3221225472 | bytes 11534336 | tf_op jit(solution)/shard_map/first_layer_early/pallas_call | solution.py:277
  104.2 4.9 %collective-permute-done.13.refs_1_.refs_7_ = bf16[1024,128]{1,0:T(8,128)(2,1)S(1)} collective-permute-done((bf16[1024,128]{1,0:T(8,128)(2,1)}, bf16[1024,128]{1,0:T(8,128)(2,1)S(1)}, u32[]{:S(2)}, u32[]{:S(2)}) %collective-permute-start.13) | collective-permute-done | bytes 262176 | tf_op jit(solution)/shard_map/ppermute | solution.py:458
  109.3 14.0 %mlp.1 = (bf16[1024,1024]{1,0:T(8,128)(2,1)S(1)}, bf16[1024,1024]{1,0:T(8,128)(2,1)S(1)}, bf16[1024,256]{1,0:T(8,128)(2,1)S(1)}, bf16[1024,1024]{1,0:T(8,128)(2,1)S(1)}, bf16[1024,1024]{1,0:T(8,128)(2,1)S(1)}) custom-call(s32[4]{0:T(128)S(1)} %pad_add_fusion.1.pos, bf16[1024,128]{1,0:T(8,128)(2,1)S(1)} %copy-done.7, ...), custom_call_target="tpu_custom_call" | custom-call | flops 6442450944 | bytes 20971520 | tf_op jit(solution)/shard_map/mlp/pallas_call | solution.py:296
  125.3 3.6 %outer_grads.1 = (bf16[4,16,16,640]{3,2,1,0:T(8,128)(2,1)S(1)}, bf16[4,16,16,640]{3,2,1,0:T(8,128)(2,1)S(1)}) custom-call(s32[4]{0:T(128)S(1)} %pad_add_fusion.1.pos, bf16[1024,1024]{1,0:T(8,128)(2,1)S(1)} %get-tuple-element.144.act1, bf16[1024,1024]{1,0:T(8,128)(2,1)S(1)} %get-tuple-element.145.act2, bf16[1024,256]{1,0:T(8,128)(2,1)S(1)} %get-tuple-element.146.gl, ...), custom_call_target="tpu_custom_call" | custom-call | flops 2684354560 | bytes 8388608 | tf_op jit(solution)/shard_map/outer_grads/pallas_call | solution.py:340
  132.9 2.9 %first_grads_13.1 = (bf16[2,16,16,1024]{3,2,1,0:T(8,128)(2,1)S(1)}, bf16[2,16,16,1024]{3,2,1,0:T(8,128)(2,1)S(1)}) custom-call(s32[4]{0:T(128)S(1)} %pad_add_fusion.1.pos, bf16[1024,128]{1,0:T(8,128)(2,1)S(1)} %collective-permute-done.1.refs_9_.refs_0_, bf16[1056,128]{1,0:T(8,128)(2,1)S(1)} %collective-permute-done.5.lab3.refs_10_.refs_1_, ...), custom_call_target="tpu_custom_call" | custom-call | flops 2147483648 | bytes 6291456 | tf_op jit(solution)/shard_map/first_grads_13/pallas_call | solution.py:370
  135.8 3.3 %collective-permute-done.17.ahead = bf16[8,16,1024]{2,1,0:T(8,128)(2,1)S(1)} collective-permute-done((bf16[8,16,1024]{2,1,0:T(8,128)(2,1)S(1)}, bf16[8,16,1024]{2,1,0:T(8,128)(2,1)S(1)}, u32[]{:S(2)}, u32[]{:S(2)}) %collective-permute-start.17) | collective-permute-done | bytes 262176 | tf_op jit(solution)/shard_map/ppermute | solution.py:458
  140.1 2.6 %collective-permute-start.22 = (bf16[8,16,640]{2,1,0:T(8,128)(2,1)S(1)}, bf16[8,16,640]{2,1,0:T(8,128)(2,1)S(1)}, u32[]{:S(2)}, u32[]{:S(2)}) collective-permute-start(bf16[8,16,640]{2,1,0:T(8,128)(2,1)S(1)} %get-tuple-element.171), channel_id=1, source_target_pairs={{0,3},{1,0},{2,1},{3,2},{4,7},{5,4},{6,5},{7,6},{8,11},{9,8},{10,9... | collective-permute-start | bytes 491528 | tf_op jit(solution)/shard_map/ppermute | solution.py:458
  144.7 2.7 %collective-permute-done.21.ahead = bf16[8,16,640]{2,1,0:T(8,128)(2,1)S(1)} collective-permute-done((bf16[8,16,640]{2,1,0:T(8,128)(2,1)S(1)}, bf16[8,16,640]{2,1,0:T(8,128)(2,1)S(1)}, u32[]{:S(2)}, u32[]{:S(2)}) %collective-permute-start.21) | collective-permute-done | bytes 163872 | tf_op jit(solution)/shard_map/ppermute | solution.py:458
  148.6 2.4 %collective-permute-start.24 = (bf16[16,16,1024]{2,1,0:T(8,128)(2,1)S(1)}, bf16[16,16,1024]{2,1,0:T(8,128)(2,1)S(1)}, u32[]{:S(2)}, u32[]{:S(2)}) collective-permute-start(bf16[16,16,1024]{2,1,0:T(8,128)(2,1)S(1)} %get-tuple-element.176), channel_id=1, source_target_pairs={{0,3},{1,0},{2,1},{3,2},{4,7},{5,4},{6,5},{7,6},{8,11},{9,8},{10,9... | collective-permute-start | bytes 1572872 | tf_op jit(solution)/shard_map/ppermute | solution.py:458
  151.3 3.2 %collective-permute-start.26 = (bf16[16,16,640]{2,1,0:T(8,128)(2,1)S(1)}, bf16[16,16,640]{2,1,0:T(8,128)(2,1)S(1)}, u32[]{:S(2)}, u32[]{:S(2)}) collective-permute-start(bf16[16,16,640]{2,1,0:T(8,128)(2,1)S(1)} %get-tuple-element.180), channel_id=1, source_target_pairs={{0,3},{1,0},{2,1},{3,2},{4,7},{5,4},{6,5},{7,6},{8,11},{9,8},{10,9... | collective-permute-start | bytes 983048 | tf_op jit(solution)/shard_map/ppermute | solution.py:458
  154.5 15.0 %collective-permute-done.25.rm1 = bf16[16,16,640]{2,1,0:T(8,128)(2,1)S(1)} collective-permute-done((bf16[16,16,640]{2,1,0:T(8,128)(2,1)S(1)}, bf16[16,16,640]{2,1,0:T(8,128)(2,1)S(1)}, u32[]{:S(2)}, u32[]{:S(2)}) %collective-permute-start.25) | collective-permute-done | bytes 327712 | tf_op jit(solution)/shard_map/ppermute | solution.py:458
  170.0 19.6 %all_to_all.20.parts = bf16[16,16,1664]{2,1,0:T(8,128)(2,1)S(1)} all-to-all(bf16[16,16,1664]{2,1,0:T(8,128)(2,1)S(1)} %own_share.1), channel_id=1, replica_groups=mesh['y'=4,'x'=4,'core'=2,'rep'=4] {'y','x'}, dimensions={0} | all-to-all | bytes 1703936 | tf_op jit(solution)/shard_map/all_to_all | solution.py:462
  (89 shorter events, 29.5 us)
Async XLA Ops:
  5.2 19.4 %all-to-all-start = ((bf16[16,144,128]{2,1,0:T(8,128)(2,1)}), bf16[16,144,128]{2,1,0:T(8,128)(2,1)S(1)}, u32[]{:S(2)}, u32[]{:S(2)}) async-start(bf16[16,144,128]{2,1,0:T(8,128)(2,1)} %get-tuple-element.93), calls=%async_computation | async-start | bytes 1179648 | tf_op jit(solution)/shard_map/all_to_all | solution.py:462
  12.3 10.1 %collective-permute-start = (bf16[1024,128]{1,0:T(8,128)(2,1)S(1)}, bf16[1024,128]{1,0:T(8,128)(2,1)S(1)}, u32[]{:S(2)}, u32[]{:S(2)}) collective-permute-start(bf16[1024,128]{1,0:T(8,128)(2,1)S(1)} %get-tuple-element.94), channel_id=1, source_target_pairs={{0,1},{1,2},{2,3},{3,0},{4,5},{5,6},{6,7},{7,4},{8,9},{9,10},{10,1... | collective-permute-start | bytes 786440 | tf_op jit(solution)/shard_map/ppermute | solution.py:458
  14.3 8.1 %collective-permute-start.1 = (bf16[1024,128]{1,0:T(8,128)(2,1)S(1)}, bf16[1024,128]{1,0:T(8,128)(2,1)S(1)}, u32[]{:S(2)}, u32[]{:S(2)}) collective-permute-start(bf16[1024,128]{1,0:T(8,128)(2,1)S(1)} %get-tuple-element.95), channel_id=1, source_target_pairs={{0,3},{1,0},{2,1},{3,2},{4,7},{5,4},{6,5},{7,6},{8,11},{9,8},{10,9... | collective-permute-start | bytes 786440 | tf_op jit(solution)/shard_map/ppermute | solution.py:458
  24.6 4.7 %collective-permute-start.2 = (bf16[16,144,128]{2,1,0:T(8,128)(2,1)S(1)}, bf16[16,144,128]{2,1,0:T(8,128)(2,1)S(1)}, u32[]{:S(2)}, u32[]{:S(2)}) collective-permute-start(bf16[16,144,128]{2,1,0:T(8,128)(2,1)S(1)} %all-to-all-done.near), channel_id=1, source_target_pairs={{0,4},{4,0},{1,5},{5,1},{2,6},{6,2},{3,7},{7,3},{8,12},{12,8},{9,1... | collective-permute-start | bytes 1769480 | tf_op jit(solution)/shard_map/ppermute | solution.py:458
  24.6 13.6 %collective-permute-start.3 = (bf16[1024,128]{1,0:T(8,128)(2,1)S(1)}, bf16[1024,128]{1,0:T(8,128)(2,1)S(1)}, u32[]{:S(2)}, u32[]{:S(2)}) collective-permute-start(bf16[1024,128]{1,0:T(8,128)(2,1)S(1)} %get-tuple-element.103), channel_id=1, source_target_pairs={{0,2},{1,3},{2,0},{3,1},{4,6},{5,7},{6,4},{7,5},{8,10},{9,11},{10,... | collective-permute-start | bytes 786440 | tf_op jit(solution)/shard_map/ppermute | solution.py:458
  38.2 15.8 %all-to-all-start.1 = ((bf16[16,128,128]{2,1,0:T(8,128)(2,1)}), bf16[16,128,128]{2,1,0:T(8,128)(2,1)S(1)}, u32[]{:S(2)}, u32[]{:S(2)}) async-start(bf16[16,128,128]{2,1,0:T(8,128)(2,1)} %get-tuple-element.106), calls=%async_computation.1 | async-start | bytes 1048576 | tf_op jit(solution)/shard_map/all_to_all | solution.py:462
  42.1 30.8 %copy-start.5 = (bf16[1056,128]{1,0:T(8,128)(2,1)S(1)}, bf16[1056,128]{1,0:T(8,128)(2,1)}, u32[]{:S(2)}) copy-start(bf16[1056,128]{1,0:T(8,128)(2,1)} %get-tuple-element.104.lab0.refs_1_) | copy-start | bytes 811012
  42.1 30.8 %copy-start.8 = (s32[1,4096]{1,0:T(1,128)S(1)}, s32[1,4096]{1,0:T(1,128)}, u32[]{:S(2)}) copy-start(s32[1,4096]{1,0:T(1,128)} %param.15) | copy-start | bytes 49156
  42.1 9.8 %collective-permute-start.4 = (bf16[1056,128]{1,0:T(8,128)(2,1)}, bf16[1056,128]{1,0:T(8,128)(2,1)S(1)}, u32[]{:S(2)}, u32[]{:S(2)}) collective-permute-start(bf16[1056,128]{1,0:T(8,128)(2,1)} %get-tuple-element.107), channel_id=1, source_target_pairs={{0,1},{1,2},{2,3},{3,0},{4,5},{5,6},{6,7},{7,4},{8,9},{9,10},{10,1... | collective-permute-start | bytes 811016 | tf_op jit(solution)/shard_map/ppermute | solution.py:458
  43.2 8.7 %collective-permute-start.5 = (bf16[1056,128]{1,0:T(8,128)(2,1)}, bf16[1056,128]{1,0:T(8,128)(2,1)S(1)}, u32[]{:S(2)}, u32[]{:S(2)}) collective-permute-start(bf16[1056,128]{1,0:T(8,128)(2,1)} %get-tuple-element.108), channel_id=1, source_target_pairs={{0,3},{1,0},{2,1},{3,2},{4,7},{5,4},{6,5},{7,6},{8,11},{9,8},{10,9... | collective-permute-start | bytes 811016 | tf_op jit(solution)/shard_map/ppermute | solution.py:458
  54.0 1.9 %collective-permute-start.6 = (bf16[16,128,128]{2,1,0:T(8,128)(2,1)S(1)}, bf16[16,128,128]{2,1,0:T(8,128)(2,1)S(1)}, u32[]{:S(2)}, u32[]{:S(2)}) collective-permute-start(bf16[16,128,128]{2,1,0:T(8,128)(2,1)S(1)} %all-to-all-done.1.near), channel_id=1, source_target_pairs={{0,4},{4,0},{1,5},{5,1},{2,6},{6,2},{3,7},{7,3},{8,12},{12,8},{9,1... | collective-permute-start | bytes 1572872 | tf_op jit(solution)/shard_map/ppermute | solution.py:458
  54.0 10.6 %collective-permute-start.7 = (bf16[1056,128]{1,0:T(8,128)(2,1)}, bf16[1056,128]{1,0:T(8,128)(2,1)S(1)}, u32[]{:S(2)}, u32[]{:S(2)}) collective-permute-start(bf16[1056,128]{1,0:T(8,128)(2,1)} %get-tuple-element.116), channel_id=1, source_target_pairs={{0,2},{1,3},{2,0},{3,1},{4,6},{5,7},{6,4},{7,5},{8,10},{9,11},{10,... | collective-permute-start | bytes 811016 | tf_op jit(solution)/shard_map/ppermute | solution.py:458
  64.6 16.9 %all-to-all-start.2 = ((bf16[16,128,128]{2,1,0:T(8,128)(2,1)}), bf16[16,128,128]{2,1,0:T(8,128)(2,1)}, u32[]{:S(2)}, u32[]{:S(2)}) async-start(bf16[16,128,128]{2,1,0:T(8,128)(2,1)} %get-tuple-element.119), calls=%async_computation.2 | async-start | bytes 1048576 | tf_op jit(solution)/shard_map/all_to_all | solution.py:462
  69.6 9.6 %collective-permute-start.8 = (bf16[1024,128]{1,0:T(8,128)(2,1)}, bf16[1024,128]{1,0:T(8,128)(2,1)S(1)}, u32[]{:S(2)}, u32[]{:S(2)}) collective-permute-start(bf16[1024,128]{1,0:T(8,128)(2,1)} %get-tuple-element.120), channel_id=1, source_target_pairs={{0,1},{1,2},{2,3},{3,0},{4,5},{5,6},{6,7},{7,4},{8,9},{9,10},{10,1... | collective-permute-start | bytes 786440 | tf_op jit(solution)/shard_map/ppermute | solution.py:458
  71.6 8.0 %collective-permute-start.9 = (bf16[1024,128]{1,0:T(8,128)(2,1)}, bf16[1024,128]{1,0:T(8,128)(2,1)S(1)}, u32[]{:S(2)}, u32[]{:S(2)}) collective-permute-start(bf16[1024,128]{1,0:T(8,128)(2,1)} %get-tuple-element.121), channel_id=1, source_target_pairs={{0,3},{1,0},{2,1},{3,2},{4,7},{5,4},{6,5},{7,6},{8,11},{9,8},{10,9... | collective-permute-start | bytes 786440 | tf_op jit(solution)/shard_map/ppermute | solution.py:458
  81.5 3.9 %collective-permute-start.10 = (bf16[16,128,128]{2,1,0:T(8,128)(2,1)}, bf16[16,128,128]{2,1,0:T(8,128)(2,1)}, u32[]{:S(2)}, u32[]{:S(2)}) collective-permute-start(bf16[16,128,128]{2,1,0:T(8,128)(2,1)} %all-to-all-done.2.near), channel_id=1, source_target_pairs={{0,4},{4,0},{1,5},{5,1},{2,6},{6,2},{3,7},{7,3},{8,12},{12,8},{9,1... | collective-permute-start | bytes 1572872 | tf_op jit(solution)/shard_map/ppermute | solution.py:458
  81.5 11.7 %collective-permute-start.11 = (bf16[1024,128]{1,0:T(8,128)(2,1)}, bf16[1024,128]{1,0:T(8,128)(2,1)S(1)}, u32[]{:S(2)}, u32[]{:S(2)}) collective-permute-start(bf16[1024,128]{1,0:T(8,128)(2,1)} %get-tuple-element.130), channel_id=1, source_target_pairs={{0,2},{1,3},{2,0},{3,1},{4,6},{5,7},{6,4},{7,5},{8,10},{9,11},{10,... | collective-permute-start | bytes 786440 | tf_op jit(solution)/shard_map/ppermute | solution.py:458
  93.2 11.0 %collective-permute-start.12 = (bf16[1024,128]{1,0:T(8,128)(2,1)}, bf16[1024,128]{1,0:T(8,128)(2,1)S(1)}, u32[]{:S(2)}, u32[]{:S(2)}) collective-permute-start(bf16[1024,128]{1,0:T(8,128)(2,1)} %get-tuple-element.134), channel_id=1, source_target_pairs={{0,2},{1,3},{2,0},{3,1},{4,6},{5,7},{6,4},{7,5},{8,10},{9,11},{10,... | collective-permute-start | bytes 786440 | tf_op jit(solution)/shard_map/ppermute | solution.py:458
  95.1 14.0 %collective-permute-start.13 = (bf16[1024,128]{1,0:T(8,128)(2,1)}, bf16[1024,128]{1,0:T(8,128)(2,1)S(1)}, u32[]{:S(2)}, u32[]{:S(2)}) collective-permute-start(bf16[1024,128]{1,0:T(8,128)(2,1)} %get-tuple-element.135), channel_id=1, source_target_pairs={{0,1},{1,2},{2,3},{3,0},{4,5},{5,6},{6,7},{7,4},{8,9},{9,10},{10,1... | collective-permute-start | bytes 786440 | tf_op jit(solution)/shard_map/ppermute | solution.py:458
  97.0 12.3 %collective-permute-start.14 = (bf16[1024,128]{1,0:T(8,128)(2,1)}, bf16[1024,128]{1,0:T(8,128)(2,1)S(1)}, u32[]{:S(2)}, u32[]{:S(2)}) collective-permute-start(bf16[1024,128]{1,0:T(8,128)(2,1)} %get-tuple-element.136), channel_id=1, source_target_pairs={{0,3},{1,0},{2,1},{3,2},{4,7},{5,4},{6,5},{7,6},{8,11},{9,8},{10,9... | collective-permute-start | bytes 786440 | tf_op jit(solution)/shard_map/ppermute | solution.py:458
  125.2 3.7 %collective-permute-start.15 = (bf16[1,16,16,1024]{3,2,1,0:T(8,128)(2,1)S(1)}, bf16[1,16,16,1024]{3,2,1,0:T(8,128)(2,1)S(1)}, u32[]{:S(2)}, u32[]{:S(2)}) collective-permute-start(bf16[1,16,16,1024]{3,2,1,0:T(8,128)(2,1)S(1)} %get-tuple-element.143), channel_id=1, source_target_pairs={{0,4},{4,0},{1,5},{5,1},{2,6},{6,2},{3,7},{7,3},{8,12},{12,8},{9,1... | collective-permute-start | bytes 1572872 | tf_op jit(solution)/shard_map/ppermute | solution.py:458
  128.9 10.5 %collective-permute-start.16 = (bf16[4,16,16,640]{3,2,1,0:T(8,128)(2,1)S(1)}, bf16[4,16,16,640]{3,2,1,0:T(8,128)(2,1)S(1)}, u32[]{:S(2)}, u32[]{:S(2)}) collective-permute-start(bf16[4,16,16,640]{3,2,1,0:T(8,128)(2,1)S(1)} %get-tuple-element.152), channel_id=1, source_target_pairs={{0,4},{4,0},{1,5},{5,1},{2,6},{6,2},{3,7},{7,3},{8,12},{12,8},{9,1... | collective-permute-start | bytes 3932168 | tf_op jit(solution)/shard_map/ppermute | solution.py:458
  129.6 9.5 %collective-permute-start.17 = (bf16[8,16,1024]{2,1,0:T(8,128)(2,1)S(1)}, bf16[8,16,1024]{2,1,0:T(8,128)(2,1)S(1)}, u32[]{:S(2)}, u32[]{:S(2)}) collective-permute-start(bf16[8,16,1024]{2,1,0:T(8,128)(2,1)S(1)} %get-tuple-element.158), channel_id=1, source_target_pairs={{0,1},{1,2},{2,3},{3,0},{4,5},{5,6},{6,7},{7,4},{8,9},{9,10},{10,1... | collective-permute-start | bytes 786440 | tf_op jit(solution)/shard_map/ppermute | solution.py:458
  131.4 8.0 %collective-permute-start.18 = (bf16[8,16,1024]{2,1,0:T(8,128)(2,1)S(1)}, bf16[8,16,1024]{2,1,0:T(8,128)(2,1)S(1)}, u32[]{:S(2)}, u32[]{:S(2)}) collective-permute-start(bf16[8,16,1024]{2,1,0:T(8,128)(2,1)S(1)} %get-tuple-element.159), channel_id=1, source_target_pairs={{0,3},{1,0},{2,1},{3,2},{4,7},{5,4},{6,5},{7,6},{8,11},{9,8},{10,9... | collective-permute-start | bytes 786440 | tf_op jit(solution)/shard_map/ppermute | solution.py:458
  139.4 8.0 %collective-permute-start.20 = (bf16[2,16,16,1024]{3,2,1,0:T(8,128)(2,1)S(1)}, bf16[2,16,16,1024]{3,2,1,0:T(8,128)(2,1)S(1)}, u32[]{:S(2)}, u32[]{:S(2)}) collective-permute-start(bf16[2,16,16,1024]{3,2,1,0:T(8,128)(2,1)S(1)} %get-tuple-element.167), channel_id=1, source_target_pairs={{0,4},{4,0},{1,5},{5,1},{2,6},{6,2},{3,7},{7,3},{8,12},{12,8},{9,1... | collective-permute-start | bytes 3145736 | tf_op jit(solution)/shard_map/ppermute | solution.py:458
  139.5 7.9 %collective-permute-start.21 = (bf16[8,16,640]{2,1,0:T(8,128)(2,1)S(1)}, bf16[8,16,640]{2,1,0:T(8,128)(2,1)S(1)}, u32[]{:S(2)}, u32[]{:S(2)}) collective-permute-start(bf16[8,16,640]{2,1,0:T(8,128)(2,1)S(1)} %get-tuple-element.170), channel_id=1, source_target_pairs={{0,1},{1,2},{2,3},{3,0},{4,5},{5,6},{6,7},{7,4},{8,9},{9,10},{10,1... | collective-permute-start | bytes 491528 | tf_op jit(solution)/shard_map/ppermute | solution.py:458
  140.1 7.2 %collective-permute-start.22 = (bf16[8,16,640]{2,1,0:T(8,128)(2,1)S(1)}, bf16[8,16,640]{2,1,0:T(8,128)(2,1)S(1)}, u32[]{:S(2)}, u32[]{:S(2)}) collective-permute-start(bf16[8,16,640]{2,1,0:T(8,128)(2,1)S(1)} %get-tuple-element.171), channel_id=1, source_target_pairs={{0,3},{1,0},{2,1},{3,2},{4,7},{5,4},{6,5},{7,6},{8,11},{9,8},{10,9... | collective-permute-start | bytes 491528 | tf_op jit(solution)/shard_map/ppermute | solution.py:458
  144.6 9.9 %collective-permute-start.19 = (bf16[1,16,16,1024]{3,2,1,0:T(8,128)(2,1)S(1)}, bf16[1,16,16,1024]{3,2,1,0:T(8,128)(2,1)S(1)}, u32[]{:S(2)}, u32[]{:S(2)}) collective-permute-start(bf16[1,16,16,1024]{3,2,1,0:T(8,128)(2,1)S(1)} %get-tuple-element.165), channel_id=1, source_target_pairs={{0,4},{4,0},{1,5},{5,1},{2,6},{6,2},{3,7},{7,3},{8,12},{12,8},{9,1... | collective-permute-start | bytes 1572872 | tf_op jit(solution)/shard_map/ppermute | solution.py:458
  147.7 21.9 %collective-permute-start.23 = (bf16[16,16,1024]{2,1,0:T(8,128)(2,1)S(1)}, bf16[16,16,1024]{2,1,0:T(8,128)(2,1)S(1)}, u32[]{:S(2)}, u32[]{:S(2)}) collective-permute-start(bf16[16,16,1024]{2,1,0:T(8,128)(2,1)S(1)} %get-tuple-element.175), channel_id=1, source_target_pairs={{0,1},{1,2},{2,3},{3,0},{4,5},{5,6},{6,7},{7,4},{8,9},{9,10},{10,1... | collective-permute-start | bytes 1572872 | tf_op jit(solution)/shard_map/ppermute | solution.py:458
  148.6 20.9 %collective-permute-start.24 = (bf16[16,16,1024]{2,1,0:T(8,128)(2,1)S(1)}, bf16[16,16,1024]{2,1,0:T(8,128)(2,1)S(1)}, u32[]{:S(2)}, u32[]{:S(2)}) collective-permute-start(bf16[16,16,1024]{2,1,0:T(8,128)(2,1)S(1)} %get-tuple-element.176), channel_id=1, source_target_pairs={{0,3},{1,0},{2,1},{3,2},{4,7},{5,4},{6,5},{7,6},{8,11},{9,8},{10,9... | collective-permute-start | bytes 1572872 | tf_op jit(solution)/shard_map/ppermute | solution.py:458
  151.2 18.4 %collective-permute-start.25 = (bf16[16,16,640]{2,1,0:T(8,128)(2,1)S(1)}, bf16[16,16,640]{2,1,0:T(8,128)(2,1)S(1)}, u32[]{:S(2)}, u32[]{:S(2)}) collective-permute-start(bf16[16,16,640]{2,1,0:T(8,128)(2,1)S(1)} %get-tuple-element.179), channel_id=1, source_target_pairs={{0,1},{1,2},{2,3},{3,0},{4,5},{5,6},{6,7},{7,4},{8,9},{9,10},{10,1... | collective-permute-start | bytes 983048 | tf_op jit(solution)/shard_map/ppermute | solution.py:458
  151.3 18.3 %collective-permute-start.26 = (bf16[16,16,640]{2,1,0:T(8,128)(2,1)S(1)}, bf16[16,16,640]{2,1,0:T(8,128)(2,1)S(1)}, u32[]{:S(2)}, u32[]{:S(2)}) collective-permute-start(bf16[16,16,640]{2,1,0:T(8,128)(2,1)S(1)} %get-tuple-element.180), channel_id=1, source_target_pairs={{0,3},{1,0},{2,1},{3,2},{4,7},{5,4},{6,5},{7,6},{8,11},{9,8},{10,9... | collective-permute-start | bytes 983048 | tf_op jit(solution)/shard_map/ppermute | solution.py:458
  (16 other events, 139.6 us)

commit v3 on v1

--- a/solution.py
+++ b/solution.py
@@ -516,8 +516,10 @@
     got2 = shift(send2, "core", 1)
     keep2, gf = lax.optimization_barrier((keep2, gf))
     keep13, send13 = first_grads(pos, pieces, gf, (1, 3))
+    got_m, got2, keep13, send13, gf = lax.optimization_barrier(
+        (got_m, got2, keep13, send13, gf)
+    )
     got13 = shift(send13, "core", 1)
-    got_m, got2, keep13, gf = lax.optimization_barrier((got_m, got2, keep13, gf))
     far_m = send_far(2, keep_m, got_m, "y", "middle")
     far_f = send_far(0, keep2, got2, "rep", "first")
     keep0, send0 = first_grads(pos, pieces, gf, (0,))

time: 185 us -> 182 us (0.984)
  waiting for transfers between devices: 41.5 us -> 38.7 us
    ppermute x27, waiting for transfers between devices: 35 us -> 31.9 us  [shift(): lax.ppermute(value, axis, [(i, (i + by) % size) for i in range(size)])]
where the time goes in v3:
time: 182 us; the launch traced here: 181 us
  Pallas kernels  62.7 us (34%)
  starting transfers between devices  57.3 us (31%)
  waiting for transfers between devices  38.7 us (21%)
  blocking collectives  14.3 us (8%)
  local copies, waits for them, and re-layouts  6.64 us (4%)
    ppermute x27, starting transfers between devices, shift(): lax.ppermute(value, axis, [(i, (i + by) % size) for i in range(size)])  36.5 us
    ppermute x27, waiting for transfers between devices, shift(): lax.ppermute(value, axis, [(i, (i + by) % size) for i in range(size)])  31.9 us
    pallas_call x3, Pallas kernels, propagate(): pl.pallas_call(functools.partial(prop_kernel, h), in_specs=[whole(pltpu.S...  23.7 us
    all_to_all x4, starting transfers between devices, swap(): return lax.all_to_all(value, axes, split_axis=0, concat_axis=0, tiled=True)  20.8 us
    all_to_all x1, blocking collectives, swap(): return lax.all_to_all(value, axes, split_axis=0, concat_axis=0, tiled=True)  14.3 us
    pallas_call x1, Pallas kernels, mlp(): pl.pallas_call(mlp_kernel, grid_spec=pltpu.PrefetchScalarGridSpec(num_sca...  14 us
    all_to_all x4, waiting for transfers between devices, swap(): return lax.all_to_all(value, axes, split_axis=0, concat_axis=0, tiled=True)  6.83 us
    pallas_call x3, Pallas kernels, first_grads(): pl.pallas_call(functools.partial(first_kernel, steps), in_specs=[whole(pl...  6.68 us
  transfers between devices with their start and end apart: 31, of which 14 were waited for; matrix products, arithmetic and copies ran while one was open for 1% of the time, Pallas kernels for 23%

profile of v3, /device:TPU:0, one launch (start us, length us, event | category | flops | bytes accessed | tf_op | source)
XLA Modules:
  0.0 181.3 jit_solution(617012520401464281)
XLA Ops:
  3.3 1.9 %export_first.1 = (bf16[16,144,128]{2,1,0:T(8,128)(2,1)}, bf16[1024,128]{1,0:T(8,128)(2,1)S(1)}, bf16[1024,128]{1,0:T(8,128)(2,1)S(1)}, bf16[1024,128]{1,0:T(8,128)(2,1)S(1)}, bf16[1024,128]{1,0:T(8,128)(2,1)S(1)}) custom-call(s32[4]{0:T(128)S(1)} %pad_add_fusion.1.pos, bf16[4096,128]{1,0:T(8,128)(2,1)S(1)} %copy-done, s32[1,128]{1,0:T(1,128)S(1)} %copy-done.1, ...), custom_call_target="tpu_custom_call" | custom-call | flops 134217728 | bytes 2097152 | tf_op jit(solution)/shard_map/export_first/pallas_call | solution.py:83
  5.2 7.1 %all-to-all-start = ((bf16[16,144,128]{2,1,0:T(8,128)(2,1)}), bf16[16,144,128]{2,1,0:T(8,128)(2,1)S(1)}, u32[]{:S(2)}, u32[]{:S(2)}) async-start(bf16[16,144,128]{2,1,0:T(8,128)(2,1)} %get-tuple-element.82), calls=%async_computation | async-start | bytes 1179648 | tf_op jit(solution)/shard_map/all_to_all | solution.py:459
  12.3 2.0 %collective-permute-start = (bf16[1024,128]{1,0:T(8,128)(2,1)S(1)}, bf16[1024,128]{1,0:T(8,128)(2,1)S(1)}, u32[]{:S(2)}, u32[]{:S(2)}) collective-permute-start(bf16[1024,128]{1,0:T(8,128)(2,1)S(1)} %get-tuple-element.83), channel_id=1, source_target_pairs={{0,1},{1,2},{2,3},{3,0},{4,5},{5,6},{6,7},{7,4},{8,9},{9,10},{10,1... | collective-permute-start | bytes 786440 | tf_op jit(solution)/shard_map/ppermute | solution.py:455
  14.3 2.2 %collective-permute-start.1 = (bf16[1024,128]{1,0:T(8,128)(2,1)S(1)}, bf16[1024,128]{1,0:T(8,128)(2,1)S(1)}, u32[]{:S(2)}, u32[]{:S(2)}) collective-permute-start(bf16[1024,128]{1,0:T(8,128)(2,1)S(1)} %get-tuple-element.84), channel_id=1, source_target_pairs={{0,3},{1,0},{2,1},{3,2},{4,7},{5,4},{6,5},{7,6},{8,11},{9,8},{10,9... | collective-permute-start | bytes 786440 | tf_op jit(solution)/shard_map/ppermute | solution.py:455
  16.5 5.9 %collective-permute-done.refs_3_.refs_4_ = bf16[1024,128]{1,0:T(8,128)(2,1)S(1)} collective-permute-done((bf16[1024,128]{1,0:T(8,128)(2,1)S(1)}, bf16[1024,128]{1,0:T(8,128)(2,1)S(1)}, u32[]{:S(2)}, u32[]{:S(2)}) %collective-permute-start) | collective-permute-done | bytes 262176 | tf_op jit(solution)/shard_map/ppermute | solution.py:455
  22.5 2.1 %all-to-all-done.near = bf16[16,144,128]{2,1,0:T(8,128)(2,1)S(1)} async-done(((bf16[16,144,128]{2,1,0:T(8,128)(2,1)}), bf16[16,144,128]{2,1,0:T(8,128)(2,1)S(1)}, u32[]{:S(2)}, u32[]{:S(2)}) %all-to-all-start) | async-done | bytes 589856 | tf_op jit(solution)/shard_map/all_to_all | solution.py:459
  24.6 3.9 %collective-permute-start.3 = (bf16[1024,128]{1,0:T(8,128)(2,1)S(1)}, bf16[1024,128]{1,0:T(8,128)(2,1)S(1)}, u32[]{:S(2)}, u32[]{:S(2)}) collective-permute-start(bf16[1024,128]{1,0:T(8,128)(2,1)S(1)} %get-tuple-element.92), channel_id=1, source_target_pairs={{0,2},{1,3},{2,0},{3,1},{4,6},{5,7},{6,4},{7,5},{8,10},{9,11},{10,... | collective-permute-start | bytes 786440 | tf_op jit(solution)/shard_map/ppermute | solution.py:455
  30.1 8.1 %propagate_0.1 = (bf16[4096,128]{1,0:T(8,128)(2,1)}, bf16[16,128,128]{2,1,0:T(8,128)(2,1)}, bf16[1056,128]{1,0:T(8,128)(2,1)}, bf16[1056,128]{1,0:T(8,128)(2,1)}...) custom-call(s32[259]{0:T(512)} %pad_add_fusion.cols, bf16[32,8,128,128]{3,2,1,0:T(8,128)(2,1)} %tiles.5, ...), custom_call_target="tpu_custom_call" | custom-call | flops 1073741824 | bytes 12582912 | tf_op jit(solution)/shard_map/propagate_0/pallas_call | solution.py:164
  38.2 3.9 %all-to-all-start.1 = ((bf16[16,128,128]{2,1,0:T(8,128)(2,1)}), bf16[16,128,128]{2,1,0:T(8,128)(2,1)S(1)}, u32[]{:S(2)}, u32[]{:S(2)}) async-start(bf16[16,128,128]{2,1,0:T(8,128)(2,1)} %get-tuple-element.95), calls=%async_computation.1 | async-start | bytes 1048576 | tf_op jit(solution)/shard_map/all_to_all | solution.py:459
  43.2 2.3 %collective-permute-start.5 = (bf16[1056,128]{1,0:T(8,128)(2,1)}, bf16[1056,128]{1,0:T(8,128)(2,1)S(1)}, u32[]{:S(2)}, u32[]{:S(2)}) collective-permute-start(bf16[1056,128]{1,0:T(8,128)(2,1)} %get-tuple-element.97), channel_id=1, source_target_pairs={{0,3},{1,0},{2,1},{3,2},{4,7},{5,4},{6,5},{7,6},{8,11},{9,8},{10,9... | collective-permute-start | bytes 811016 | tf_op jit(solution)/shard_map/ppermute | solution.py:455
  45.4 6.5 %collective-permute-done.4.lab1.refs_4_.refs_5_ = bf16[1056,128]{1,0:T(8,128)(2,1)S(1)} collective-permute-done((bf16[1056,128]{1,0:T(8,128)(2,1)}, bf16[1056,128]{1,0:T(8,128)(2,1)S(1)}, u32[]{:S(2)}, u32[]{:S(2)}) %collective-permute-start.4) | collective-permute-done | bytes 270368 | tf_op jit(solution)/shard_map/ppermute | solution.py:455
  51.9 2.0 %all-to-all-done.1.near = bf16[16,128,128]{2,1,0:T(8,128)(2,1)S(1)} async-done(((bf16[16,128,128]{2,1,0:T(8,128)(2,1)}), bf16[16,128,128]{2,1,0:T(8,128)(2,1)S(1)}, u32[]{:S(2)}, u32[]{:S(2)}) %all-to-all-start.1) | async-done | bytes 524320 | tf_op jit(solution)/shard_map/all_to_all | solution.py:459
  56.7 7.9 %propagate_1.1 = (bf16[4096,128]{1,0:T(8,128)(2,1)}, bf16[16,128,128]{2,1,0:T(8,128)(2,1)}, bf16[1024,128]{1,0:T(8,128)(2,1)}, bf16[1024,128]{1,0:T(8,128)(2,1)}...) custom-call(s32[259]{0:T(512)} %pad_add_fusion.cols, bf16[32,8,128,128]{3,2,1,0:T(8,128)(2,1)} %tiles.5, ...), custom_call_target="tpu_custom_call" | custom-call | flops 1073741824 | bytes 12582912 | tf_op jit(solution)/shard_map/propagate_1/pallas_call | solution.py:164
  64.6 5.0 %all-to-all-start.2 = ((bf16[16,128,128]{2,1,0:T(8,128)(2,1)}), bf16[16,128,128]{2,1,0:T(8,128)(2,1)}, u32[]{:S(2)}, u32[]{:S(2)}) async-start(bf16[16,128,128]{2,1,0:T(8,128)(2,1)} %get-tuple-element.108), calls=%async_computation.2 | async-start | bytes 1048576 | tf_op jit(solution)/shard_map/all_to_all | solution.py:459
  69.6 2.0 %collective-permute-start.8 = (bf16[1024,128]{1,0:T(8,128)(2,1)}, bf16[1024,128]{1,0:T(8,128)(2,1)S(1)}, u32[]{:S(2)}, u32[]{:S(2)}) collective-permute-start(bf16[1024,128]{1,0:T(8,128)(2,1)} %get-tuple-element.109), channel_id=1, source_target_pairs={{0,1},{1,2},{2,3},{3,0},{4,5},{5,6},{6,7},{7,4},{8,9},{9,10},{10,1... | collective-permute-start | bytes 786440 | tf_op jit(solution)/shard_map/ppermute | solution.py:455
  72.9 3.8 %count_labels.1.refs_5_ = f32[1024,256]{1,0:T(8,128)S(1)} custom-call(s32[4]{0:T(128)S(1)} %pad_add_fusion.1.pos, bf16[1056,128]{1,0:T(8,128)(2,1)S(1)} %copy-done.5, bf16[1056,128]{1,0:T(8,128)(2,1)S(1)} %collective-permute-done.4.lab1.refs_4_.refs_5_, bf16[1056,128]{1,0:T(8,128)(2,1)S(1)} %collective-permute-done.7.lab2.refs_7_.refs_1_, ...), custom_call_target="tpu_custom_call" | custom-call | flops 2147483648 | bytes 2097152 | tf_op jit(solution)/shard_map/count_labels/pallas_call | solution.py:211
  79.6 1.9 %all-to-all-done.2.near = bf16[16,128,128]{2,1,0:T(8,128)(2,1)} async-done(((bf16[16,128,128]{2,1,0:T(8,128)(2,1)}), bf16[16,128,128]{2,1,0:T(8,128)(2,1)}, u32[]{:S(2)}, u32[]{:S(2)}) %all-to-all-start.2) | async-done | bytes 524320 | tf_op jit(solution)/shard_map/all_to_all | solution.py:459
  84.6 7.8 %propagate_2.1 = (bf16[1024,128]{1,0:T(8,128)(2,1)}, bf16[1024,128]{1,0:T(8,128)(2,1)}, bf16[1024,128]{1,0:T(8,128)(2,1)}, bf16[1024,128]{1,0:T(8,128)(2,1)}) custom-call(s32[259]{0:T(512)} %pad_add_fusion.cols, bf16[32,8,128,128]{3,2,1,0:T(8,128)(2,1)} %tiles.5, bf16[4096,128]{1,0:T(8,128)(2,1)} %get-tuple-element.107.hop, ...), custom_call_target="tpu_custom_call" | custom-call | flops 1073741824 | bytes 12582912 | tf_op jit(solution)/shard_map/propagate_2/pallas_call | solution.py:164
  92.3 2.1 %collective-permute-start.12 = (bf16[1024,128]{1,0:T(8,128)(2,1)}, bf16[1024,128]{1,0:T(8,128)(2,1)S(1)}, u32[]{:S(2)}, u32[]{:S(2)}) collective-permute-start(bf16[1024,128]{1,0:T(8,128)(2,1)} %get-tuple-element.121), channel_id=1, source_target_pairs={{0,1},{1,2},{2,3},{3,0},{4,5},{5,6},{6,7},{7,4},{8,9},{9,10},{10,1... | collective-permute-start | bytes 786440 | tf_op jit(solution)/shard_map/ppermute | solution.py:455
  94.4 2.3 %collective-permute-start.13 = (bf16[1024,128]{1,0:T(8,128)(2,1)}, bf16[1024,128]{1,0:T(8,128)(2,1)S(1)}, u32[]{:S(2)}, u32[]{:S(2)}) collective-permute-start(bf16[1024,128]{1,0:T(8,128)(2,1)} %get-tuple-element.122), channel_id=1, source_target_pairs={{0,2},{1,3},{2,0},{3,1},{4,6},{5,7},{6,4},{7,5},{8,10},{9,11},{10,... | collective-permute-start | bytes 786440 | tf_op jit(solution)/shard_map/ppermute | solution.py:455
  97.4 5.6 %first_layer_early.1.refs_4_ = f32[1024,1024]{1,0:T(8,128)S(1)} custom-call(s32[4]{0:T(128)S(1)} %pad_add_fusion.1.pos, bf16[1024,128]{1,0:T(8,128)(2,1)S(1)} %get-tuple-element.81.refs_0_, bf16[1056,128]{1,0:T(8,128)(2,1)S(1)} %copy-done.5, bf16[1024,128]{1,0:T(8,128)(2,1)S(1)} %copy-done.6, bf16[1024,128]{1,0:T(8,128)(2,1)S(1)} %collective-permute-done.refs_3_.refs_4_, ...), custom_call_target="tpu_custom_call" | custom-call | flops 3221225472 | bytes 11534336 | tf_op jit(solution)/shard_map/first_layer_early/pallas_call | solution.py:277
  103.0 6.0 %collective-permute-done.13.refs_2_.refs_3_ = bf16[1024,128]{1,0:T(8,128)(2,1)S(1)} collective-permute-done((bf16[1024,128]{1,0:T(8,128)(2,1)}, bf16[1024,128]{1,0:T(8,128)(2,1)S(1)}, u32[]{:S(2)}, u32[]{:S(2)}) %collective-permute-start.13) | collective-permute-done | bytes 262176 | tf_op jit(solution)/shard_map/ppermute | solution.py:455
  109.0 14.0 %mlp.1 = (bf16[1024,1024]{1,0:T(8,128)(2,1)S(1)}, bf16[1024,1024]{1,0:T(8,128)(2,1)S(1)}, bf16[1024,256]{1,0:T(8,128)(2,1)S(1)}, bf16[1024,1024]{1,0:T(8,128)(2,1)S(1)}, bf16[1024,1024]{1,0:T(8,128)(2,1)S(1)}) custom-call(s32[4]{0:T(128)S(1)} %pad_add_fusion.1.pos, bf16[1024,128]{1,0:T(8,128)(2,1)S(1)} %copy-done.7, ...), custom_call_target="tpu_custom_call" | custom-call | flops 6442450944 | bytes 20971520 | tf_op jit(solution)/shard_map/mlp/pallas_call | solution.py:296
  123.0 3.7 %outer_grads.1 = (bf16[4,16,16,640]{3,2,1,0:T(8,128)(2,1)S(1)}, bf16[4,16,16,640]{3,2,1,0:T(8,128)(2,1)S(1)}) custom-call(s32[4]{0:T(128)S(1)} %pad_add_fusion.1.pos, bf16[1024,1024]{1,0:T(8,128)(2,1)S(1)} %get-tuple-element.131.act1, bf16[1024,1024]{1,0:T(8,128)(2,1)S(1)} %get-tuple-element.132.act2, bf16[1024,256]{1,0:T(8,128)(2,1)S(1)} %get-tuple-element.133.gl, ...), custom_call_target="tpu_custom_call" | custom-call | flops 2684354560 | bytes 8388608 | tf_op jit(solution)/shard_map/outer_grads/pallas_call | solution.py:337
  126.8 1.9 %first_grads_2.1 = (bf16[1,16,16,1024]{3,2,1,0:T(8,128)(2,1)S(1)}, bf16[1,16,16,1024]{3,2,1,0:T(8,128)(2,1)S(1)}) custom-call(s32[4]{0:T(128)S(1)} %pad_add_fusion.1.pos, bf16[1024,128]{1,0:T(8,128)(2,1)S(1)} %collective-permute-done.3.refs_6_.refs_0_, bf16[1056,128]{1,0:T(8,128)(2,1)S(1)} %collective-permute-done.7.lab2.refs_7_.refs_1_, ...), custom_call_target="tpu_custom_call" | custom-call | flops 1073741824 | bytes 6291456 | tf_op jit(solution)/shard_map/first_grads_2/pallas_call | solution.py:367
  129.2 3.0 %first_grads_13.1 = (bf16[2,16,16,1024]{3,2,1,0:T(8,128)(2,1)S(1)}, bf16[2,16,16,1024]{3,2,1,0:T(8,128)(2,1)S(1)}) custom-call(s32[4]{0:T(128)S(1)} %pad_add_fusion.1.pos, bf16[1024,128]{1,0:T(8,128)(2,1)S(1)} %collective-permute-done.1.refs_9_.refs_0_, bf16[1056,128]{1,0:T(8,128)(2,1)S(1)} %collective-permute-done.5.lab3.refs_10_.refs_1_, ...), custom_call_target="tpu_custom_call" | custom-call | flops 2147483648 | bytes 6291456 | tf_op jit(solution)/shard_map/first_grads_13/pallas_call | solution.py:367
  132.5 3.2 %collective-permute-start.24 = (bf16[8,16,640]{2,1,0:T(8,128)(2,1)S(1)}, bf16[8,16,640]{2,1,0:T(8,128)(2,1)S(1)}, u32[]{:S(2)}, u32[]{:S(2)}) collective-permute-start(bf16[8,16,640]{2,1,0:T(8,128)(2,1)S(1)} %get-tuple-element.156), channel_id=1, source_target_pairs={{0,96},{32,0},{64,32},{96,64},{1,97},{33,1},{65,33},{97,65},{2,98}... | collective-permute-start | bytes 491528 | tf_op jit(solution)/shard_map/ppermute | solution.py:455
  140.5 3.2 %collective-permute-start.26 = (bf16[16,16,640]{2,1,0:T(8,128)(2,1)S(1)}, bf16[16,16,640]{2,1,0:T(8,128)(2,1)S(1)}, u32[]{:S(2)}, u32[]{:S(2)}) collective-permute-start(bf16[16,16,640]{2,1,0:T(8,128)(2,1)S(1)} %get-tuple-element.158), channel_id=1, source_target_pairs={{0,96},{32,0},{64,32},{96,64},{1,97},{33,1},{65,33},{97,65},{2,98}... | collective-permute-start | bytes 983048 | tf_op jit(solution)/shard_map/ppermute | solution.py:455
  143.8 1.8 %first_grads_0.1 = (bf16[1,16,16,1024]{3,2,1,0:T(8,128)(2,1)S(1)}, bf16[1,16,16,1024]{3,2,1,0:T(8,128)(2,1)S(1)}) custom-call(s32[4]{0:T(128)S(1)} %pad_add_fusion.1.pos, bf16[1024,128]{1,0:T(8,128)(2,1)S(1)} %get-tuple-element.81.refs_0_, bf16[1056,128]{1,0:T(8,128)(2,1)S(1)} %copy-done.5, bf16[1024,128]{1,0:T(8,128)(2,1)S(1)} %copy-done.6, ...), custom_call_target="tpu_custom_call" | custom-call | flops 1073741824 | bytes 6291456 | tf_op jit(solution)/shard_map/first_grads_0/pallas_call | solution.py:367
  151.9 4.8 %all-to-all-start.4 = ((bf16[16,16,640]{2,1,0:T(8,128)(2,1)}), bf16[16,16,640]{2,1,0:T(8,128)(2,1)S(1)}, u32[]{:S(2)}, u32[]{:S(2)}) async-start(bf16[16,16,640]{2,1,0:T(8,128)(2,1)} %own_middle.1), calls=%async_computation.4 | async-start | bytes 655360 | tf_op jit(solution)/shard_map/all_to_all | solution.py:459
  156.8 8.4 %collective-permute-done.21.r1 = bf16[16,16,1024]{2,1,0:T(8,128)(2,1)S(1)} collective-permute-done((bf16[16,16,1024]{2,1,0:T(8,128)(2,1)}, bf16[16,16,1024]{2,1,0:T(8,128)(2,1)S(1)}, u32[]{:S(2)}, u32[]{:S(2)}) %collective-permute-start.21) | collective-permute-done | bytes 524320 | tf_op jit(solution)/shard_map/ppermute | solution.py:455
  166.3 14.3 %all_to_all.25.part_f = bf16[16,16,1024]{2,1,0:T(8,128)(2,1)S(1)} all-to-all(bf16[16,16,1024]{2,1,0:T(8,128)(2,1)S(1)} %own_first.1), channel_id=1, replica_groups=mesh['y'=4,'x'=4,'core'=2,'rep'=4] {'y','x'}, dimensions={0} | all-to-all | bytes 1048576 | tf_op jit(solution)/shard_map/all_to_all | solution.py:459
  (90 shorter events, 29.8 us)
Async XLA Ops:
  5.2 19.4 %all-to-all-start = ((bf16[16,144,128]{2,1,0:T(8,128)(2,1)}), bf16[16,144,128]{2,1,0:T(8,128)(2,1)S(1)}, u32[]{:S(2)}, u32[]{:S(2)}) async-start(bf16[16,144,128]{2,1,0:T(8,128)(2,1)} %get-tuple-element.82), calls=%async_computation | async-start | bytes 1179648 | tf_op jit(solution)/shard_map/all_to_all | solution.py:459
  12.3 10.1 %collective-permute-start = (bf16[1024,128]{1,0:T(8,128)(2,1)S(1)}, bf16[1024,128]{1,0:T(8,128)(2,1)S(1)}, u32[]{:S(2)}, u32[]{:S(2)}) collective-permute-start(bf16[1024,128]{1,0:T(8,128)(2,1)S(1)} %get-tuple-element.83), channel_id=1, source_target_pairs={{0,1},{1,2},{2,3},{3,0},{4,5},{5,6},{6,7},{7,4},{8,9},{9,10},{10,1... | collective-permute-start | bytes 786440 | tf_op jit(solution)/shard_map/ppermute | solution.py:455
  14.3 8.1 %collective-permute-start.1 = (bf16[1024,128]{1,0:T(8,128)(2,1)S(1)}, bf16[1024,128]{1,0:T(8,128)(2,1)S(1)}, u32[]{:S(2)}, u32[]{:S(2)}) collective-permute-start(bf16[1024,128]{1,0:T(8,128)(2,1)S(1)} %get-tuple-element.84), channel_id=1, source_target_pairs={{0,3},{1,0},{2,1},{3,2},{4,7},{5,4},{6,5},{7,6},{8,11},{9,8},{10,9... | collective-permute-start | bytes 786440 | tf_op jit(solution)/shard_map/ppermute | solution.py:455
  24.6 4.7 %collective-permute-start.2 = (bf16[16,144,128]{2,1,0:T(8,128)(2,1)S(1)}, bf16[16,144,128]{2,1,0:T(8,128)(2,1)S(1)}, u32[]{:S(2)}, u32[]{:S(2)}) collective-permute-start(bf16[16,144,128]{2,1,0:T(8,128)(2,1)S(1)} %all-to-all-done.near), channel_id=1, source_target_pairs={{0,4},{4,0},{1,5},{5,1},{2,6},{6,2},{3,7},{7,3},{8,12},{12,8},{9,1... | collective-permute-start | bytes 1769480 | tf_op jit(solution)/shard_map/ppermute | solution.py:455
  24.6 13.6 %collective-permute-start.3 = (bf16[1024,128]{1,0:T(8,128)(2,1)S(1)}, bf16[1024,128]{1,0:T(8,128)(2,1)S(1)}, u32[]{:S(2)}, u32[]{:S(2)}) collective-permute-start(bf16[1024,128]{1,0:T(8,128)(2,1)S(1)} %get-tuple-element.92), channel_id=1, source_target_pairs={{0,2},{1,3},{2,0},{3,1},{4,6},{5,7},{6,4},{7,5},{8,10},{9,11},{10,... | collective-permute-start | bytes 786440 | tf_op jit(solution)/shard_map/ppermute | solution.py:455
  38.2 15.8 %all-to-all-start.1 = ((bf16[16,128,128]{2,1,0:T(8,128)(2,1)}), bf16[16,128,128]{2,1,0:T(8,128)(2,1)S(1)}, u32[]{:S(2)}, u32[]{:S(2)}) async-start(bf16[16,128,128]{2,1,0:T(8,128)(2,1)} %get-tuple-element.95), calls=%async_computation.1 | async-start | bytes 1048576 | tf_op jit(solution)/shard_map/all_to_all | solution.py:459
  42.1 30.8 %copy-start.5 = (bf16[1056,128]{1,0:T(8,128)(2,1)S(1)}, bf16[1056,128]{1,0:T(8,128)(2,1)}, u32[]{:S(2)}) copy-start(bf16[1056,128]{1,0:T(8,128)(2,1)} %get-tuple-element.93.lab0.refs_1_) | copy-start | bytes 811012
  42.1 9.8 %collective-permute-start.4 = (bf16[1056,128]{1,0:T(8,128)(2,1)}, bf16[1056,128]{1,0:T(8,128)(2,1)S(1)}, u32[]{:S(2)}, u32[]{:S(2)}) collective-permute-start(bf16[1056,128]{1,0:T(8,128)(2,1)} %get-tuple-element.96), channel_id=1, source_target_pairs={{0,1},{1,2},{2,3},{3,0},{4,5},{5,6},{6,7},{7,4},{8,9},{9,10},{10,1... | collective-permute-start | bytes 811016 | tf_op jit(solution)/shard_map/ppermute | solution.py:455
  43.2 8.8 %collective-permute-start.5 = (bf16[1056,128]{1,0:T(8,128)(2,1)}, bf16[1056,128]{1,0:T(8,128)(2,1)S(1)}, u32[]{:S(2)}, u32[]{:S(2)}) collective-permute-start(bf16[1056,128]{1,0:T(8,128)(2,1)} %get-tuple-element.97), channel_id=1, source_target_pairs={{0,3},{1,0},{2,1},{3,2},{4,7},{5,4},{6,5},{7,6},{8,11},{9,8},{10,9... | collective-permute-start | bytes 811016 | tf_op jit(solution)/shard_map/ppermute | solution.py:455
  54.0 1.9 %collective-permute-start.6 = (bf16[16,128,128]{2,1,0:T(8,128)(2,1)S(1)}, bf16[16,128,128]{2,1,0:T(8,128)(2,1)S(1)}, u32[]{:S(2)}, u32[]{:S(2)}) collective-permute-start(bf16[16,128,128]{2,1,0:T(8,128)(2,1)S(1)} %all-to-all-done.1.near), channel_id=1, source_target_pairs={{0,4},{4,0},{1,5},{5,1},{2,6},{6,2},{3,7},{7,3},{8,12},{12,8},{9,1... | collective-permute-start | bytes 1572872 | tf_op jit(solution)/shard_map/ppermute | solution.py:455
  54.0 10.6 %collective-permute-start.7 = (bf16[1056,128]{1,0:T(8,128)(2,1)}, bf16[1056,128]{1,0:T(8,128)(2,1)S(1)}, u32[]{:S(2)}, u32[]{:S(2)}) collective-permute-start(bf16[1056,128]{1,0:T(8,128)(2,1)} %get-tuple-element.105), channel_id=1, source_target_pairs={{0,2},{1,3},{2,0},{3,1},{4,6},{5,7},{6,4},{7,5},{8,10},{9,11},{10,... | collective-permute-start | bytes 811016 | tf_op jit(solution)/shard_map/ppermute | solution.py:455
  64.6 16.9 %all-to-all-start.2 = ((bf16[16,128,128]{2,1,0:T(8,128)(2,1)}), bf16[16,128,128]{2,1,0:T(8,128)(2,1)}, u32[]{:S(2)}, u32[]{:S(2)}) async-start(bf16[16,128,128]{2,1,0:T(8,128)(2,1)} %get-tuple-element.108), calls=%async_computation.2 | async-start | bytes 1048576 | tf_op jit(solution)/shard_map/all_to_all | solution.py:459
  69.6 9.6 %collective-permute-start.8 = (bf16[1024,128]{1,0:T(8,128)(2,1)}, bf16[1024,128]{1,0:T(8,128)(2,1)S(1)}, u32[]{:S(2)}, u32[]{:S(2)}) collective-permute-start(bf16[1024,128]{1,0:T(8,128)(2,1)} %get-tuple-element.109), channel_id=1, source_target_pairs={{0,1},{1,2},{2,3},{3,0},{4,5},{5,6},{6,7},{7,4},{8,9},{9,10},{10,1... | collective-permute-start | bytes 786440 | tf_op jit(solution)/shard_map/ppermute | solution.py:455
  71.6 8.0 %collective-permute-start.9 = (bf16[1024,128]{1,0:T(8,128)(2,1)}, bf16[1024,128]{1,0:T(8,128)(2,1)S(1)}, u32[]{:S(2)}, u32[]{:S(2)}) collective-permute-start(bf16[1024,128]{1,0:T(8,128)(2,1)} %get-tuple-element.110), channel_id=1, source_target_pairs={{0,3},{1,0},{2,1},{3,2},{4,7},{5,4},{6,5},{7,6},{8,11},{9,8},{10,9... | collective-permute-start | bytes 786440 | tf_op jit(solution)/shard_map/ppermute | solution.py:455
  81.5 3.0 %collective-permute-start.10 = (bf16[16,128,128]{2,1,0:T(8,128)(2,1)}, bf16[16,128,128]{2,1,0:T(8,128)(2,1)}, u32[]{:S(2)}, u32[]{:S(2)}) collective-permute-start(bf16[16,128,128]{2,1,0:T(8,128)(2,1)} %all-to-all-done.2.near), channel_id=1, source_target_pairs={{0,4},{4,0},{1,5},{5,1},{2,6},{6,2},{3,7},{7,3},{8,12},{12,8},{9,1... | collective-permute-start | bytes 1572872 | tf_op jit(solution)/shard_map/ppermute | solution.py:455
  81.5 10.8 %collective-permute-start.11 = (bf16[1024,128]{1,0:T(8,128)(2,1)}, bf16[1024,128]{1,0:T(8,128)(2,1)S(1)}, u32[]{:S(2)}, u32[]{:S(2)}) collective-permute-start(bf16[1024,128]{1,0:T(8,128)(2,1)} %get-tuple-element.119), channel_id=1, source_target_pairs={{0,2},{1,3},{2,0},{3,1},{4,6},{5,7},{6,4},{7,5},{8,10},{9,11},{10,... | collective-permute-start | bytes 786440 | tf_op jit(solution)/shard_map/ppermute | solution.py:455
  92.3 10.6 %collective-permute-start.12 = (bf16[1024,128]{1,0:T(8,128)(2,1)}, bf16[1024,128]{1,0:T(8,128)(2,1)S(1)}, u32[]{:S(2)}, u32[]{:S(2)}) collective-permute-start(bf16[1024,128]{1,0:T(8,128)(2,1)} %get-tuple-element.121), channel_id=1, source_target_pairs={{0,1},{1,2},{2,3},{3,0},{4,5},{5,6},{6,7},{7,4},{8,9},{9,10},{10,1... | collective-permute-start | bytes 786440 | tf_op jit(solution)/shard_map/ppermute | solution.py:455
  94.4 14.6 %collective-permute-start.13 = (bf16[1024,128]{1,0:T(8,128)(2,1)}, bf16[1024,128]{1,0:T(8,128)(2,1)S(1)}, u32[]{:S(2)}, u32[]{:S(2)}) collective-permute-start(bf16[1024,128]{1,0:T(8,128)(2,1)} %get-tuple-element.122), channel_id=1, source_target_pairs={{0,2},{1,3},{2,0},{3,1},{4,6},{5,7},{6,4},{7,5},{8,10},{9,11},{10,... | collective-permute-start | bytes 786440 | tf_op jit(solution)/shard_map/ppermute | solution.py:455
  96.7 12.2 %collective-permute-start.14 = (bf16[1024,128]{1,0:T(8,128)(2,1)}, bf16[1024,128]{1,0:T(8,128)(2,1)S(1)}, u32[]{:S(2)}, u32[]{:S(2)}) collective-permute-start(bf16[1024,128]{1,0:T(8,128)(2,1)} %get-tuple-element.123), channel_id=1, source_target_pairs={{0,3},{1,0},{2,1},{3,2},{4,7},{5,4},{6,5},{7,6},{8,11},{9,8},{10,9... | collective-permute-start | bytes 786440 | tf_op jit(solution)/shard_map/ppermute | solution.py:455
  126.7 5.5 %collective-permute-start.15 = (bf16[4,16,16,640]{3,2,1,0:T(8,128)(2,1)S(1)}, bf16[4,16,16,640]{3,2,1,0:T(8,128)(2,1)S(1)}, u32[]{:S(2)}, u32[]{:S(2)}) collective-permute-start(bf16[4,16,16,640]{3,2,1,0:T(8,128)(2,1)S(1)} %get-tuple-element.135), channel_id=1, source_target_pairs={{0,4},{4,0},{1,5},{5,1},{2,6},{6,2},{3,7},{7,3},{8,12},{12,8},{9,1... | collective-permute-start | bytes 3932168 | tf_op jit(solution)/shard_map/ppermute | solution.py:455
  128.7 3.5 %collective-permute-start.16 = (bf16[1,16,16,1024]{3,2,1,0:T(8,128)(2,1)S(1)}, bf16[1,16,16,1024]{3,2,1,0:T(8,128)(2,1)S(1)}, u32[]{:S(2)}, u32[]{:S(2)}) collective-permute-start(bf16[1,16,16,1024]{3,2,1,0:T(8,128)(2,1)S(1)} %get-tuple-element.137), channel_id=1, source_target_pairs={{0,4},{4,0},{1,5},{5,1},{2,6},{6,2},{3,7},{7,3},{8,12},{12,8},{9,1... | collective-permute-start | bytes 1572872 | tf_op jit(solution)/shard_map/ppermute | solution.py:455
  132.2 13.5 %collective-permute-start.18 = (bf16[2,16,16,1024]{3,2,1,0:T(8,128)(2,1)S(1)}, bf16[2,16,16,1024]{3,2,1,0:T(8,128)(2,1)S(1)}, u32[]{:S(2)}, u32[]{:S(2)}) collective-permute-start(bf16[2,16,16,1024]{3,2,1,0:T(8,128)(2,1)S(1)} %get-tuple-element.146), channel_id=1, source_target_pairs={{0,4},{4,0},{1,5},{5,1},{2,6},{6,2},{3,7},{7,3},{8,12},{12,8},{9,1... | collective-permute-start | bytes 3145736 | tf_op jit(solution)/shard_map/ppermute | solution.py:455
  132.4 7.9 %collective-permute-start.23 = (bf16[8,16,640]{2,1,0:T(8,128)(2,1)S(1)}, bf16[8,16,640]{2,1,0:T(8,128)(2,1)S(1)}, u32[]{:S(2)}, u32[]{:S(2)}) collective-permute-start(bf16[8,16,640]{2,1,0:T(8,128)(2,1)S(1)} %get-tuple-element.155), channel_id=1, source_target_pairs={{0,32},{32,64},{64,96},{96,0},{1,33},{33,65},{65,97},{97,1},{2,34}... | collective-permute-start | bytes 491528 | tf_op jit(solution)/shard_map/ppermute | solution.py:455
  132.5 7.8 %collective-permute-start.24 = (bf16[8,16,640]{2,1,0:T(8,128)(2,1)S(1)}, bf16[8,16,640]{2,1,0:T(8,128)(2,1)S(1)}, u32[]{:S(2)}, u32[]{:S(2)}) collective-permute-start(bf16[8,16,640]{2,1,0:T(8,128)(2,1)S(1)} %get-tuple-element.156), channel_id=1, source_target_pairs={{0,96},{32,0},{64,32},{96,64},{1,97},{33,1},{65,33},{97,65},{2,98}... | collective-permute-start | bytes 491528 | tf_op jit(solution)/shard_map/ppermute | solution.py:455
  135.8 9.8 %collective-permute-start.19 = (bf16[8,16,1024]{2,1,0:T(8,128)(2,1)S(1)}, bf16[8,16,1024]{2,1,0:T(8,128)(2,1)S(1)}, u32[]{:S(2)}, u32[]{:S(2)}) collective-permute-start(bf16[8,16,1024]{2,1,0:T(8,128)(2,1)S(1)} %get-tuple-element.149), channel_id=1, source_target_pairs={{0,1},{1,2},{2,3},{3,0},{4,5},{5,6},{6,7},{7,4},{8,9},{9,10},{10,1... | collective-permute-start | bytes 786440 | tf_op jit(solution)/shard_map/ppermute | solution.py:455
  137.3 8.4 %collective-permute-start.20 = (bf16[8,16,1024]{2,1,0:T(8,128)(2,1)S(1)}, bf16[8,16,1024]{2,1,0:T(8,128)(2,1)S(1)}, u32[]{:S(2)}, u32[]{:S(2)}) collective-permute-start(bf16[8,16,1024]{2,1,0:T(8,128)(2,1)S(1)} %get-tuple-element.150), channel_id=1, source_target_pairs={{0,3},{1,0},{2,1},{3,2},{4,7},{5,4},{6,5},{7,6},{8,11},{9,8},{10,9... | collective-permute-start | bytes 786440 | tf_op jit(solution)/shard_map/ppermute | solution.py:455
  140.5 10.6 %collective-permute-start.25 = (bf16[16,16,640]{2,1,0:T(8,128)(2,1)S(1)}, bf16[16,16,640]{2,1,0:T(8,128)(2,1)S(1)}, u32[]{:S(2)}, u32[]{:S(2)}) collective-permute-start(bf16[16,16,640]{2,1,0:T(8,128)(2,1)S(1)} %get-tuple-element.157), channel_id=1, source_target_pairs={{0,32},{32,64},{64,96},{96,0},{1,33},{33,65},{65,97},{97,1},{2,34}... | collective-permute-start | bytes 983048 | tf_op jit(solution)/shard_map/ppermute | solution.py:455
  140.5 10.5 %collective-permute-start.26 = (bf16[16,16,640]{2,1,0:T(8,128)(2,1)S(1)}, bf16[16,16,640]{2,1,0:T(8,128)(2,1)S(1)}, u32[]{:S(2)}, u32[]{:S(2)}) collective-permute-start(bf16[16,16,640]{2,1,0:T(8,128)(2,1)S(1)} %get-tuple-element.158), channel_id=1, source_target_pairs={{0,96},{32,0},{64,32},{96,64},{1,97},{33,1},{65,33},{97,65},{2,98}... | collective-permute-start | bytes 983048 | tf_op jit(solution)/shard_map/ppermute | solution.py:455
  145.6 11.1 %collective-permute-start.17 = (bf16[1,16,16,1024]{3,2,1,0:T(8,128)(2,1)S(1)}, bf16[1,16,16,1024]{3,2,1,0:T(8,128)(2,1)S(1)}, u32[]{:S(2)}, u32[]{:S(2)}) collective-permute-start(bf16[1,16,16,1024]{3,2,1,0:T(8,128)(2,1)S(1)} %get-tuple-element.144), channel_id=1, source_target_pairs={{0,4},{4,0},{1,5},{5,1},{2,6},{6,2},{3,7},{7,3},{8,12},{12,8},{9,1... | collective-permute-start | bytes 1572872 | tf_op jit(solution)/shard_map/ppermute | solution.py:455
  146.8 18.4 %collective-permute-start.21 = (bf16[16,16,1024]{2,1,0:T(8,128)(2,1)}, bf16[16,16,1024]{2,1,0:T(8,128)(2,1)S(1)}, u32[]{:S(2)}, u32[]{:S(2)}) collective-permute-start(bf16[16,16,1024]{2,1,0:T(8,128)(2,1)} %get-tuple-element.151), channel_id=1, source_target_pairs={{0,1},{1,2},{2,3},{3,0},{4,5},{5,6},{6,7},{7,4},{8,9},{9,10},{10,1... | collective-permute-start | bytes 1572872 | tf_op jit(solution)/shard_map/ppermute | solution.py:455
  148.2 17.1 %collective-permute-start.22 = (bf16[16,16,1024]{2,1,0:T(8,128)(2,1)S(1)}, bf16[16,16,1024]{2,1,0:T(8,128)(2,1)S(1)}, u32[]{:S(2)}, u32[]{:S(2)}) collective-permute-start(bf16[16,16,1024]{2,1,0:T(8,128)(2,1)S(1)} %get-tuple-element.152), channel_id=1, source_target_pairs={{0,3},{1,0},{2,1},{3,2},{4,7},{5,4},{6,5},{7,6},{8,11},{9,8},{10,9... | collective-permute-start | bytes 1572872 | tf_op jit(solution)/shard_map/ppermute | solution.py:455
  151.9 14.4 %all-to-all-start.4 = ((bf16[16,16,640]{2,1,0:T(8,128)(2,1)}), bf16[16,16,640]{2,1,0:T(8,128)(2,1)S(1)}, u32[]{:S(2)}, u32[]{:S(2)}) async-start(bf16[16,16,640]{2,1,0:T(8,128)(2,1)} %own_middle.1), calls=%async_computation.4 | async-start | bytes 655360 | tf_op jit(solution)/shard_map/all_to_all | solution.py:459
  (16 other events, 161.8 us)

commit v4 on v3

--- a/solution.py
+++ b/solution.py
@@ -225,7 +225,7 @@
     )(pos, *both, shuffle, train)
 
 
-MLP_ROWS = 256
+MLP_ROWS = 512
 
 
 def slab_of(rep, d):
@@ -304,7 +304,7 @@
             out_specs=[row_block(w) for w in widths],
         ),
         out_shape=[struct((ROWS, w)) for w in widths],
-        compiler_params=params(36),
+        compiler_params=params(48),
         name="mlp",
         cost_estimate=pl.CostEstimate(
             flops=2 * ROWS * HID * (2 * HID + 512 + 2 * CP),

time: 182 us -> 187 us (1.027)
  local copies, waits for them, and re-layouts: 6.64 us -> 12.7 us
    unnamed x35 -> x43, local copies, waits for them, and re-layouts: 6.38 us -> 11.4 us
  transfers between devices with their start and end apart: 31 -> 31, of which waited for: 14 -> 13; matrix products, arithmetic and copies ran while one was open for 1% -> 2% of each run, Pallas kernels for 23% -> 22%
where the time goes in v4:
time: 187 us
  Pallas kernels  63.4 us (34%)
  starting transfers between devices  57.5 us (31%)
  waiting for transfers between devices  37.1 us (20%)
  blocking collectives  14.3 us (8%)
  local copies, waits for them, and re-layouts  12.7 us (7%)
    ppermute x27, starting transfers between devices, shift(): lax.ppermute(value, axis, [(i, (i + by) % size) for i in range(size)])  36.7 us
    ppermute x27, waiting for transfers between devices, shift(): lax.ppermute(value, axis, [(i, (i + by) % size) for i in range(size)])  30.5 us
    pallas_call x3, Pallas kernels, propagate(): pl.pallas_call(functools.partial(prop_kernel, h), in_specs=[whole(pltpu.S...  23.7 us
    all_to_all x4, starting transfers between devices, swap(): return lax.all_to_all(value, axes, split_axis=0, concat_axis=0, tiled=True)  20.8 us
    pallas_call x1, Pallas kernels, mlp(): pl.pallas_call(mlp_kernel, grid_spec=pltpu.PrefetchScalarGridSpec(num_sca...  15.1 us
    all_to_all x1, blocking collectives, swap(): return lax.all_to_all(value, axes, split_axis=0, concat_axis=0, tiled=True)  14.3 us
    unnamed x43, local copies, waits for them, and re-layouts  11.4 us
    pallas_call x3, Pallas kernels, first_grads(): pl.pallas_call(functools.partial(first_kernel, steps), in_specs=[whole(pl...  6.65 us
  transfers between devices with their start and end apart: 31, of which 13 were waited for; matrix products, arithmetic and copies ran while one was open for 2% of the time, Pallas kernels for 22%

profile of v4, /device:TPU:0, one launch (start us, length us, event | category | flops | bytes accessed | tf_op | source)
XLA Modules:
  0.0 186.7 jit_solution(7200472518914174910)
XLA Ops:
  3.3 1.9 %export_first.1 = (bf16[16,144,128]{2,1,0:T(8,128)(2,1)}, bf16[1024,128]{1,0:T(8,128)(2,1)S(1)}, bf16[1024,128]{1,0:T(8,128)(2,1)S(1)}, bf16[1024,128]{1,0:T(8,128)(2,1)S(1)}, bf16[1024,128]{1,0:T(8,128)(2,1)S(1)}) custom-call(s32[4]{0:T(128)S(1)} %pad_add_fusion.1.pos, bf16[4096,128]{1,0:T(8,128)(2,1)S(1)} %copy-done, s32[1,128]{1,0:T(1,128)S(1)} %copy-done.1, ...), custom_call_target="tpu_custom_call" | custom-call | flops 134217728 | bytes 2097152 | tf_op jit(solution)/shard_map/export_first/pallas_call | solution.py:83
  5.2 7.1 %all-to-all-start = ((bf16[16,144,128]{2,1,0:T(8,128)(2,1)}), bf16[16,144,128]{2,1,0:T(8,128)(2,1)S(1)}, u32[]{:S(2)}, u32[]{:S(2)}) async-start(bf16[16,144,128]{2,1,0:T(8,128)(2,1)} %get-tuple-element.82), calls=%async_computation | async-start | bytes 1179648 | tf_op jit(solution)/shard_map/all_to_all | solution.py:459
  12.3 2.0 %collective-permute-start = (bf16[1024,128]{1,0:T(8,128)(2,1)S(1)}, bf16[1024,128]{1,0:T(8,128)(2,1)S(1)}, u32[]{:S(2)}, u32[]{:S(2)}) collective-permute-start(bf16[1024,128]{1,0:T(8,128)(2,1)S(1)} %get-tuple-element.83), channel_id=1, source_target_pairs={{0,1},{1,2},{2,3},{3,0},{4,5},{5,6},{6,7},{7,4},{8,9},{9,10},{10,1... | collective-permute-start | bytes 786440 | tf_op jit(solution)/shard_map/ppermute | solution.py:455
  14.3 2.2 %collective-permute-start.1 = (bf16[1024,128]{1,0:T(8,128)(2,1)S(1)}, bf16[1024,128]{1,0:T(8,128)(2,1)S(1)}, u32[]{:S(2)}, u32[]{:S(2)}) collective-permute-start(bf16[1024,128]{1,0:T(8,128)(2,1)S(1)} %get-tuple-element.84), channel_id=1, source_target_pairs={{0,3},{1,0},{2,1},{3,2},{4,7},{5,4},{6,5},{7,6},{8,11},{9,8},{10,9... | collective-permute-start | bytes 786440 | tf_op jit(solution)/shard_map/ppermute | solution.py:455
  16.5 5.9 %collective-permute-done.refs_3_.refs_4_ = bf16[1024,128]{1,0:T(8,128)(2,1)S(1)} collective-permute-done((bf16[1024,128]{1,0:T(8,128)(2,1)S(1)}, bf16[1024,128]{1,0:T(8,128)(2,1)S(1)}, u32[]{:S(2)}, u32[]{:S(2)}) %collective-permute-start) | collective-permute-done | bytes 262176 | tf_op jit(solution)/shard_map/ppermute | solution.py:455
  22.5 2.1 %all-to-all-done.near = bf16[16,144,128]{2,1,0:T(8,128)(2,1)S(1)} async-done(((bf16[16,144,128]{2,1,0:T(8,128)(2,1)}), bf16[16,144,128]{2,1,0:T(8,128)(2,1)S(1)}, u32[]{:S(2)}, u32[]{:S(2)}) %all-to-all-start) | async-done | bytes 589856 | tf_op jit(solution)/shard_map/all_to_all | solution.py:459
  24.6 3.9 %collective-permute-start.3 = (bf16[1024,128]{1,0:T(8,128)(2,1)S(1)}, bf16[1024,128]{1,0:T(8,128)(2,1)S(1)}, u32[]{:S(2)}, u32[]{:S(2)}) collective-permute-start(bf16[1024,128]{1,0:T(8,128)(2,1)S(1)} %get-tuple-element.92), channel_id=1, source_target_pairs={{0,2},{1,3},{2,0},{3,1},{4,6},{5,7},{6,4},{7,5},{8,10},{9,11},{10,... | collective-permute-start | bytes 786440 | tf_op jit(solution)/shard_map/ppermute | solution.py:455
  30.1 8.0 %propagate_0.1 = (bf16[4096,128]{1,0:T(8,128)(2,1)}, bf16[16,128,128]{2,1,0:T(8,128)(2,1)}, bf16[1056,128]{1,0:T(8,128)(2,1)}, bf16[1056,128]{1,0:T(8,128)(2,1)}...) custom-call(s32[259]{0:T(512)} %pad_add_fusion.cols, bf16[32,8,128,128]{3,2,1,0:T(8,128)(2,1)} %tiles.5, ...), custom_call_target="tpu_custom_call" | custom-call | flops 1073741824 | bytes 12582912 | tf_op jit(solution)/shard_map/propagate_0/pallas_call | solution.py:164
  38.2 3.9 %all-to-all-start.1 = ((bf16[16,128,128]{2,1,0:T(8,128)(2,1)}), bf16[16,128,128]{2,1,0:T(8,128)(2,1)S(1)}, u32[]{:S(2)}, u32[]{:S(2)}) async-start(bf16[16,128,128]{2,1,0:T(8,128)(2,1)} %get-tuple-element.95), calls=%async_computation.1 | async-start | bytes 1048576 | tf_op jit(solution)/shard_map/all_to_all | solution.py:459
  43.2 2.3 %collective-permute-start.5 = (bf16[1056,128]{1,0:T(8,128)(2,1)}, bf16[1056,128]{1,0:T(8,128)(2,1)S(1)}, u32[]{:S(2)}, u32[]{:S(2)}) collective-permute-start(bf16[1056,128]{1,0:T(8,128)(2,1)} %get-tuple-element.97), channel_id=1, source_target_pairs={{0,3},{1,0},{2,1},{3,2},{4,7},{5,4},{6,5},{7,6},{8,11},{9,8},{10,9... | collective-permute-start | bytes 811016 | tf_op jit(solution)/shard_map/ppermute | solution.py:455
  45.4 6.5 %collective-permute-done.4.lab1.refs_4_.refs_5_ = bf16[1056,128]{1,0:T(8,128)(2,1)S(1)} collective-permute-done((bf16[1056,128]{1,0:T(8,128)(2,1)}, bf16[1056,128]{1,0:T(8,128)(2,1)S(1)}, u32[]{:S(2)}, u32[]{:S(2)}) %collective-permute-start.4) | collective-permute-done | bytes 270368 | tf_op jit(solution)/shard_map/ppermute | solution.py:455
  51.9 2.0 %all-to-all-done.1.near = bf16[16,128,128]{2,1,0:T(8,128)(2,1)S(1)} async-done(((bf16[16,128,128]{2,1,0:T(8,128)(2,1)}), bf16[16,128,128]{2,1,0:T(8,128)(2,1)S(1)}, u32[]{:S(2)}, u32[]{:S(2)}) %all-to-all-start.1) | async-done | bytes 524320 | tf_op jit(solution)/shard_map/all_to_all | solution.py:459
  56.7 7.9 %propagate_1.1 = (bf16[4096,128]{1,0:T(8,128)(2,1)}, bf16[16,128,128]{2,1,0:T(8,128)(2,1)}, bf16[1024,128]{1,0:T(8,128)(2,1)}, bf16[1024,128]{1,0:T(8,128)(2,1)}...) custom-call(s32[259]{0:T(512)} %pad_add_fusion.cols, bf16[32,8,128,128]{3,2,1,0:T(8,128)(2,1)} %tiles.5, ...), custom_call_target="tpu_custom_call" | custom-call | flops 1073741824 | bytes 12582912 | tf_op jit(solution)/shard_map/propagate_1/pallas_call | solution.py:164
  64.6 5.0 %all-to-all-start.2 = ((bf16[16,128,128]{2,1,0:T(8,128)(2,1)}), bf16[16,128,128]{2,1,0:T(8,128)(2,1)}, u32[]{:S(2)}, u32[]{:S(2)}) async-start(bf16[16,128,128]{2,1,0:T(8,128)(2,1)} %get-tuple-element.108), calls=%async_computation.2 | async-start | bytes 1048576 | tf_op jit(solution)/shard_map/all_to_all | solution.py:459
  69.6 2.0 %collective-permute-start.8 = (bf16[1024,128]{1,0:T(8,128)(2,1)}, bf16[1024,128]{1,0:T(8,128)(2,1)S(1)}, u32[]{:S(2)}, u32[]{:S(2)}) collective-permute-start(bf16[1024,128]{1,0:T(8,128)(2,1)} %get-tuple-element.109), channel_id=1, source_target_pairs={{0,1},{1,2},{2,3},{3,0},{4,5},{5,6},{6,7},{7,4},{8,9},{9,10},{10,1... | collective-permute-start | bytes 786440 | tf_op jit(solution)/shard_map/ppermute | solution.py:455
  72.9 3.8 %count_labels.1.refs_5_ = f32[1024,256]{1,0:T(8,128)S(1)} custom-call(s32[4]{0:T(128)S(1)} %pad_add_fusion.1.pos, bf16[1056,128]{1,0:T(8,128)(2,1)S(1)} %copy-done.4, bf16[1056,128]{1,0:T(8,128)(2,1)S(1)} %collective-permute-done.4.lab1.refs_4_.refs_5_, bf16[1056,128]{1,0:T(8,128)(2,1)S(1)} %collective-permute-done.7.lab2.refs_7_.refs_1_, ...), custom_call_target="tpu_custom_call" | custom-call | flops 2147483648 | bytes 2097152 | tf_op jit(solution)/shard_map/count_labels/pallas_call | solution.py:211
  79.6 1.9 %all-to-all-done.2.near = bf16[16,128,128]{2,1,0:T(8,128)(2,1)} async-done(((bf16[16,128,128]{2,1,0:T(8,128)(2,1)}), bf16[16,128,128]{2,1,0:T(8,128)(2,1)}, u32[]{:S(2)}, u32[]{:S(2)}) %all-to-all-start.2) | async-done | bytes 524320 | tf_op jit(solution)/shard_map/all_to_all | solution.py:459
  85.4 7.8 %propagate_2.1 = (bf16[1024,128]{1,0:T(8,128)(2,1)}, bf16[1024,128]{1,0:T(8,128)(2,1)}, bf16[1024,128]{1,0:T(8,128)(2,1)}, bf16[1024,128]{1,0:T(8,128)(2,1)}) custom-call(s32[259]{0:T(512)} %pad_add_fusion.cols, bf16[32,8,128,128]{3,2,1,0:T(8,128)(2,1)} %tiles.5, bf16[4096,128]{1,0:T(8,128)(2,1)} %get-tuple-element.107.hop, ...), custom_call_target="tpu_custom_call" | custom-call | flops 1073741824 | bytes 12582912 | tf_op jit(solution)/shard_map/propagate_2/pallas_call | solution.py:164
  93.2 2.1 %collective-permute-start.12 = (bf16[1024,128]{1,0:T(8,128)(2,1)}, bf16[1024,128]{1,0:T(8,128)(2,1)S(1)}, u32[]{:S(2)}, u32[]{:S(2)}) collective-permute-start(bf16[1024,128]{1,0:T(8,128)(2,1)} %get-tuple-element.121), channel_id=1, source_target_pairs={{0,1},{1,2},{2,3},{3,0},{4,5},{5,6},{6,7},{7,4},{8,9},{9,10},{10,1... | collective-permute-start | bytes 786440 | tf_op jit(solution)/shard_map/ppermute | solution.py:455
  95.2 2.3 %collective-permute-start.13 = (bf16[1024,128]{1,0:T(8,128)(2,1)}, bf16[1024,128]{1,0:T(8,128)(2,1)S(1)}, u32[]{:S(2)}, u32[]{:S(2)}) collective-permute-start(bf16[1024,128]{1,0:T(8,128)(2,1)} %get-tuple-element.122), channel_id=1, source_target_pairs={{0,2},{1,3},{2,0},{3,1},{4,6},{5,7},{6,4},{7,5},{8,10},{9,11},{10,... | collective-permute-start | bytes 786440 | tf_op jit(solution)/shard_map/ppermute | solution.py:455
  98.2 5.3 %first_layer_early.1.refs_4_ = f32[1024,1024]{1,0:T(8,128)S(1)} custom-call(s32[4]{0:T(128)S(1)} %pad_add_fusion.1.pos, bf16[1024,128]{1,0:T(8,128)(2,1)S(1)} %get-tuple-element.81.refs_0_, bf16[1056,128]{1,0:T(8,128)(2,1)S(1)} %copy-done.4, bf16[1024,128]{1,0:T(8,128)(2,1)S(1)} %copy-done.5, bf16[1024,128]{1,0:T(8,128)(2,1)S(1)} %collective-permute-done.refs_3_.refs_4_, ...), custom_call_target="tpu_custom_call" | custom-call | flops 3221225472 | bytes 11534336 | tf_op jit(solution)/shard_map/first_layer_early/pallas_call | solution.py:277
  103.5 2.0 %copy-done.9 = f32[1024,1024]{1,0:T(8,128)} copy-done((f32[1024,1024]{1,0:T(8,128)}, f32[1024,1024]{1,0:T(8,128)S(1)}, u32[]{:S(2)}) %copy-start.9) | copy-done | bytes 4194328
  105.4 4.4 %collective-permute-done.13.refs_2_.refs_3_ = bf16[1024,128]{1,0:T(8,128)(2,1)S(1)} collective-permute-done((bf16[1024,128]{1,0:T(8,128)(2,1)}, bf16[1024,128]{1,0:T(8,128)(2,1)S(1)}, u32[]{:S(2)}, u32[]{:S(2)}) %collective-permute-start.13) | collective-permute-done | bytes 262176 | tf_op jit(solution)/shard_map/ppermute | solution.py:455
  109.8 15.1 %mlp.1 = (bf16[1024,1024]{1,0:T(8,128)(2,1)S(1)}, bf16[1024,1024]{1,0:T(8,128)(2,1)}, bf16[1024,256]{1,0:T(8,128)(2,1)S(1)}, bf16[1024,1024]{1,0:T(8,128)(2,1)}, bf16[1024,1024]{1,0:T(8,128)(2,1)}) custom-call(s32[4]{0:T(128)S(1)} %pad_add_fusion.1.pos, bf16[1024,128]{1,0:T(8,128)(2,1)S(1)} %copy-done.6, ...), custom_call_target="tpu_custom_call" | custom-call | flops 6442450944 | bytes 20971520 | tf_op jit(solution)/shard_map/mlp/pallas_call | solution.py:296
  128.1 3.7 %outer_grads.1 = (bf16[4,16,16,640]{3,2,1,0:T(8,128)(2,1)S(1)}, bf16[4,16,16,640]{3,2,1,0:T(8,128)(2,1)S(1)}) custom-call(s32[4]{0:T(128)S(1)} %pad_add_fusion.1.pos, bf16[1024,1024]{1,0:T(8,128)(2,1)S(1)} %get-tuple-element.131.act1, bf16[1024,1024]{1,0:T(8,128)(2,1)S(1)} %copy-done.11, bf16[1024,256]{1,0:T(8,128)(2,1)S(1)} %get-tuple-element.133.gl, ...), custom_call_target="tpu_custom_call" | custom-call | flops 2684354560 | bytes 8388608 | tf_op jit(solution)/shard_map/outer_grads/pallas_call | solution.py:337
  131.9 1.8 first_grads_2.1
  134.5 3.0 %first_grads_13.1 = (bf16[2,16,16,1024]{3,2,1,0:T(8,128)(2,1)S(1)}, bf16[2,16,16,1024]{3,2,1,0:T(8,128)(2,1)S(1)}) custom-call(s32[4]{0:T(128)S(1)} %pad_add_fusion.1.pos, bf16[1024,128]{1,0:T(8,128)(2,1)S(1)} %collective-permute-done.1.refs_9_.refs_0_, bf16[1056,128]{1,0:T(8,128)(2,1)S(1)} %collective-permute-done.5.lab3.refs_10_.refs_1_, ...), custom_call_target="tpu_custom_call" | custom-call | flops 2147483648 | bytes 6291456 | tf_op jit(solution)/shard_map/first_grads_13/pallas_call | solution.py:367
  137.8 3.2 %collective-permute-start.24 = (bf16[8,16,640]{2,1,0:T(8,128)(2,1)S(1)}, bf16[8,16,640]{2,1,0:T(8,128)(2,1)S(1)}, u32[]{:S(2)}, u32[]{:S(2)}) collective-permute-start(bf16[8,16,640]{2,1,0:T(8,128)(2,1)S(1)} %get-tuple-element.156), channel_id=1, source_target_pairs={{0,96},{32,0},{64,32},{96,64},{1,97},{33,1},{65,33},{97,65},{2,98}... | collective-permute-start | bytes 491528 | tf_op jit(solution)/shard_map/ppermute | solution.py:455
  145.9 3.2 %collective-permute-start.26 = (bf16[16,16,640]{2,1,0:T(8,128)(2,1)S(1)}, bf16[16,16,640]{2,1,0:T(8,128)(2,1)S(1)}, u32[]{:S(2)}, u32[]{:S(2)}) collective-permute-start(bf16[16,16,640]{2,1,0:T(8,128)(2,1)S(1)} %get-tuple-element.158), channel_id=1, source_target_pairs={{0,96},{32,0},{64,32},{96,64},{1,97},{33,1},{65,33},{97,65},{2,98}... | collective-permute-start | bytes 983048 | tf_op jit(solution)/shard_map/ppermute | solution.py:455
  157.3 4.8 %all-to-all-start.4 = ((bf16[16,16,640]{2,1,0:T(8,128)(2,1)}), bf16[16,16,640]{2,1,0:T(8,128)(2,1)S(1)}, u32[]{:S(2)}, u32[]{:S(2)}) async-start(bf16[16,16,640]{2,1,0:T(8,128)(2,1)} %own_middle.1), calls=%async_computation.4 | async-start | bytes 655360 | tf_op jit(solution)/shard_map/all_to_all | solution.py:459
  162.1 8.8 %collective-permute-done.21.r1 = bf16[16,16,1024]{2,1,0:T(8,128)(2,1)S(1)} collective-permute-done((bf16[16,16,1024]{2,1,0:T(8,128)(2,1)}, bf16[16,16,1024]{2,1,0:T(8,128)(2,1)S(1)}, u32[]{:S(2)}, u32[]{:S(2)}) %collective-permute-start.21) | collective-permute-done | bytes 524320 | tf_op jit(solution)/shard_map/ppermute | solution.py:455
  171.7 14.3 %all_to_all.25.part_f = bf16[16,16,1024]{2,1,0:T(8,128)(2,1)S(1)} all-to-all(bf16[16,16,1024]{2,1,0:T(8,128)(2,1)S(1)} %own_first.1), channel_id=1, replica_groups=mesh['y'=4,'x'=4,'core'=2,'rep'=4] {'y','x'}, dimensions={0} | all-to-all | bytes 1048576 | tf_op jit(solution)/shard_map/all_to_all | solution.py:459
  (98 shorter events, 35.6 us)
Async XLA Ops:
  5.2 19.4 %all-to-all-start = ((bf16[16,144,128]{2,1,0:T(8,128)(2,1)}), bf16[16,144,128]{2,1,0:T(8,128)(2,1)S(1)}, u32[]{:S(2)}, u32[]{:S(2)}) async-start(bf16[16,144,128]{2,1,0:T(8,128)(2,1)} %get-tuple-element.82), calls=%async_computation | async-start | bytes 1179648 | tf_op jit(solution)/shard_map/all_to_all | solution.py:459
  12.3 10.1 %collective-permute-start = (bf16[1024,128]{1,0:T(8,128)(2,1)S(1)}, bf16[1024,128]{1,0:T(8,128)(2,1)S(1)}, u32[]{:S(2)}, u32[]{:S(2)}) collective-permute-start(bf16[1024,128]{1,0:T(8,128)(2,1)S(1)} %get-tuple-element.83), channel_id=1, source_target_pairs={{0,1},{1,2},{2,3},{3,0},{4,5},{5,6},{6,7},{7,4},{8,9},{9,10},{10,1... | collective-permute-start | bytes 786440 | tf_op jit(solution)/shard_map/ppermute | solution.py:455
  14.3 8.1 %collective-permute-start.1 = (bf16[1024,128]{1,0:T(8,128)(2,1)S(1)}, bf16[1024,128]{1,0:T(8,128)(2,1)S(1)}, u32[]{:S(2)}, u32[]{:S(2)}) collective-permute-start(bf16[1024,128]{1,0:T(8,128)(2,1)S(1)} %get-tuple-element.84), channel_id=1, source_target_pairs={{0,3},{1,0},{2,1},{3,2},{4,7},{5,4},{6,5},{7,6},{8,11},{9,8},{10,9... | collective-permute-start | bytes 786440 | tf_op jit(solution)/shard_map/ppermute | solution.py:455
  24.6 4.7 %collective-permute-start.2 = (bf16[16,144,128]{2,1,0:T(8,128)(2,1)S(1)}, bf16[16,144,128]{2,1,0:T(8,128)(2,1)S(1)}, u32[]{:S(2)}, u32[]{:S(2)}) collective-permute-start(bf16[16,144,128]{2,1,0:T(8,128)(2,1)S(1)} %all-to-all-done.near), channel_id=1, source_target_pairs={{0,4},{4,0},{1,5},{5,1},{2,6},{6,2},{3,7},{7,3},{8,12},{12,8},{9,1... | collective-permute-start | bytes 1769480 | tf_op jit(solution)/shard_map/ppermute | solution.py:455
  24.6 13.6 %collective-permute-start.3 = (bf16[1024,128]{1,0:T(8,128)(2,1)S(1)}, bf16[1024,128]{1,0:T(8,128)(2,1)S(1)}, u32[]{:S(2)}, u32[]{:S(2)}) collective-permute-start(bf16[1024,128]{1,0:T(8,128)(2,1)S(1)} %get-tuple-element.92), channel_id=1, source_target_pairs={{0,2},{1,3},{2,0},{3,1},{4,6},{5,7},{6,4},{7,5},{8,10},{9,11},{10,... | collective-permute-start | bytes 786440 | tf_op jit(solution)/shard_map/ppermute | solution.py:455
  38.2 15.8 %all-to-all-start.1 = ((bf16[16,128,128]{2,1,0:T(8,128)(2,1)}), bf16[16,128,128]{2,1,0:T(8,128)(2,1)S(1)}, u32[]{:S(2)}, u32[]{:S(2)}) async-start(bf16[16,128,128]{2,1,0:T(8,128)(2,1)} %get-tuple-element.95), calls=%async_computation.1 | async-start | bytes 1048576 | tf_op jit(solution)/shard_map/all_to_all | solution.py:459
  42.1 30.8 %copy-start.4 = (bf16[1056,128]{1,0:T(8,128)(2,1)S(1)}, bf16[1056,128]{1,0:T(8,128)(2,1)}, u32[]{:S(2)}) copy-start(bf16[1056,128]{1,0:T(8,128)(2,1)} %get-tuple-element.93.lab0.refs_1_) | copy-start | bytes 811012
  42.1 9.8 %collective-permute-start.4 = (bf16[1056,128]{1,0:T(8,128)(2,1)}, bf16[1056,128]{1,0:T(8,128)(2,1)S(1)}, u32[]{:S(2)}, u32[]{:S(2)}) collective-permute-start(bf16[1056,128]{1,0:T(8,128)(2,1)} %get-tuple-element.96), channel_id=1, source_target_pairs={{0,1},{1,2},{2,3},{3,0},{4,5},{5,6},{6,7},{7,4},{8,9},{9,10},{10,1... | collective-permute-start | bytes 811016 | tf_op jit(solution)/shard_map/ppermute | solution.py:455
  43.2 8.8 %collective-permute-start.5 = (bf16[1056,128]{1,0:T(8,128)(2,1)}, bf16[1056,128]{1,0:T(8,128)(2,1)S(1)}, u32[]{:S(2)}, u32[]{:S(2)}) collective-permute-start(bf16[1056,128]{1,0:T(8,128)(2,1)} %get-tuple-element.97), channel_id=1, source_target_pairs={{0,3},{1,0},{2,1},{3,2},{4,7},{5,4},{6,5},{7,6},{8,11},{9,8},{10,9... | collective-permute-start | bytes 811016 | tf_op jit(solution)/shard_map/ppermute | solution.py:455
  54.0 1.9 %collective-permute-start.6 = (bf16[16,128,128]{2,1,0:T(8,128)(2,1)S(1)}, bf16[16,128,128]{2,1,0:T(8,128)(2,1)S(1)}, u32[]{:S(2)}, u32[]{:S(2)}) collective-permute-start(bf16[16,128,128]{2,1,0:T(8,128)(2,1)S(1)} %all-to-all-done.1.near), channel_id=1, source_target_pairs={{0,4},{4,0},{1,5},{5,1},{2,6},{6,2},{3,7},{7,3},{8,12},{12,8},{9,1... | collective-permute-start | bytes 1572872 | tf_op jit(solution)/shard_map/ppermute | solution.py:455
  54.0 10.6 %collective-permute-start.7 = (bf16[1056,128]{1,0:T(8,128)(2,1)}, bf16[1056,128]{1,0:T(8,128)(2,1)S(1)}, u32[]{:S(2)}, u32[]{:S(2)}) collective-permute-start(bf16[1056,128]{1,0:T(8,128)(2,1)} %get-tuple-element.105), channel_id=1, source_target_pairs={{0,2},{1,3},{2,0},{3,1},{4,6},{5,7},{6,4},{7,5},{8,10},{9,11},{10,... | collective-permute-start | bytes 811016 | tf_op jit(solution)/shard_map/ppermute | solution.py:455
  64.6 16.9 %all-to-all-start.2 = ((bf16[16,128,128]{2,1,0:T(8,128)(2,1)}), bf16[16,128,128]{2,1,0:T(8,128)(2,1)}, u32[]{:S(2)}, u32[]{:S(2)}) async-start(bf16[16,128,128]{2,1,0:T(8,128)(2,1)} %get-tuple-element.108), calls=%async_computation.2 | async-start | bytes 1048576 | tf_op jit(solution)/shard_map/all_to_all | solution.py:459
  69.6 9.6 %collective-permute-start.8 = (bf16[1024,128]{1,0:T(8,128)(2,1)}, bf16[1024,128]{1,0:T(8,128)(2,1)S(1)}, u32[]{:S(2)}, u32[]{:S(2)}) collective-permute-start(bf16[1024,128]{1,0:T(8,128)(2,1)} %get-tuple-element.109), channel_id=1, source_target_pairs={{0,1},{1,2},{2,3},{3,0},{4,5},{5,6},{6,7},{7,4},{8,9},{9,10},{10,1... | collective-permute-start | bytes 786440 | tf_op jit(solution)/shard_map/ppermute | solution.py:455
  71.6 8.0 %collective-permute-start.9 = (bf16[1024,128]{1,0:T(8,128)(2,1)}, bf16[1024,128]{1,0:T(8,128)(2,1)S(1)}, u32[]{:S(2)}, u32[]{:S(2)}) collective-permute-start(bf16[1024,128]{1,0:T(8,128)(2,1)} %get-tuple-element.110), channel_id=1, source_target_pairs={{0,3},{1,0},{2,1},{3,2},{4,7},{5,4},{6,5},{7,6},{8,11},{9,8},{10,9... | collective-permute-start | bytes 786440 | tf_op jit(solution)/shard_map/ppermute | solution.py:455
  81.5 3.9 %collective-permute-start.10 = (bf16[16,128,128]{2,1,0:T(8,128)(2,1)}, bf16[16,128,128]{2,1,0:T(8,128)(2,1)}, u32[]{:S(2)}, u32[]{:S(2)}) collective-permute-start(bf16[16,128,128]{2,1,0:T(8,128)(2,1)} %all-to-all-done.2.near), channel_id=1, source_target_pairs={{0,4},{4,0},{1,5},{5,1},{2,6},{6,2},{3,7},{7,3},{8,12},{12,8},{9,1... | collective-permute-start | bytes 1572872 | tf_op jit(solution)/shard_map/ppermute | solution.py:455
  81.5 11.7 %collective-permute-start.11 = (bf16[1024,128]{1,0:T(8,128)(2,1)}, bf16[1024,128]{1,0:T(8,128)(2,1)S(1)}, u32[]{:S(2)}, u32[]{:S(2)}) collective-permute-start(bf16[1024,128]{1,0:T(8,128)(2,1)} %get-tuple-element.119), channel_id=1, source_target_pairs={{0,2},{1,3},{2,0},{3,1},{4,6},{5,7},{6,4},{7,5},{8,10},{9,11},{10,... | collective-permute-start | bytes 786440 | tf_op jit(solution)/shard_map/ppermute | solution.py:455
  93.2 12.3 %collective-permute-start.12 = (bf16[1024,128]{1,0:T(8,128)(2,1)}, bf16[1024,128]{1,0:T(8,128)(2,1)S(1)}, u32[]{:S(2)}, u32[]{:S(2)}) collective-permute-start(bf16[1024,128]{1,0:T(8,128)(2,1)} %get-tuple-element.121), channel_id=1, source_target_pairs={{0,1},{1,2},{2,3},{3,0},{4,5},{5,6},{6,7},{7,4},{8,9},{9,10},{10,1... | collective-permute-start | bytes 786440 | tf_op jit(solution)/shard_map/ppermute | solution.py:455
  95.2 14.6 %collective-permute-start.13 = (bf16[1024,128]{1,0:T(8,128)(2,1)}, bf16[1024,128]{1,0:T(8,128)(2,1)S(1)}, u32[]{:S(2)}, u32[]{:S(2)}) collective-permute-start(bf16[1024,128]{1,0:T(8,128)(2,1)} %get-tuple-element.122), channel_id=1, source_target_pairs={{0,2},{1,3},{2,0},{3,1},{4,6},{5,7},{6,4},{7,5},{8,10},{9,11},{10,... | collective-permute-start | bytes 786440 | tf_op jit(solution)/shard_map/ppermute | solution.py:455
  97.6 12.2 %collective-permute-start.14 = (bf16[1024,128]{1,0:T(8,128)(2,1)}, bf16[1024,128]{1,0:T(8,128)(2,1)S(1)}, u32[]{:S(2)}, u32[]{:S(2)}) collective-permute-start(bf16[1024,128]{1,0:T(8,128)(2,1)} %get-tuple-element.123), channel_id=1, source_target_pairs={{0,3},{1,0},{2,1},{3,2},{4,7},{5,4},{6,5},{7,6},{8,11},{9,8},{10,9... | collective-permute-start | bytes 786440 | tf_op jit(solution)/shard_map/ppermute | solution.py:455
  131.8 5.7 %collective-permute-start.15 = (bf16[4,16,16,640]{3,2,1,0:T(8,128)(2,1)S(1)}, bf16[4,16,16,640]{3,2,1,0:T(8,128)(2,1)S(1)}, u32[]{:S(2)}, u32[]{:S(2)}) collective-permute-start(bf16[4,16,16,640]{3,2,1,0:T(8,128)(2,1)S(1)} %get-tuple-element.135), channel_id=1, source_target_pairs={{0,4},{4,0},{1,5},{5,1},{2,6},{6,2},{3,7},{7,3},{8,12},{12,8},{9,1... | collective-permute-start | bytes 3932168 | tf_op jit(solution)/shard_map/ppermute | solution.py:455
  133.7 3.8 %collective-permute-start.16 = (bf16[1,16,16,1024]{3,2,1,0:T(8,128)(2,1)S(1)}, bf16[1,16,16,1024]{3,2,1,0:T(8,128)(2,1)S(1)}, u32[]{:S(2)}, u32[]{:S(2)}) collective-permute-start(bf16[1,16,16,1024]{3,2,1,0:T(8,128)(2,1)S(1)} %get-tuple-element.137), channel_id=1, source_target_pairs={{0,4},{4,0},{1,5},{5,1},{2,6},{6,2},{3,7},{7,3},{8,12},{12,8},{9,1... | collective-permute-start | bytes 1572872 | tf_op jit(solution)/shard_map/ppermute | solution.py:455
  137.5 13.5 %collective-permute-start.18 = (bf16[2,16,16,1024]{3,2,1,0:T(8,128)(2,1)S(1)}, bf16[2,16,16,1024]{3,2,1,0:T(8,128)(2,1)S(1)}, u32[]{:S(2)}, u32[]{:S(2)}) collective-permute-start(bf16[2,16,16,1024]{3,2,1,0:T(8,128)(2,1)S(1)} %get-tuple-element.146), channel_id=1, source_target_pairs={{0,4},{4,0},{1,5},{5,1},{2,6},{6,2},{3,7},{7,3},{8,12},{12,8},{9,1... | collective-permute-start | bytes 3145736 | tf_op jit(solution)/shard_map/ppermute | solution.py:455
  137.7 7.9 %collective-permute-start.23 = (bf16[8,16,640]{2,1,0:T(8,128)(2,1)S(1)}, bf16[8,16,640]{2,1,0:T(8,128)(2,1)S(1)}, u32[]{:S(2)}, u32[]{:S(2)}) collective-permute-start(bf16[8,16,640]{2,1,0:T(8,128)(2,1)S(1)} %get-tuple-element.155), channel_id=1, source_target_pairs={{0,32},{32,64},{64,96},{96,0},{1,33},{33,65},{65,97},{97,1},{2,34}... | collective-permute-start | bytes 491528 | tf_op jit(solution)/shard_map/ppermute | solution.py:455
  137.8 7.8 %collective-permute-start.24 = (bf16[8,16,640]{2,1,0:T(8,128)(2,1)S(1)}, bf16[8,16,640]{2,1,0:T(8,128)(2,1)S(1)}, u32[]{:S(2)}, u32[]{:S(2)}) collective-permute-start(bf16[8,16,640]{2,1,0:T(8,128)(2,1)S(1)} %get-tuple-element.156), channel_id=1, source_target_pairs={{0,96},{32,0},{64,32},{96,64},{1,97},{33,1},{65,33},{97,65},{2,98}... | collective-permute-start | bytes 491528 | tf_op jit(solution)/shard_map/ppermute | solution.py:455
  141.1 9.8 %collective-permute-start.19 = (bf16[8,16,1024]{2,1,0:T(8,128)(2,1)S(1)}, bf16[8,16,1024]{2,1,0:T(8,128)(2,1)S(1)}, u32[]{:S(2)}, u32[]{:S(2)}) collective-permute-start(bf16[8,16,1024]{2,1,0:T(8,128)(2,1)S(1)} %get-tuple-element.149), channel_id=1, source_target_pairs={{0,1},{1,2},{2,3},{3,0},{4,5},{5,6},{6,7},{7,4},{8,9},{9,10},{10,1... | collective-permute-start | bytes 786440 | tf_op jit(solution)/shard_map/ppermute | solution.py:455
  142.6 8.4 %collective-permute-start.20 = (bf16[8,16,1024]{2,1,0:T(8,128)(2,1)S(1)}, bf16[8,16,1024]{2,1,0:T(8,128)(2,1)S(1)}, u32[]{:S(2)}, u32[]{:S(2)}) collective-permute-start(bf16[8,16,1024]{2,1,0:T(8,128)(2,1)S(1)} %get-tuple-element.150), channel_id=1, source_target_pairs={{0,3},{1,0},{2,1},{3,2},{4,7},{5,4},{6,5},{7,6},{8,11},{9,8},{10,9... | collective-permute-start | bytes 786440 | tf_op jit(solution)/shard_map/ppermute | solution.py:455
  145.8 10.6 %collective-permute-start.25 = (bf16[16,16,640]{2,1,0:T(8,128)(2,1)S(1)}, bf16[16,16,640]{2,1,0:T(8,128)(2,1)S(1)}, u32[]{:S(2)}, u32[]{:S(2)}) collective-permute-start(bf16[16,16,640]{2,1,0:T(8,128)(2,1)S(1)} %get-tuple-element.157), channel_id=1, source_target_pairs={{0,32},{32,64},{64,96},{96,0},{1,33},{33,65},{65,97},{97,1},{2,34}... | collective-permute-start | bytes 983048 | tf_op jit(solution)/shard_map/ppermute | solution.py:455
  145.9 10.5 %collective-permute-start.26 = (bf16[16,16,640]{2,1,0:T(8,128)(2,1)S(1)}, bf16[16,16,640]{2,1,0:T(8,128)(2,1)S(1)}, u32[]{:S(2)}, u32[]{:S(2)}) collective-permute-start(bf16[16,16,640]{2,1,0:T(8,128)(2,1)S(1)} %get-tuple-element.158), channel_id=1, source_target_pairs={{0,96},{32,0},{64,32},{96,64},{1,97},{33,1},{65,33},{97,65},{2,98}... | collective-permute-start | bytes 983048 | tf_op jit(solution)/shard_map/ppermute | solution.py:455
  150.9 11.1 %collective-permute-start.17 = (bf16[1,16,16,1024]{3,2,1,0:T(8,128)(2,1)S(1)}, bf16[1,16,16,1024]{3,2,1,0:T(8,128)(2,1)S(1)}, u32[]{:S(2)}, u32[]{:S(2)}) collective-permute-start(bf16[1,16,16,1024]{3,2,1,0:T(8,128)(2,1)S(1)} %get-tuple-element.144), channel_id=1, source_target_pairs={{0,4},{4,0},{1,5},{5,1},{2,6},{6,2},{3,7},{7,3},{8,12},{12,8},{9,1... | collective-permute-start | bytes 1572872 | tf_op jit(solution)/shard_map/ppermute | solution.py:455
  152.1 18.8 %collective-permute-start.21 = (bf16[16,16,1024]{2,1,0:T(8,128)(2,1)}, bf16[16,16,1024]{2,1,0:T(8,128)(2,1)S(1)}, u32[]{:S(2)}, u32[]{:S(2)}) collective-permute-start(bf16[16,16,1024]{2,1,0:T(8,128)(2,1)} %get-tuple-element.151), channel_id=1, source_target_pairs={{0,1},{1,2},{2,3},{3,0},{4,5},{5,6},{6,7},{7,4},{8,9},{9,10},{10,1... | collective-permute-start | bytes 1572872 | tf_op jit(solution)/shard_map/ppermute | solution.py:455
  153.5 17.4 %collective-permute-start.22 = (bf16[16,16,1024]{2,1,0:T(8,128)(2,1)S(1)}, bf16[16,16,1024]{2,1,0:T(8,128)(2,1)S(1)}, u32[]{:S(2)}, u32[]{:S(2)}) collective-permute-start(bf16[16,16,1024]{2,1,0:T(8,128)(2,1)S(1)} %get-tuple-element.152), channel_id=1, source_target_pairs={{0,3},{1,0},{2,1},{3,2},{4,7},{5,4},{6,5},{7,6},{8,11},{9,8},{10,9... | collective-permute-start | bytes 1572872 | tf_op jit(solution)/shard_map/ppermute | solution.py:455
  157.3 14.4 %all-to-all-start.4 = ((bf16[16,16,640]{2,1,0:T(8,128)(2,1)}), bf16[16,16,640]{2,1,0:T(8,128)(2,1)S(1)}, u32[]{:S(2)}, u32[]{:S(2)}) async-start(bf16[16,16,640]{2,1,0:T(8,128)(2,1)} %own_middle.1), calls=%async_computation.4 | async-start | bytes 655360 | tf_op jit(solution)/shard_map/all_to_all | solution.py:459
  (20 other events, 169.5 us)
